TPU v7x, 32 devices: a whole 2x2x4 slice. The times are simulated.
32 devices in a mesh: member: 2 (over y), tx: 4 (over z), ty: 4 (over x, core).
Axes of the slice: x: 2, y: 2, z: 4, core: 2. Of those that a mesh axis runs over, the one named last changes fastest.
Arguments:
- tracers: float32 [80, 3, 128, 512], P('member', None, 'tx', 'ty'), parts along dimension 0, may hold values from 0.05 to 2
- velocity: float32 [2, 3, 128, 512], P(None, None, 'tx', 'ty'), may hold values from -0.4 to 0.4
- land_mask: int32 [3, 128, 512], P(None, 'tx', 'ty'), may hold values 0 or 1
- sunlight: float32 [128, 512], P('tx', 'ty'), may hold values from 0.3 to 3
- growth_max: float32 [52], P('member'), parts along dimension 0, may hold values from 0.2 to 1.5
- half_sat: float32 [8, 26], P('member'), parts along dimension 0, may hold values from 0.05 to 1
- light_half: float32 [52], P('member'), parts along dimension 0, may hold values from 0.1 to 1
- graze_max: float32 [20], P('member'), parts along dimension 0, may hold values from 0.2 to 1.5
- graze_half: float32 [20], P('member'), parts along dimension 0, may hold values from 0.2 to 2
- palatable: int32 [20, 26], P('member'), parts along dimension 0, may hold values 0 or 1
- stoichiometry: float32 [4], replicated, may hold values from 0.05 to 1
Outputs:
- updated: float32 [80, 3, 128, 512], P('member', None, 'tx', 'ty'), parts along dimension 0
There are 2 independent parts, one for each index of `member`. A program takes and returns all parts, laid end to end along the dimension named above; an argument that names none is the same for every part. Nothing has to cross between parts.
All inputs are finite; a program needn't handle non-finite values. No bound on the sum of `land_mask` on one device may be relied on, other than what follows from the above.
Results may differ from a plain program's by a relative error of at most 0.000064.
Values sent between devices are 32-bit elements; how exact they have to be, the bound alone decides.
No kernel may reach another device: no remote copies, remote signals or barrier semaphores. Data moves between devices by JAX's collectives and lax.ppermute only.
A program may use at most 64 MiB of HBM per device.

v0:
```python
import jax
import jax.numpy as jnp
from jax import lax
from jax.sharding import PartitionSpec as P

NNUT = 4
NPHY = 26


plankton_mortality = 0.05
grazer_mortality = 0.3
assimilation = 0.3
attenuation = 0.4


def extended(array, sides, width, wrap):
    for axis, dim in sides:
        size, length = (lax.axis_size(axis), array.shape[dim])
        up = [(i, (i + 1) % size) for i in range(size if wrap else size - 1)]
        down = [(j, i) for i, j in up]
        last = lax.slice_in_dim(array, length - width, length, axis=dim)
        first = lax.slice_in_dim(array, 0, width, axis=dim)
        before = lax.ppermute(last, axis, up)
        after = lax.ppermute(first, axis, down)
        array = jnp.concatenate([before, array, after], axis=dim)
    return array


def window(values, offset, amount, axis_dim):
    return lax.slice_in_dim(values, offset, offset + amount, axis=axis_dim)


def advect(padded, courant, wet_mask, axis_dim, length):
    face_count = length + 1
    far_left = window(padded, 0, face_count, axis_dim)
    near_left = window(padded, 1, face_count, axis_dim)
    near_right = window(padded, 2, face_count, axis_dim)
    far_right = window(padded, 3, face_count, axis_dim)
    opened = window(wet_mask, 1, face_count, axis_dim) * window(wet_mask, 2, face_count, axis_dim)
    transport = window(courant, 2, face_count, axis_dim) * opened
    face_flux = transport * (
        7.0 / 12.0 * (near_left + near_right) - 1.0 / 12.0 * (far_left + far_right)
    )
    face_flux = face_flux + jnp.abs(transport) * (1.0 / 12.0) * (
        far_right - 3.0 * near_right + 3.0 * near_left - far_left
    )
    centre = window(padded, 2, length, axis_dim)
    outflow = window(face_flux, 1, length, axis_dim) - window(face_flux, 0, length, axis_dim)
    spread = window(transport, 1, length, axis_dim) - window(transport, 0, length, axis_dim)
    return centre - outflow + centre * spread


def ecology(
    concentration,
    irradiance,
    growth_max,
    half_sat,
    light_half,
    graze_max,
    graze_half,
    palatable,
    stoichiometry,
):
    nutrients = concentration[:NNUT]
    phytoplankton = concentration[NNUT : NNUT + NPHY]
    zooplankton = concentration[NNUT + NPHY :]
    saturation = nutrients[:, None, :] / (nutrients[:, None, :] + half_sat[:, :, None])
    nutrient_limit = jnp.min(saturation, axis=0)
    light_limit = irradiance[None, :] / (irradiance[None, :] + light_half[:, None])
    growth = growth_max[:, None] * nutrient_limit * light_limit * phytoplankton
    prey_weights = palatable.astype(jnp.float32)
    available = jnp.dot(prey_weights, phytoplankton, precision=lax.Precision.HIGHEST)
    grazing_rate = graze_max[:, None] * zooplankton / (graze_half[:, None] + available)
    grazed = phytoplankton * jnp.dot(prey_weights.T, grazing_rate, precision=lax.Precision.HIGHEST)
    ingested = grazing_rate * available
    plankton_loss = plankton_mortality * phytoplankton
    grazer_loss = grazer_mortality * zooplankton * zooplankton
    phyto_change = growth - grazed - plankton_loss
    grazer_change = assimilation * ingested - grazer_loss
    recycled = (
        jnp.sum(plankton_loss, axis=0)
        + jnp.sum(grazer_loss, axis=0)
        + (1.0 - assimilation) * jnp.sum(ingested, axis=0)
        - jnp.sum(growth, axis=0)
    )
    nutrient_change = stoichiometry[:, None] * recycled[None, :]
    return jnp.concatenate([nutrient_change, phyto_change, grazer_change], axis=0)


def shards(
    tracers,
    velocity,
    land_mask,
    sunlight,
    growth_max,
    half_sat,
    light_half,
    graze_max,
    graze_half,
    palatable,
    stoichiometry,
):
    tracer_count = tracers.shape[0]
    along_count = tracers.shape[2]
    across_count = tracers.shape[3]
    wet_mask = land_mask.astype(jnp.float32)[None]
    stacked = jnp.concatenate([tracers, velocity, wet_mask], axis=0)
    padded = extended(stacked, (("tx", 2),), 2, True)
    after_along = advect(
        padded[:tracer_count],
        padded[tracer_count : tracer_count + 1],
        padded[tracer_count + 2 : tracer_count + 3],
        2,
        along_count,
    )
    second = jnp.concatenate([after_along, velocity[1:2], wet_mask], axis=0)
    across = extended(second, (("ty", 3),), 2, False)
    advected = advect(
        across[:tracer_count],
        across[tracer_count : tracer_count + 1],
        across[tracer_count + 1 : tracer_count + 2],
        3,
        across_count,
    )
    levels = lax.broadcasted_iota(jnp.float32, (tracers.shape[1], 1, 1), 0)
    irradiance = (sunlight[None] * jnp.exp(-attenuation * (levels + 0.5))).reshape(-1)
    tendency = ecology(
        tracers.reshape(tracer_count, -1),
        irradiance,
        growth_max,
        half_sat,
        light_half,
        graze_max,
        graze_half,
        palatable,
        stoichiometry,
    )
    return advected + wet_mask * tendency.reshape(tracers.shape)


def solution(mesh):
    return jax.shard_map(
        shards,
        mesh=mesh,
        in_specs=(
            P("member", None, "tx", "ty"),
            P(None, None, "tx", "ty"),
            P(None, "tx", "ty"),
            P("tx", "ty"),
            P("member"),
            P("member", None),
            P("member"),
            P("member"),
            P("member"),
            P("member", None),
            P(),
        ),
        out_specs=P("member", None, "tx", "ty"),
        check_vma=False,
    )
```

profile of v0, /device:TPU:0, one launch (start us, length us, event | category | flops | bytes accessed | tf_op | source)
XLA Modules:
  0.0 57.3 jit_solution(4100524613495818624)
XLA Ops:
  0.0 0.9 %fusion.21 = (f32[3,32,128]{2,1,0:T(8,128)S(1)}, f32[1,3,32,128]{3,2,1,0:T(8,128)S(1)}) fusion(s32[3,32,128]{2,1,0:T(8,128)} %param.13), kind=kLoop, calls=%fused_computation.52 | loop fusion | flops 12288 | bytes 147456 | tf_op jit(solution)/shard_map/convert_element_type | solution.py:106
  1.0 1.4 %pad_maximum_fusion.3 = (f32[43,3,2,128]{3,2,1,0:T(2,128)S(1)}, f32[43,3,2,128]{3,2,1,0:T(2,128)S(1)}) fusion(f32[1,3,32,128]{3,2,1,0:T(8,128)S(1)} %get-tuple-element.25, f32[2,3,32,128]{3,2,1,0:T(8,128)} %param.12, f32[40,3,32,128]{3,2,1,0:T(8,128)} %param.11), kind=kLoop, calls=%fused_computation.30 | loop fusion | flops 132096 | bytes 2377728 | tf_op jit(solution)/shard_map/concatenate | solution.py:107
  2.3 5.1 %collective-permute-start = (f32[43,3,2,128]{3,0,2,1:T(8,128)S(1)}, f32[43,3,2,128]{3,0,2,1:T(8,128)}, u32[]{:S(2)}, u32[]{:S(2)}) collective-permute-start(f32[43,3,2,128]{3,0,2,1:T(8,128)S(1)} %copy.31), channel_id=1, source_target_pairs={{4,0},{8,4},{12,8},{0,12},{5,1},{9,5},{13,9},{1,13},{6,2},{10,6},{... | collective-permute-start | bytes 396296 | tf_op jit(solution)/shard_map/ppermute | solution.py:24
  7.5 0.7 %copy.33 = f32[43,3,2,128]{3,0,2,1:T(8,128)} copy(f32[43,3,2,128]{3,2,1,0:T(2,128)S(1)} %get-tuple-element.13) | data formatting | bytes 264192 | tf_op jit(solution)/shard_map/slice | solution.py:21
  8.5 4.6 %fusion.3 = f32[26,12288]{1,0:T(8,128)S(1)} fusion(f32[4,26]{0,1:T(8,128)S(1)} %copy.39, f32[4,12288]{1,0:T(4,128)S(1)} %bitcast.58), kind=kLoop, calls=%fused_computation.5 | loop fusion | flops 3514368 | bytes 1474976 | tf_op jit(solution)/shard_map/reduce_min | solution.py:68
  13.1 0.3 copy.43
  13.5 0.6 %copy-done.6 = f32[32,128]{1,0:T(8,128)S(1)} copy-done((f32[32,128]{1,0:T(8,128)S(1)}, f32[32,128]{1,0:T(8,128)}, u32[]{:S(2)}) %copy-start.6) | copy-done | bytes 16408
  14.2 0.6 multiply_reduce_fusion.1
  14.9 0.9 %copy.41 = f32[4,8,96,128]{3,1,2,0:T(8,128)S(1)} copy(f32[4,8,96,128]{3,2,1,0:T(8,128)S(1)} %bitcast.48) | data formatting | bytes 3145728
  15.9 0.5 copy.40
  16.5 1.2 %multiply_reduce_fusion.2 = (f32[12288]{0:T(1024)S(1)}, f32[10,12288]{1,0:T(8,128)S(1)}, f32[10,12288]{1,0:T(8,128)S(1)}) fusion(f32[10]{0:T(128)S(1)} %copy-done.12, f32[10,12288]{1,0:T(8,128)S(1)} %bitcast.59, f32[10]{0:T(128)S(1)} %copy-done.13, f32[26,12288]{1,0:T(8,128)S(1)} %bitcast.54, s32[10,26]{1,0:T(8,128)S(1)} %copy-done.11), kind=kOutput, calls=%fused_computation.28 | convolution fusion | flops 39432452 | bytes 2802784 | tf_op jit(solution)/shard_map/dot_general | solution.py:72
  17.9 3.2 %fusion.2 = f32[26,12288]{1,0:T(8,128)} fusion(f32[26,12288]{1,0:T(8,128)S(1)} %bitcast.55, f32[26,12288]{1,0:T(8,128)S(1)} %fusion.3, f32[26]{0:T(128)S(1)} %copy-done.9, f32[12288]{0:T(1024)S(1)} %bitcast.61, f32[26]{0:T(128)S(1)} %copy-done.10, s32[10,26]{1,0:T(8,128)S(1)} %copy-done.11, f32[10,12288]{1,0:T(8,128)S(1)} %get-tuple-element.26, ...), kind=kOutput, calls=%fused_computation.3 | convolution fusion | flops 41582852 | bytes 4867376 | tf_op jit(solution)/shard_map/dot_general | solution.py:74
  21.1 1.0 %copy.32 = f32[43,3,2,128]{3,2,1,0:T(2,128)S(1)} copy(f32[43,3,2,128]{3,0,2,1:T(8,128)} %collective-permute-done) | data formatting | bytes 264192 | tf_op jit(solution)/shard_map/ppermute | solution.py:24
  22.1 1.0 %copy.34 = f32[43,3,2,128]{3,2,1,0:T(2,128)S(1)} copy(f32[43,3,2,128]{3,0,2,1:T(8,128)} %collective-permute-done.1) | data formatting | bytes 264192 | tf_op jit(solution)/shard_map/ppermute | solution.py:23
  23.1 0.5 maximum_maximum_fusion.1
  23.7 1.6 %multiply_add_fusion.1 = f32[40,3,33,128]{3,2,1,0:T(8,128)S(1)} fusion(f32[43,3,34,128]{3,2,1,0:T(8,128)S(1)} %get-tuple-element.12, f32[43,3,34,128]{3,2,1,0:T(8,128)S(1)} %get-tuple-element.11, f32[3,33,128]{2,1,0:T(8,128)S(1)} %get-tuple-element.9, f32[3,33,128]{2,1,0:T(8,128)S(1)} %bitcast.57), kind=kLoop, calls=%fused_computation.11 | loop fusion | flops 6589440 | bytes 10238976 | tf_op jit(solution)/shard_map/add | solution.py:44
  25.3 0.4 fusion.8
  25.9 2.7 %fusion.20 = (f32[42,3,32,2]{3,2,1,0:T(8,128)}, f32[42,3,32,2]{3,2,1,0:T(8,128)}) fusion(f32[42,3,32,128]{3,2,1,0:T(8,128)S(1)} %pad_maximum_fusion.2), kind=kLoop, calls=%fused_computation.51 | loop fusion | bytes 129024 | tf_op jit(solution)/shard_map/slice | solution.py:21
  28.6 2.7 %copy.35 = f32[42,3,32,2]{0,2,3,1:T(8,128)S(1)} copy(f32[42,3,32,2]{3,2,1,0:T(8,128)} %get-tuple-element.18) | data formatting | bytes 64512 | tf_op jit(solution)/shard_map/slice | solution.py:22
  31.3 1.3 %collective-permute-start.2 = (f32[42,3,32,2]{0,2,3,1:T(8,128)S(1)}, f32[42,3,32,2]{0,2,3,1:T(8,128)S(1)}, u32[]{:S(2)}, u32[]{:S(2)}) collective-permute-start(f32[42,3,32,2]{0,2,3,1:T(8,128)S(1)} %copy.35), channel_id=1, source_target_pairs={{1,0},{2,1},{3,2},{5,4},{6,5},{7,6},{9,8},{10,9},{11,10},{13,12},{... | collective-permute-start | bytes 96776 | tf_op jit(solution)/shard_map/ppermute | solution.py:24
  32.6 2.7 %copy.37 = f32[42,3,32,2]{0,2,3,1:T(8,128)S(1)} copy(f32[42,3,32,2]{3,2,1,0:T(8,128)} %get-tuple-element.17) | data formatting | bytes 64512 | tf_op jit(solution)/shard_map/slice | solution.py:21
  35.4 3.0 %collective-permute-start.3 = (f32[42,3,32,2]{0,2,3,1:T(8,128)S(1)}, f32[42,3,32,2]{0,2,3,1:T(8,128)S(1)}, u32[]{:S(2)}, u32[]{:S(2)}) collective-permute-start(f32[42,3,32,2]{0,2,3,1:T(8,128)S(1)} %copy.37), channel_id=1, source_target_pairs={{0,1},{1,2},{2,3},{4,5},{5,6},{6,7},{8,9},{9,10},{10,11},{12,13},{... | collective-permute-start | bytes 96776 | tf_op jit(solution)/shard_map/ppermute | solution.py:23
  38.4 1.7 %maximum_bitcast_fusion = f32[5,8,96,128]{3,1,2,0:T(8,128)S(1)} fusion(f32[10,12288]{1,0:T(8,128)S(1)} %get-tuple-element.23, f32[26,12288]{1,0:T(8,128)} %fusion.2, f32[4,12288]{1,0:T(4,128)S(1)} %broadcast_multiply_fusion), kind=kLoop, calls=%fused_computation.20 | loop fusion | flops 983040 | bytes 3932160
  40.1 1.6 %copy.44 = f32[5,8,96,128]{3,2,1,0:T(8,128)} copy(f32[5,8,96,128]{3,1,2,0:T(8,128)S(1)} %maximum_bitcast_fusion) | data formatting | bytes 3932160
  41.7 3.0 %copy.36 = f32[42,3,32,2]{3,2,1,0:T(8,128)} copy(f32[42,3,32,2]{0,2,3,1:T(8,128)S(1)} %collective-permute-done.2) | data formatting | bytes 64512 | tf_op jit(solution)/shard_map/ppermute | solution.py:24
  44.7 3.0 %copy.38 = f32[42,3,32,2]{3,2,1,0:T(8,128)} copy(f32[42,3,32,2]{0,2,3,1:T(8,128)S(1)} %collective-permute-done.3) | data formatting | bytes 64512 | tf_op jit(solution)/shard_map/ppermute | solution.py:23
  47.8 1.1 %multiply_bitcast_fusion = (f32[3,32,129]{2,1,0:T(8,128)S(1)}, f32[1,3,32,129]{3,2,1,0:T(8,128)S(1)}) fusion(f32[42,3,32,2]{3,2,1,0:T(8,128)} %copy.36, f32[1,3,32,128]{3,2,1,0:T(8,128)S(1)} %get-tuple-element.25, f32[1,3,32,128]{3,2,1,0:T(8,128)S(1)} %slice.150, f32[40,3,32,128]{3,2,1,0:T(8,128)S(1)} %fusion.8, f32[42,3,32,2]{3,2,1,0:T(8,128)} %copy.38), kind=kLoop, calls=%fused_computation.36 | loop fusion | flops 160992 | bytes 2227968 | tf_op jit(solution)/shard_map/mul | solution.py:44
  48.9 0.5 copy-done.2
  49.4 0.6 %copy-done.3 = f32[42,3,32,2]{3,2,1,0:T(8,128)S(1)} copy-done((f32[42,3,32,2]{3,2,1,0:T(8,128)S(1)}, f32[42,3,32,2]{3,2,1,0:T(8,128)}, u32[]{:S(2)}) %copy-start.3) | copy-done | bytes 32280
  50.0 2.6 %maximum_maximum_fusion = (f32[42,3,32,130]{3,2,1,0:T(8,128)S(1)}, f32[42,3,32,130]{3,2,1,0:T(8,128)S(1)}) fusion(f32[1,3,32,128]{3,2,1,0:T(8,128)S(1)} %get-tuple-element.25, f32[1,3,32,128]{3,2,1,0:T(8,128)S(1)} %slice.150, f32[40,3,32,128]{3,2,1,0:T(8,128)S(1)} %fusion.8, f32[42,3,32,2]{3,2,1,0:T(8,128)S(1)} %copy-done.3, f32[42,3,32,2]{3,2,1,0:T(8,128)S(1)} %copy-done.2), kind=kLoop, calls=%fused_computation.7 | loop fusion | flops 3144960 | bytes 6322176 | tf_op jit(solution)/shard_map/concatenate | solution.py:25
  52.7 2.5 %multiply_add_fusion = f32[40,3,32,129]{3,2,1,0:T(8,128)S(1)} fusion(f32[42,3,32,130]{3,2,1,0:T(8,128)S(1)} %get-tuple-element.16, f32[42,3,32,130]{3,2,1,0:T(8,128)S(1)} %get-tuple-element.15, f32[3,32,129]{2,1,0:T(8,128)S(1)} %get-tuple-element.7, f32[3,32,129]{2,1,0:T(8,128)S(1)} %bitcast.56), kind=kLoop, calls=%fused_computation.8 | loop fusion | flops 6439680 | bytes 10006272 | tf_op jit(solution)/shard_map/add | solution.py:44
  55.2 2.1 %fusion.6 = f32[40,3,32,128]{3,2,1,0:T(8,128)} fusion(f32[40,3,32,128]{3,2,1,0:T(8,128)S(1)} %fusion.8, f32[40,3,32,129]{3,2,1,0:T(8,128)S(1)} %multiply_add_fusion, f32[40,3,32,128]{3,2,1,0:T(8,128)S(1)} %bitcast.46, f32[3,32,128]{2,1,0:T(8,128)S(1)} %get-tuple-element.24, f32[3,32,128]{2,1,0:T(8,128)S(1)} %fusion.13), kind=kLoop, calls=%fused_computation.16 | loop fusion | flops 2949120 | bytes 9928704 | tf_op jit(solution)/shard_map/add | solution.py:138
  (49 shorter events, 1.3 us)
Async XLA Ops:
  0.0 8.2 %copy-start = (f32[40,3,32,128]{3,2,1,0:T(8,128)S(1)}, f32[40,3,32,128]{3,2,1,0:T(8,128)}, u32[]{:S(2)}) copy-start(f32[40,3,32,128]{3,2,1,0:T(8,128)} %param.11) | copy-start | bytes 5898244
  1.0 7.3 %slice-start = ((f32[40,3,32,128]{3,2,1,0:T(8,128)}), f32[4,3,32,128]{3,2,1,0:T(8,128)S(1)}, s32[]{:S(2)}) async-start(f32[40,3,32,128]{3,2,1,0:T(8,128)} %param.11), calls=%async_computation | async-start | bytes 393216 | tf_op jit(solution)/shard_map/slice | solution.py:64
  1.0 7.4 %copy-start.7 = (f32[4,26]{1,0:T(4,128)S(1)}, f32[4,26]{1,0:T(4,128)}, u32[]{:S(2)}) copy-start(f32[4,26]{1,0:T(4,128)} %param.16) | copy-start | bytes 1252
  2.3 18.8 %collective-permute-start = (f32[43,3,2,128]{3,0,2,1:T(8,128)S(1)}, f32[43,3,2,128]{3,0,2,1:T(8,128)}, u32[]{:S(2)}, u32[]{:S(2)}) collective-permute-start(f32[43,3,2,128]{3,0,2,1:T(8,128)S(1)} %copy.31), channel_id=1, source_target_pairs={{4,0},{8,4},{12,8},{0,12},{5,1},{9,5},{13,9},{1,13},{6,2},{10,6},{... | collective-permute-start | bytes 396296 | tf_op jit(solution)/shard_map/ppermute | solution.py:24
  8.2 13.9 %collective-permute-start.1 = (f32[43,3,2,128]{3,0,2,1:T(8,128)}, f32[43,3,2,128]{3,0,2,1:T(8,128)}, u32[]{:S(2)}, u32[]{:S(2)}) collective-permute-start(f32[43,3,2,128]{3,0,2,1:T(8,128)} %copy.33), channel_id=1, source_target_pairs={{0,4},{4,8},{8,12},{12,0},{1,5},{5,9},{9,13},{13,1},{2,6},{6,10},{... | collective-permute-start | bytes 396296 | tf_op jit(solution)/shard_map/ppermute | solution.py:23
  13.4 0.7 %copy-start.6 = (f32[32,128]{1,0:T(8,128)S(1)}, f32[32,128]{1,0:T(8,128)}, u32[]{:S(2)}) copy-start(f32[32,128]{1,0:T(8,128)} %param.14) | copy-start | bytes 49156
  13.4 0.8 %copy-start.9 = (f32[26]{0:T(128)S(1)}, f32[26]{0:T(128)}, u32[]{:S(2)}) copy-start(f32[26]{0:T(128)} %param.17) | copy-start | bytes 316
  13.4 0.8 %copy-start.10 = (f32[26]{0:T(128)S(1)}, f32[26]{0:T(128)}, u32[]{:S(2)}) copy-start(f32[26]{0:T(128)} %param.15) | copy-start | bytes 316
  15.8 0.7 %copy-start.11 = (s32[10,26]{1,0:T(8,128)S(1)}, s32[10,26]{1,0:T(8,128)}, u32[]{:S(2)}) copy-start(s32[10,26]{1,0:T(8,128)} %param.20) | copy-start | bytes 3124
  15.8 0.7 %copy-start.12 = (f32[10]{0:T(128)S(1)}, f32[10]{0:T(128)}, u32[]{:S(2)}) copy-start(f32[10]{0:T(128)} %param.19) | copy-start | bytes 124
  15.9 0.7 %copy-start.13 = (f32[10]{0:T(128)S(1)}, f32[10]{0:T(128)}, u32[]{:S(2)}) copy-start(f32[10]{0:T(128)} %param.18) | copy-start | bytes 124
  16.5 1.2 %copy-start.8 = (f32[4]{0:T(128)S(1)}, f32[4]{0:T(128)}, u32[]{:S(2)}) copy-start(f32[4]{0:T(128)} %param.21) | copy-start | bytes 52
  17.9 3.2 %copy-start.5 = (f32[2,3,32,128]{3,2,1,0:T(8,128)S(1)}, f32[2,3,32,128]{3,2,1,0:T(8,128)}, u32[]{:S(2)}) copy-start(f32[2,3,32,128]{3,2,1,0:T(8,128)} %param.12) | copy-start | bytes 294916
  23.7 1.6 %copy-start.1 = (f32[40,3,32,128]{3,2,1,0:T(8,128)S(1)}, f32[40,3,32,128]{3,2,1,0:T(8,128)}, u32[]{:S(2)}) copy-start(f32[40,3,32,128]{3,2,1,0:T(8,128)} %param.11) | copy-start | bytes 5898244
  31.3 10.4 %collective-permute-start.2 = (f32[42,3,32,2]{0,2,3,1:T(8,128)S(1)}, f32[42,3,32,2]{0,2,3,1:T(8,128)S(1)}, u32[]{:S(2)}, u32[]{:S(2)}) collective-permute-start(f32[42,3,32,2]{0,2,3,1:T(8,128)S(1)} %copy.35), channel_id=1, source_target_pairs={{1,0},{2,1},{3,2},{5,4},{6,5},{7,6},{9,8},{10,9},{11,10},{13,12},{... | collective-permute-start | bytes 96776 | tf_op jit(solution)/shard_map/ppermute | solution.py:24
  35.4 9.4 %collective-permute-start.3 = (f32[42,3,32,2]{0,2,3,1:T(8,128)S(1)}, f32[42,3,32,2]{0,2,3,1:T(8,128)S(1)}, u32[]{:S(2)}, u32[]{:S(2)}) collective-permute-start(f32[42,3,32,2]{0,2,3,1:T(8,128)S(1)} %copy.37), channel_id=1, source_target_pairs={{0,1},{1,2},{2,3},{4,5},{5,6},{6,7},{8,9},{9,10},{10,11},{12,13},{... | collective-permute-start | bytes 96776 | tf_op jit(solution)/shard_map/ppermute | solution.py:23
  47.8 1.6 %copy-start.2 = (f32[42,3,32,2]{3,2,1,0:T(8,128)S(1)}, f32[42,3,32,2]{3,2,1,0:T(8,128)}, u32[]{:S(2)}) copy-start(f32[42,3,32,2]{3,2,1,0:T(8,128)} %copy.36) | copy-start | bytes 96772
  47.8 2.3 %copy-start.3 = (f32[42,3,32,2]{3,2,1,0:T(8,128)S(1)}, f32[42,3,32,2]{3,2,1,0:T(8,128)}, u32[]{:S(2)}) copy-start(f32[42,3,32,2]{3,2,1,0:T(8,128)} %copy.38) | copy-start | bytes 96772
  52.7 2.5 %copy-start.4 = (f32[5,8,96,128]{3,2,1,0:T(8,128)S(1)}, f32[5,8,96,128]{3,2,1,0:T(8,128)}, u32[]{:S(2)}) copy-start(f32[5,8,96,128]{3,2,1,0:T(8,128)} %copy.44) | copy-start | bytes 5898244
where the time goes:
time: 58.3 us; the launch traced here: 57.3 us
  local copies, waits for them, and re-layouts  22.6 us (39%)
  other arithmetic  20.5 us (35%)
  starting transfers between devices  9.44 us (16%)
  matrix products  4.4 us (8%)
    ppermute x2, starting transfers between devices, extended(): after = lax.ppermute(first, axis, down)  6.41 us
    slice x3, local copies, waits for them, and re-layouts, extended(): last = lax.slice_in_dim(array, length - width, length, axis=dim)  6.08 us
    unnamed x37, local copies, waits for them, and re-layouts  5.74 us
    reduce_min x1, other arithmetic, ecology(): nutrient_limit = jnp.min(saturation, axis=0)  4.58 us
    add x2, other arithmetic, advect(): face_flux + jnp.abs(transport) * (1.0 / 12.0) * (far_right - 3.0 * near_r...  4.1 us
    ppermute x2, local copies, waits for them, and re-layouts, extended(): before = lax.ppermute(last, axis, up)  4.02 us
    ppermute x2, local copies, waits for them, and re-layouts, extended(): after = lax.ppermute(first, axis, down)  4.01 us
    dot_general x1, matrix products, ecology(): jnp.dot(prey_weights.T, grazing_rate, precision=lax.Precision.HIGHEST)  3.21 us
  transfers between devices with their start and end apart: 4, of which 0 were waited for; matrix products, arithmetic and copies ran while one was open for 40% of the time, Pallas kernels for 0%

commit v1 on v0

v1 whole, which is shorter than its diff:
```python
import functools

import jax
import jax.numpy as jnp
from jax import lax
from jax.experimental import pallas as pl
from jax.experimental.pallas import tpu as pltpu
from jax.sharding import PartitionSpec as P

NNUT = 4
NPHY = 26
PAD = 4

plankton_mortality = 0.05
grazer_mortality = 0.3
assimilation = 0.3
attenuation = 0.4

VMEM = pl.BlockSpec(memory_space=pltpu.VMEM)
SMEM = pl.BlockSpec(memory_space=pltpu.SMEM)
ANY = pl.BlockSpec(memory_space=pl.ANY)


def in_vmem(array):
    return pltpu.with_memory_space_constraint(array, pltpu.VMEM)


def call(kernel, outs, specs, scratch=(), flops=0, bytes_accessed=0, limit=8 << 20, **more):
    return pl.pallas_call(
        kernel,
        out_shape=outs,
        in_specs=specs,
        scratch_shapes=list(scratch),
        cost_estimate=pl.CostEstimate(flops=flops, bytes_accessed=bytes_accessed, transcendentals=0),
        compiler_params=pltpu.CompilerParams(vmem_limit_bytes=limit),
        **more,
    )


def pack_rows(tracers, velocity, mask, first, last, edge, sems):
    count, length = tracers.shape[0], tracers.shape[1]
    levels = mask.shape[0]
    groups = first.shape[0]
    copies = []
    for side, (out, start) in enumerate(((first, 0), (last, length - 2))):
        rows = pl.ds(start, 2)
        copies += [
            pltpu.make_async_copy(tracers.at[:, rows], out.at[pl.ds(PAD, count)], sems.at[side, 0]),
            pltpu.make_async_copy(
                velocity.at[0, :, rows], out.at[pl.ds(PAD + count, levels)], sems.at[side, 1]
            ),
            pltpu.make_async_copy(mask.at[:, rows], edge.at[side], sems.at[side, 2]),
        ]
    for copy in copies:
        copy.start()
    for out in (first, last):
        out[0:PAD] = jnp.zeros((PAD,) + out.shape[1:], out.dtype)
        out[groups - PAD : groups] = jnp.zeros((PAD,) + out.shape[1:], out.dtype)
    for copy in copies:
        copy.wait()
    for side, out in enumerate((first, last)):
        out[PAD + count + levels : PAD + count + 2 * levels] = edge[side].astype(jnp.float32)


def ecology(
    tracers,
    mask,
    sunlight,
    growth_max,
    half_sat,
    light_half,
    graze_max,
    graze_half,
    palatable,
    stoichiometry,
    tendency,
):
    count, levels, length, _ = tracers.shape
    grazers = count - NNUT - NPHY
    chunk = 16 if length % 16 == 0 else 8

    def level_step(level, carry):
        depth = jnp.exp(
            jnp.full((8, 128), -attenuation, jnp.float32) * (level.astype(jnp.float32) + 0.5)
        )[0:1, 0:1]
        for start in range(0, length, chunk):
            rows = pl.ds(start, chunk)
            wet = mask[level, rows].astype(jnp.float32)
            darkness = 1.0 / (sunlight[rows] * depth)
            scarcity = [1.0 / tracers[j, level, rows] for j in range(NNUT)]
            available = [None] * grazers
            eaten = None
            total_growth = None
            for k in range(NPHY):
                plant = tracers[NNUT + k, level, rows]
                worst = half_sat[0, k] * scarcity[0]
                for j in range(1, NNUT):
                    worst = jnp.maximum(worst, half_sat[j, k] * scarcity[j])
                growth = (growth_max[k] * plant) / (
                    (1.0 + worst) * (1.0 + light_half[k] * darkness)
                )
                tendency[NNUT + k, level, rows] = growth - plankton_mortality * plant
                total_growth = growth if total_growth is None else total_growth + growth
                eaten = plant if eaten is None else eaten + plant
                for z in range(grazers):
                    term = palatable[z, k] * plant
                    available[z] = term if available[z] is None else available[z] + term
            recycled = plankton_mortality * eaten - total_growth
            rates = []
            for z in range(grazers):
                grazer = tracers[NNUT + NPHY + z, level, rows]
                rate = graze_max[z] * grazer / (graze_half[z] + available[z])
                ingested = rate * available[z]
                loss = grazer_mortality * grazer * grazer
                tendency[NNUT + NPHY + z, level, rows] = wet * (assimilation * ingested - loss)
                recycled = recycled + (loss + (1.0 - assimilation) * ingested)
                rates.append(rate)
            for j in range(NNUT):
                tendency[j, level, rows] = wet * (stoichiometry[j] * recycled)
            for k in range(NPHY):
                pressure = palatable[0, k] * rates[0]
                for z in range(1, grazers):
                    pressure = pressure + palatable[z, k] * rates[z]
                plant = tracers[NNUT + k, level, rows]
                tendency[NNUT + k, level, rows] = wet * (
                    tendency[NNUT + k, level, rows] - plant * pressure
                )
        return carry

    lax.fori_loop(0, levels, level_step, 0)


def face_terms(u):
    up, down = jnp.maximum(u, 0.0), jnp.minimum(u, 0.0)
    return (
        up * (-1.0 / 6.0),
        up * (5.0 / 6.0) + down * (1.0 / 3.0),
        up * (1.0 / 3.0) + down * (5.0 / 6.0),
        down * (-1.0 / 6.0),
    )


def stencil(lower, upper):
    a0, b0, d0, e0 = face_terms(lower)
    a1, b1, d1, e1 = face_terms(upper)
    return a0, b0 - a1, 1.0 + (upper - lower) + d0 - b1, e0 - d1, -e1


def along(tracers, velocity, mask, before, after, swept, pack_left, pack_right, weights):
    count, levels, length, lanes = tracers.shape
    blocks = length // 8
    rows = lax.broadcasted_iota(jnp.int32, (length, lanes), 0)
    row8 = lax.broadcasted_iota(jnp.int32, (8, lanes), 0)
    slot = lax.broadcasted_iota(jnp.int32, (8, lanes), 1) // 2
    base = 2 * PAD

    def level_step(level, carry):
        wet = mask[level].astype(jnp.float32)
        flow = velocity[0, level]
        pick = lambda ref, field, row: ref[pl.ds(base + 2 * ((count + field) * levels + level) + row, 1)]
        wet_before, wet_after = pick(before, 1, 1), pick(after, 1, 0)
        flow_after = pick(after, 0, 0)
        wet_up = jnp.where(rows == 0, wet_before, pltpu.roll(wet, 1, 0))
        lower = flow * (wet_up * wet)
        upper = jnp.where(
            rows == length - 1,
            flow_after * (wet * wet_after),
            pltpu.roll(lower, length - 1, 0),
        )
        for n, w in enumerate(stencil(lower, upper)):
            weights[n] = w
        for block in range(blocks):
            here = pl.ds(8 * block, 8)
            wm2, wm1, w0, wp1, wp2 = [weights[n, here] for n in range(5)]
            top, bottom = block == 0, block == blocks - 1
            if top:
                zm2, zm1 = jnp.where(row8 < 2, wm2, 0.0), jnp.where(row8 < 1, wm1, 0.0)
                wm2, wm1 = jnp.where(row8 < 2, 0.0, wm2), jnp.where(row8 < 1, 0.0, wm1)
            if bottom:
                zp2, zp1 = jnp.where(row8 > 5, wp2, 0.0), jnp.where(row8 > 6, wp1, 0.0)
                wp2, wp1 = jnp.where(row8 > 5, 0.0, wp2), jnp.where(row8 > 6, 0.0, wp1)
            right = jnp.zeros((8, lanes), jnp.float32)
            left = right
            for t in range(count):
                centre = tracers[t, level, here]

                def shifted(offset):
                    if (top and offset < 0) or (bottom and offset > 0):
                        return pltpu.roll(centre, -offset % 8, 0)
                    return tracers[t, level, pl.ds(8 * block + offset, 8)]

                value = (
                    w0 * centre
                    + (wm1 * shifted(-1) + wm2 * shifted(-2))
                    + (wp1 * shifted(1) + wp2 * shifted(2))
                )
                group = base + 2 * (t * levels + level)
                if top:
                    value = value + (
                        zm2 * before[pl.ds(group, 8)] + zm1 * before[pl.ds(group + 1, 8)]
                    )
                if bottom:
                    value = value + (
                        zp2 * after[pl.ds(group - 6, 8)] + zp1 * after[pl.ds(group - 7, 8)]
                    )
                swept[t, level, here] = value
                turned = pltpu.roll(value, 2 * t + 2, 1)
                right = jnp.where(slot == t, turned, right)
                left = jnp.where(slot == t + 1, turned, left)
            across_flow = velocity[1, level, here]
            wet_here = mask[level, here].astype(jnp.float32)
            for t, value in ((count, across_flow), (count + 1, wet_here)):
                turned = pltpu.roll(value, 2 * t + 2, 1)
                right = jnp.where(slot == t, turned, right)
                left = jnp.where(slot == t + 1, turned, left)
            pack_right[level, here] = right
            pack_left[level, here] = left
        return carry

    lax.fori_loop(0, levels, level_step, 0)


def across(swept, velocity, mask, tendency, partial):
    count, levels, length, lanes = swept.shape
    blocks = length // 8
    lane = lax.broadcasted_iota(jnp.int32, (8, lanes), 1)

    def level_step(level, carry):
        for block in range(blocks):
            here = pl.ds(8 * block, 8)
            wet = mask[level, here].astype(jnp.float32)
            lower = jnp.where(lane == 0, 0.0, velocity[1, level, here] * wet * pltpu.roll(wet, 1, 1))
            upper = pltpu.roll(lower, lanes - 1, 1)
            wm2, wm1, w0, wp1, wp2 = stencil(lower, upper)
            wm2 = jnp.where(lane < 2, 0.0, wm2)
            wm1 = jnp.where(lane < 1, 0.0, wm1)
            wp1 = jnp.where(lane > lanes - 2, 0.0, wp1)
            wp2 = jnp.where(lane > lanes - 3, 0.0, wp2)
            for t in range(count):
                centre = swept[t, level, here]
                partial[t, level, here] = (
                    (tendency[t, level, here] + w0 * centre)
                    + (wm1 * pltpu.roll(centre, 1, 1) + wm2 * pltpu.roll(centre, 2, 1))
                    + (wp1 * pltpu.roll(centre, lanes - 1, 1) + wp2 * pltpu.roll(centre, lanes - 2, 1))
                )
        return carry

    lax.fori_loop(0, levels, level_step, 0)


def finish(
    partial, velocity, mask, my_left, my_right, from_left, from_right, edges, updated, even, odd, done, sems
):
    count, levels, length, lanes = partial.shape
    blocks = length // 8
    lane = lax.broadcasted_iota(jnp.int32, (8, lanes), 1)
    is_odd = lane % 2 == 1
    slot_odd = (lane // 2) % 2 == 1
    has_left, has_right = edges[0], edges[1]

    def level_step(level, carry):
        for block in range(blocks):
            here = pl.ds(8 * block, 8)
            wet = mask[level, here].astype(jnp.float32)
            flow = velocity[1, level, here]
            own_left = pltpu.roll(my_left[level, here], lanes - 2, 1)
            own_right = my_right[level, here]
            left = from_left[level, here] * has_left
            right = pltpu.roll(from_right[level, here], lanes - 2, 1) * has_right
            col = lambda value, n: jnp.broadcast_to(value[:, n : n + 1], value.shape)
            s_wet, s_flow = 2 * (count + 1), 2 * count
            wet_first, wet_last = col(wet, 0), col(wet, lanes - 1)
            u0 = col(flow, 0) * (wet_first * col(left, s_wet + 1))
            u1 = col(flow, 1) * (wet_first * col(wet, 1))
            u127 = col(flow, lanes - 1) * (wet_last * col(wet, lanes - 2))
            u128 = col(right, s_flow) * (wet_last * col(right, s_wet))
            a0, b0, d0, e0 = face_terms(u0)
            a1 = face_terms(u1)[0]
            e127 = face_terms(u127)[3]
            a128, b128, d128, e128 = face_terms(u128)
            low = (
                jnp.where(is_odd, a1, a0) * left
                + jnp.where(is_odd, 0.0, b0 - a1) * pltpu.roll(left, lanes - 1, 1)
                + jnp.where(is_odd, 0.0, d0 - u0) * own_left
                + jnp.where(is_odd, 0.0, e0) * pltpu.roll(own_left, lanes - 1, 1)
            )
            high = (
                jnp.where(is_odd, -e128, -e127) * right
                + jnp.where(is_odd, e127 - d128, 0.0) * pltpu.roll(right, 1, 1)
                + jnp.where(is_odd, u128 - b128, 0.0) * own_right
                + jnp.where(is_odd, -a128, 0.0) * pltpu.roll(own_right, 1, 1)
            )
            high = pltpu.roll(high, lanes - 2, 1)
            even[level, here] = jnp.where(slot_odd, high, low)
            odd[level, here] = jnp.where(slot_odd, low, high)
        return carry

    lax.fori_loop(0, levels, level_step, 0)
    outer = (lane < 2) | (lane > lanes - 3)
    step = max(n for n in (10, 8, 5, 4, 2, 1) if count % n == 0)
    copies = []
    for first in range(0, count, step):

        def level_add(level, carry):
            for block in range(blocks):
                here = pl.ds(8 * block, 8)
                packs = (even[level, here], odd[level, here])
                for t in range(first, first + step):
                    edge = pltpu.roll(packs[t % 2], -2 * t % lanes, 1)
                    done[t, level, here] = partial[t, level, here] + jnp.where(outer, edge, 0.0)
            return carry

        lax.fori_loop(0, levels, level_add, 0)
        part = pl.ds(first, step)
        copies.append(pltpu.make_async_copy(done.at[part], updated.at[part], sems.at[first // step]))
        copies[-1].start()
    for copy in copies:
        copy.wait()


def shards(
    tracers,
    velocity,
    land_mask,
    sunlight,
    growth_max,
    half_sat,
    light_half,
    graze_max,
    graze_half,
    palatable,
    stoichiometry,
):
    f32 = jnp.float32
    count, levels, length, lanes = tracers.shape
    tx, ty = lax.axis_size("tx"), lax.axis_size("ty")
    up = lambda n: [(i, (i + 1) % n) for i in range(n)]
    down = lambda n: [((i + 1) % n, i) for i in range(n)]
    cells = count * levels * length * lanes

    groups = 2 * PAD + (count + 2) * levels
    row_message = pltpu.VMEM((groups, 2, 1, lanes), f32)
    first, last = call(
        pack_rows,
        (row_message, row_message),
        [ANY, ANY, ANY],
        scratch=[pltpu.VMEM((2, levels, 2, 1, lanes), jnp.int32), pltpu.SemaphoreType.DMA((2, 3))],
        bytes_accessed=8 * groups * lanes,
        limit=2 << 20,
    )(
        tracers.reshape(count * levels, length, 1, lanes),
        velocity.reshape(2, levels, length, 1, lanes),
        land_mask.reshape(levels, length, 1, lanes),
    )
    first, last = first.reshape(2 * groups, lanes), last.reshape(2 * groups, lanes)
    before = lax.ppermute(last, "tx", up(tx))
    after = lax.ppermute(first, "tx", down(tx))

    held, flow, mask = in_vmem(tracers), in_vmem(velocity), in_vmem(land_mask)
    tendency = call(
        ecology,
        pltpu.VMEM(tracers.shape, f32),
        [VMEM, VMEM, VMEM] + [SMEM] * 7,
        flops=40 * cells,
        bytes_accessed=8 * cells,
        limit=2 << 20,
    )(
        held,
        mask,
        in_vmem(sunlight),
        growth_max,
        half_sat,
        light_half,
        graze_max,
        graze_half,
        palatable.astype(f32),
        stoichiometry,
    )
    column_message = pltpu.VMEM((levels, length, lanes), f32)
    swept, pack_left, pack_right = call(
        along,
        (pltpu.VMEM(tracers.shape, f32), column_message, column_message),
        [VMEM] * 5,
        scratch=[pltpu.VMEM((5, length, lanes), f32)],
        flops=20 * cells,
        bytes_accessed=8 * cells,
        limit=2 << 20,
    )(held, flow, mask, in_vmem(before), in_vmem(after))
    from_left = lax.ppermute(pack_right, "ty", up(ty))
    from_right = lax.ppermute(pack_left, "ty", down(ty))
    partial = call(
        across,
        pltpu.VMEM(tracers.shape, f32),
        [VMEM] * 4,
        flops=20 * cells,
        bytes_accessed=12 * cells,
        limit=2 << 20,
    )(swept, flow, mask, tendency)
    place = lax.axis_index("ty")
    edges = jnp.stack([place > 0, place < ty - 1]).astype(f32)
    return call(
        finish,
        jax.ShapeDtypeStruct(tracers.shape, f32),
        [VMEM] * 7 + [SMEM],
        out_specs=ANY,
        scratch=[
            pltpu.VMEM((levels, length, lanes), f32),
            pltpu.VMEM((levels, length, lanes), f32),
            pltpu.VMEM(tracers.shape, f32),
            pltpu.SemaphoreType.DMA((count,)),
        ],
        flops=4 * cells,
        bytes_accessed=8 * cells,
        limit=4 << 20,
    )(partial, flow, mask, pack_left, pack_right, in_vmem(from_left), in_vmem(from_right), edges)


def solution(mesh):
    return jax.shard_map(
        shards,
        mesh=mesh,
        in_specs=(
            P("member", None, "tx", "ty"),
            P(None, None, "tx", "ty"),
            P(None, "tx", "ty"),
            P("tx", "ty"),
            P("member"),
            P("member", None),
            P("member"),
            P("member"),
            P("member"),
            P("member", None),
            P(),
        ),
        out_specs=P("member", None, "tx", "ty"),
        check_vma=False,
    )
```

time: 58.3 us -> 28.9 us (0.50); the launches traced: 57.3 us -> 28.7 us
  other arithmetic: 20.5 us -> 0.08 us
  local copies, waits for them, and re-layouts: 22.6 us -> 3.51 us
  Pallas kernels: 0 us -> 11.9 us
  waiting for transfers between devices: 0.01 us -> 6.08 us
  matrix products: 4.4 us -> 0 us
  starting transfers between devices: 9.44 us -> 6.99 us
    pallas_call x0 -> x5, Pallas kernels: none -> 11.9 us  [the longest x1 4 us: shards(): call(ecology, pltpu.VMEM(tracers.shape, f32), [VMEM, VMEM, VMEM] + [SMEM]...]
    slice x8 -> x0, local copies, waits for them, and re-layouts: 8.84 us -> none  [the longest x3 6.08 us: extended(): last = lax.slice_in_dim(array, length - width, length, axis=dim)]
    ppermute x4 -> x0, local copies, waits for them, and re-layouts: 8.02 us -> none  [the longest x2 4.02 us: extended(): before = lax.ppermute(last, axis, up)]
    add x5 -> x0, other arithmetic: 6.62 us -> none  [the longest x2 4.1 us: advect(): face_flux + jnp.abs(transport) * (1.0 / 12.0) * (far_right - 3.0 * near_r...]
    ppermute x4, waiting for transfers between devices: 0.01 us -> 6.08 us  [the longest x1 4.35 us: shards(): before = lax.ppermute(last, 'tx', up(tx))]
    concatenate x4 -> x0, other arithmetic: 4.64 us -> none  [the longest x2 3.11 us: extended(): array = jnp.concatenate([before, array, after], axis=dim)]
    reduce_min x1 -> x0, other arithmetic: 4.58 us -> none  [ecology(): nutrient_limit = jnp.min(saturation, axis=0)]
    dot_general x2 -> x0, matrix products: 4.4 us -> none  [the longest x1 3.21 us: ecology(): jnp.dot(prey_weights.T, grazing_rate, precision=lax.Precision.HIGHEST)]
  transfers between devices with their start and end apart: 4 -> 4, of which waited for: 0 -> 2; matrix products, arithmetic and copies ran while one was open for 40% -> 1% of each run, Pallas kernels for 0% -> 23%
where the time goes in v1:
time: 28.9 us; the launch traced here: 28.7 us
  Pallas kernels  11.9 us (41%)
  starting transfers between devices  6.99 us (24%)
  waiting for transfers between devices  6.08 us (21%)
  local copies, waits for them, and re-layouts  3.51 us (12%)
    ppermute x1, waiting for transfers between devices, shards(): before = lax.ppermute(last, 'tx', up(tx))  4.35 us
    pallas_call x1, Pallas kernels, shards(): call(ecology, pltpu.VMEM(tracers.shape, f32), [VMEM, VMEM, VMEM] + [SMEM]...  4 us
    pallas_call x1, Pallas kernels, shards(): call(finish, jax.ShapeDtypeStruct(tracers.shape, f32), [VMEM] * 7 + [SMEM...  3.72 us
    unnamed x32, local copies, waits for them, and re-layouts  3.51 us
    ppermute x1, starting transfers between devices, shards(): before = lax.ppermute(last, 'tx', up(tx))  3.1 us
    pallas_call x1, Pallas kernels, shards(): call(across, pltpu.VMEM(tracers.shape, f32), [VMEM] * 4, flops=20 * cells...  2.48 us
    ppermute x1, starting transfers between devices, shards(): after = lax.ppermute(first, 'tx', down(tx))  2.1 us
    ppermute x1, starting transfers between devices, shards(): from_right = lax.ppermute(pack_left, 'ty', down(ty))  1.73 us
  transfers between devices with their start and end apart: 4, of which 2 were waited for; matrix products, arithmetic and copies ran while one was open for 1% of the time, Pallas kernels for 23%

profile of v1, /device:TPU:0, one launch (start us, length us, event | category | flops | bytes accessed | tf_op | source)
XLA Modules:
  0.0 28.7 jit_solution(17046823578511008528)
XLA Ops:
  0.0 1.5 %copy-done = f32[40,3,32,128]{3,2,1,0:T(8,128)S(1)} copy-done((f32[40,3,32,128]{3,2,1,0:T(8,128)S(1)}, f32[40,3,32,128]{3,2,1,0:T(8,128)}, u32[]{:S(2)}) %copy-start) | copy-done | bytes 1966104
  1.5 0.9 %copy-done.2 = f32[2,3,32,128]{3,2,1,0:T(8,128)S(1)} copy-done((f32[2,3,32,128]{3,2,1,0:T(8,128)S(1)}, f32[2,3,32,128]{3,2,1,0:T(8,128)}, u32[]{:S(2)}) %copy-start.2) | copy-done | bytes 98328
  2.4 0.8 %copy-done.4 = s32[3,32,128]{2,1,0:T(8,128)S(1)} copy-done((s32[3,32,128]{2,1,0:T(8,128)S(1)}, s32[3,32,128]{2,1,0:T(8,128)}, u32[]{:S(2)}) %copy-start.4) | copy-done | bytes 49176
  3.2 0.2 shard_map.109
  3.5 0.0 copy-start.13
  3.5 0.0 copy-start.6
  3.5 0.0 copy-start.7
  3.5 0.0 copy-start.8
  3.5 0.0 copy-start.9
  3.5 0.0 copy-start.10
  3.5 0.0 copy-start.11
  3.5 0.0 copy-start.12
  3.6 0.1 pad.4
  3.7 3.1 %collective-permute-start = (f32[268,128]{1,0:T(8,128)S(1)}, f32[268,128]{1,0:T(8,128)S(1)}, u32[]{:S(2)}, u32[]{:S(2)}) collective-permute-start(f32[268,128]{1,0:T(8,128)S(1)} %bitcast.22), channel_id=1, source_target_pairs={{0,4},{4,8},{8,12},{12,0},{1,5},{5,9},{9,13},{13,1},{2,6},{6,10},{... | collective-permute-start | bytes 411656 | tf_op jit(solution)/shard_map/ppermute | solution.py:356
  6.8 0.1 pad.5
  6.9 2.1 %collective-permute-start.1 = (f32[268,128]{1,0:T(8,128)S(1)}, f32[268,128]{1,0:T(8,128)S(1)}, u32[]{:S(2)}, u32[]{:S(2)}) collective-permute-start(f32[268,128]{1,0:T(8,128)S(1)} %bitcast.23), channel_id=1, source_target_pairs={{4,0},{8,4},{12,8},{0,12},{5,1},{9,5},{13,9},{1,13},{6,2},{10,6},{... | collective-permute-start | bytes 411656 | tf_op jit(solution)/shard_map/ppermute | solution.py:357
  9.0 4.3 %collective-permute-done.before = f32[268,128]{1,0:T(8,128)S(1)} collective-permute-done((f32[268,128]{1,0:T(8,128)S(1)}, f32[268,128]{1,0:T(8,128)S(1)}, u32[]{:S(2)}, u32[]{:S(2)}) %collective-permute-start) | collective-permute-done | bytes 137248 | tf_op jit(solution)/shard_map/ppermute | solution.py:356
  13.4 1.7 %collective-permute-done.1.after = f32[268,128]{1,0:T(8,128)S(1)} collective-permute-done((f32[268,128]{1,0:T(8,128)S(1)}, f32[268,128]{1,0:T(8,128)S(1)}, u32[]{:S(2)}, u32[]{:S(2)}) %collective-permute-start.1) | collective-permute-done | bytes 137248 | tf_op jit(solution)/shard_map/ppermute | solution.py:357
  15.1 0.0 copy-done.1
  15.1 0.0 copy-done.3
  15.1 0.0 copy-done.5
  15.1 1.4 %shard_map.110 = (f32[40,3,32,128]{3,2,1,0:T(8,128)S(1)}, f32[3,32,128]{2,1,0:T(8,128)S(1)}, f32[3,32,128]{2,1,0:T(8,128)S(1)}) custom-call(f32[40,3,32,128]{3,2,1,0:T(8,128)S(1)} %copy-done.1, f32[2,3,32,128]{3,2,1,0:T(8,128)S(1)} %copy-done.3, s32[3,32,128]{2,1,0:T(8,128)S(1)} %copy-done.5, f32[268,128]{1,0:T(8,128)S(1)} %collective-permute-done.before, ...), custom_call_target="tpu_custom_call" | custom-call | flops 9830400 | bytes 3932160 | tf_op jit(solution)/shard_map/pallas_call | solution.py:380
  16.5 0.1 collective-permute-start.2
  16.6 1.7 %collective-permute-start.3 = (f32[3,32,128]{2,1,0:T(8,128)S(1)}, f32[3,32,128]{2,1,0:T(8,128)S(1)}, u32[]{:S(2)}, u32[]{:S(2)}) collective-permute-start(f32[3,32,128]{2,1,0:T(8,128)S(1)} %get-tuple-element.13.my_left), channel_id=1, source_target_pairs={{1,0},{2,1},{3,2},{0,3},{5,4},{6,5},{7,6},{4,7},{9,8},{10,9},{11,1... | collective-permute-start | bytes 147464 | tf_op jit(solution)/shard_map/ppermute | solution.py:390
  18.3 0.1 add_convert_fusion.edges
  18.4 0.0 copy-done.13
  18.4 0.0 copy-done.6
  18.5 4.0 %shard_map.111.tendency = f32[40,3,32,128]{3,2,1,0:T(8,128)S(1)} custom-call(f32[40,3,32,128]{3,2,1,0:T(8,128)S(1)} %copy-done.1, s32[3,32,128]{2,1,0:T(8,128)S(1)} %copy-done.5, f32[32,128]{1,0:T(8,128)S(1)} %copy-done.6, f32[26]{0:T(128)S(1)} %copy-done.8, f32[4,26]{1,0:T(4,128)S(1)} %copy-done.7, f32[26]{0:T(128)S(1)} %copy-done.9, f32[10]{0:T(128)S(1)} %copy-done.10, ...), custom_call_target="tpu_custom_call" | custom-call | flops 19660800 | bytes 3932160 | tf_op jit(solution)/shard_map/pallas_call | solution.py:360
  22.5 2.5 %shard_map.112.partial = f32[40,3,32,128]{3,2,1,0:T(8,128)S(1)} custom-call(f32[40,3,32,128]{3,2,1,0:T(8,128)S(1)} %get-tuple-element.12.swept, f32[2,3,32,128]{3,2,1,0:T(8,128)S(1)} %copy-done.3, s32[3,32,128]{2,1,0:T(8,128)S(1)} %copy-done.5, f32[40,3,32,128]{3,2,1,0:T(8,128)S(1)} %shard_map.111.tendency), custom_call_target="tpu_custom_call" | custom-call | flops 9830400 | bytes 5898240 | tf_op jit(solution)/shard_map/pallas_call | solution.py:391
  25.0 0.0 collective-permute-done.2.from_left
  25.0 0.0 collective-permute-done.3.from_right
  25.0 3.7 %shard_map.113 = f32[40,3,32,128]{3,2,1,0:T(8,128)} custom-call(f32[40,3,32,128]{3,2,1,0:T(8,128)S(1)} %shard_map.112.partial, f32[2,3,32,128]{3,2,1,0:T(8,128)S(1)} %copy-done.3, s32[3,32,128]{2,1,0:T(8,128)S(1)} %copy-done.5, f32[3,32,128]{2,1,0:T(8,128)S(1)} %get-tuple-element.13.my_left, f32[3,32,128]{2,1,0:T(8,128)S(1)} %get-tuple-element.14.my_right, ...), custom_call_target="tpu_custom_call" | custom-call | flops 1966080 | bytes 3932160 | tf_op jit(solution)/shard_map/pallas_call | solution.py:401
  (15 shorter events, 0.0 us)
Async XLA Ops:
  0.0 1.5 %copy-start = (f32[40,3,32,128]{3,2,1,0:T(8,128)S(1)}, f32[40,3,32,128]{3,2,1,0:T(8,128)}, u32[]{:S(2)}) copy-start(f32[40,3,32,128]{3,2,1,0:T(8,128)} %tracers.3) | copy-start | bytes 5898244
  1.5 0.9 %copy-start.2 = (f32[2,3,32,128]{3,2,1,0:T(8,128)S(1)}, f32[2,3,32,128]{3,2,1,0:T(8,128)}, u32[]{:S(2)}) copy-start(f32[2,3,32,128]{3,2,1,0:T(8,128)} %velocity.5) | copy-start | bytes 294916
  2.4 0.8 %copy-start.4 = (s32[3,32,128]{2,1,0:T(8,128)S(1)}, s32[3,32,128]{2,1,0:T(8,128)}, u32[]{:S(2)}) copy-start(s32[3,32,128]{2,1,0:T(8,128)} %mask.7) | copy-start | bytes 147460
  3.2 11.8 %copy-start.1 = (f32[40,3,32,128]{3,2,1,0:T(8,128)S(1)}, f32[40,3,32,128]{3,2,1,0:T(8,128)}, u32[]{:S(2)}) copy-start(f32[40,3,32,128]{3,2,1,0:T(8,128)} %tracers.3) | copy-start | bytes 5898244
  3.2 11.8 %copy-start.3 = (f32[2,3,32,128]{3,2,1,0:T(8,128)S(1)}, f32[2,3,32,128]{3,2,1,0:T(8,128)}, u32[]{:S(2)}) copy-start(f32[2,3,32,128]{3,2,1,0:T(8,128)} %velocity.5) | copy-start | bytes 294916
  3.2 11.8 %copy-start.5 = (s32[3,32,128]{2,1,0:T(8,128)S(1)}, s32[3,32,128]{2,1,0:T(8,128)}, u32[]{:S(2)}) copy-start(s32[3,32,128]{2,1,0:T(8,128)} %mask.7) | copy-start | bytes 147460
  3.5 14.9 %copy-start.13 = (s32[10,26]{1,0:T(8,128)S(1)}, s32[10,26]{1,0:T(8,128)}, u32[]{:S(2)}) copy-start(s32[10,26]{1,0:T(8,128)} %param.20) | copy-start | bytes 3124
  3.5 14.9 %copy-start.6 = (f32[32,128]{1,0:T(8,128)S(1)}, f32[32,128]{1,0:T(8,128)}, u32[]{:S(2)}) copy-start(f32[32,128]{1,0:T(8,128)} %sunlight.1) | copy-start | bytes 49156
  3.5 14.9 %copy-start.7 = (f32[4,26]{1,0:T(4,128)S(1)}, f32[4,26]{1,0:T(4,128)}, u32[]{:S(2)}) copy-start(f32[4,26]{1,0:T(4,128)} %half_sat.1) | copy-start | bytes 1252
  3.5 14.9 %copy-start.8 = (f32[26]{0:T(128)S(1)}, f32[26]{0:T(128)}, u32[]{:S(2)}) copy-start(f32[26]{0:T(128)} %growth_max.1) | copy-start | bytes 316
  3.5 14.9 %copy-start.9 = (f32[26]{0:T(128)S(1)}, f32[26]{0:T(128)}, u32[]{:S(2)}) copy-start(f32[26]{0:T(128)} %light_half.1) | copy-start | bytes 316
  3.5 14.9 %copy-start.10 = (f32[10]{0:T(128)S(1)}, f32[10]{0:T(128)}, u32[]{:S(2)}) copy-start(f32[10]{0:T(128)} %graze_max.1) | copy-start | bytes 124
  3.5 14.9 %copy-start.11 = (f32[10]{0:T(128)S(1)}, f32[10]{0:T(128)}, u32[]{:S(2)}) copy-start(f32[10]{0:T(128)} %graze_half.1) | copy-start | bytes 124
  3.5 14.9 %copy-start.12 = (f32[4]{0:T(128)S(1)}, f32[4]{0:T(128)}, u32[]{:S(2)}) copy-start(f32[4]{0:T(128)} %stoichiometry.1) | copy-start | bytes 52
  3.7 9.7 %collective-permute-start = (f32[268,128]{1,0:T(8,128)S(1)}, f32[268,128]{1,0:T(8,128)S(1)}, u32[]{:S(2)}, u32[]{:S(2)}) collective-permute-start(f32[268,128]{1,0:T(8,128)S(1)} %bitcast.22), channel_id=1, source_target_pairs={{0,4},{4,8},{8,12},{12,0},{1,5},{5,9},{9,13},{13,1},{2,6},{6,10},{... | collective-permute-start | bytes 411656 | tf_op jit(solution)/shard_map/ppermute | solution.py:356
  6.9 8.2 %collective-permute-start.1 = (f32[268,128]{1,0:T(8,128)S(1)}, f32[268,128]{1,0:T(8,128)S(1)}, u32[]{:S(2)}, u32[]{:S(2)}) collective-permute-start(f32[268,128]{1,0:T(8,128)S(1)} %bitcast.23), channel_id=1, source_target_pairs={{4,0},{8,4},{12,8},{0,12},{5,1},{9,5},{13,9},{1,13},{6,2},{10,6},{... | collective-permute-start | bytes 411656 | tf_op jit(solution)/shard_map/ppermute | solution.py:357
  16.5 8.4 %collective-permute-start.2 = (f32[3,32,128]{2,1,0:T(8,128)S(1)}, f32[3,32,128]{2,1,0:T(8,128)S(1)}, u32[]{:S(2)}, u32[]{:S(2)}) collective-permute-start(f32[3,32,128]{2,1,0:T(8,128)S(1)} %get-tuple-element.14.my_right), channel_id=1, source_target_pairs={{0,1},{1,2},{2,3},{3,0},{4,5},{5,6},{6,7},{7,4},{8,9},{9,10},{10,1... | collective-permute-start | bytes 147464 | tf_op jit(solution)/shard_map/ppermute | solution.py:389
  16.6 8.4 %collective-permute-start.3 = (f32[3,32,128]{2,1,0:T(8,128)S(1)}, f32[3,32,128]{2,1,0:T(8,128)S(1)}, u32[]{:S(2)}, u32[]{:S(2)}) collective-permute-start(f32[3,32,128]{2,1,0:T(8,128)S(1)} %get-tuple-element.13.my_left), channel_id=1, source_target_pairs={{1,0},{2,1},{3,2},{0,3},{5,4},{6,5},{7,6},{4,7},{9,8},{10,9},{11,1... | collective-permute-start | bytes 147464 | tf_op jit(solution)/shard_map/ppermute | solution.py:390

commit v2 on v1

--- a/solution.py
+++ b/solution.py
@@ -1,5 +1,3 @@
-import functools
-
 import jax
 import jax.numpy as jnp
 from jax import lax
@@ -7,8 +5,10 @@
 from jax.experimental.pallas import tpu as pltpu
 from jax.sharding import PartitionSpec as P
 
+
 NNUT = 4
 NPHY = 26
+DEPTH = 12
 PAD = 4
 
 plankton_mortality = 0.05
@@ -19,10 +19,15 @@
 VMEM = pl.BlockSpec(memory_space=pltpu.VMEM)
 SMEM = pl.BlockSpec(memory_space=pltpu.SMEM)
 ANY = pl.BlockSpec(memory_space=pl.ANY)
+HBM = pl.BlockSpec(memory_space=pltpu.HBM)
 
 
 def in_vmem(array):
     return pltpu.with_memory_space_constraint(array, pltpu.VMEM)
+
+
+def in_hbm(array):
+    return pltpu.with_memory_space_constraint(array, pltpu.HBM)
 
 
 def call(kernel, outs, specs, scratch=(), flops=0, bytes_accessed=0, limit=8 << 20, **more):
@@ -37,10 +42,27 @@
     )
 
 
+class Deferred:
+    def __init__(self, depth):
+        self.depth, self.queue = depth, []
+
+    def put(self, ref, index, value):
+        self.queue.append((ref, index, value))
+        if len(self.queue) > self.depth:
+            self.pop()
+
+    def pop(self):
+        ref, index, value = self.queue.pop(0)
+        ref[index] = value
+
+    def flush(self):
+        while self.queue:
+            self.pop()
+
+
 def pack_rows(tracers, velocity, mask, first, last, edge, sems):
     count, length = tracers.shape[0], tracers.shape[1]
     levels = mask.shape[0]
-    groups = first.shape[0]
     copies = []
     for side, (out, start) in enumerate(((first, 0), (last, length - 2))):
         rows = pl.ds(start, 2)
@@ -55,7 +77,7 @@
         copy.start()
     for out in (first, last):
         out[0:PAD] = jnp.zeros((PAD,) + out.shape[1:], out.dtype)
-        out[groups - PAD : groups] = jnp.zeros((PAD,) + out.shape[1:], out.dtype)
+        out[PAD + count + 2 * levels :] = jnp.zeros_like(out[PAD + count + 2 * levels :])
     for copy in copies:
         copy.wait()
     for side, out in enumerate((first, last)):
@@ -146,112 +168,167 @@
     return a0, b0 - a1, 1.0 + (upper - lower) + d0 - b1, e0 - d1, -e1
 
 
-def along(tracers, velocity, mask, before, after, swept, pack_left, pack_right, weights):
+def row_weights(velocity, mask, level, wet_before, wet_after, flow_after):
+    length, lanes = mask.shape[1:]
+    rows = lax.broadcasted_iota(jnp.int32, (length, lanes), 0)
+    wet = mask[level].astype(jnp.float32)
+    wet_up = jnp.where(rows == 0, wet_before, pltpu.roll(wet, 1, 0))
+    lower = velocity[0, level] * (wet_up * wet)
+    upper = jnp.where(
+        rows == length - 1, flow_after * (wet * wet_after), pltpu.roll(lower, length - 1, 0)
+    )
+    return stencil(lower, upper)
+
+
+def column_weights(velocity, mask, level, here):
+    lanes = mask.shape[2]
+    lane = lax.broadcasted_iota(jnp.int32, (8, lanes), 1)
+    wet = mask[level, here].astype(jnp.float32)
+    lower = jnp.where(lane == 0, 0.0, velocity[1, level, here] * wet * pltpu.roll(wet, 1, 1))
+    upper = pltpu.roll(lower, lanes - 1, 1)
+    wm2, wm1, w0, wp1, wp2 = stencil(lower, upper)
+    return (
+        jnp.where(lane < 2, 0.0, wm2),
+        jnp.where(lane < 1, 0.0, wm1),
+        w0,
+        jnp.where(lane > lanes - 2, 0.0, wp1),
+        jnp.where(lane > lanes - 3, 0.0, wp2),
+    )
+
+
+def sweep_across(centre, weights):
+    wm2, wm1, w0, wp1, wp2 = weights
+    lanes = centre.shape[1]
+    return (
+        w0 * centre
+        + (wm1 * pltpu.roll(centre, 1, 1) + wm2 * pltpu.roll(centre, 2, 1))
+        + (wp1 * pltpu.roll(centre, lanes - 1, 1) + wp2 * pltpu.roll(centre, lanes - 2, 1))
+    )
+
+
+class Packer:
+    def __init__(self, lanes):
+        self.slot = lax.broadcasted_iota(jnp.int32, (8, lanes), 1) // 2
+        self.left = self.right = jnp.zeros((8, lanes), jnp.float32)
+
+    def add(self, t, value):
+        turned = pltpu.roll(value, 2 * t + 2, 1)
+        self.right = jnp.where(self.slot == t, turned, self.right)
+        self.left = jnp.where(self.slot == t + 1, turned, self.left)
+
+
+def pack_forcing(packer, count, velocity, mask, level, here):
+    packer.add(count, velocity[1, level, here])
+    packer.add(count + 1, mask[level, here].astype(jnp.float32))
+
+
+def interior(tracers, velocity, mask, _, partial, pack_left, pack_right, weights):
     count, levels, length, lanes = tracers.shape
-    blocks = length // 8
-    rows = lax.broadcasted_iota(jnp.int32, (length, lanes), 0)
+    zero = jnp.zeros((1, lanes), jnp.float32)
+
+    def level_step(level, carry):
+        for n, w in enumerate(row_weights(velocity, mask, level, zero, zero, zero)):
+            weights[n] = w
+
+        def block_step(block, carry):
+            begin = pl.multiple_of(8 * block, 8)
+            here = pl.ds(begin, 8)
+            wm2, wm1, w0, wp1, wp2 = [weights[n, here] for n in range(5)]
+            columns = column_weights(velocity, mask, level, here)
+            packer = Packer(lanes)
+            later = Deferred(DEPTH)
+            for t in range(count):
+                at = lambda offset: tracers[t, level, pl.ds(begin + offset, 8)]
+                value = (
+                    w0 * at(0) + (wm1 * at(-1) + wm2 * at(-2)) + (wp1 * at(1) + wp2 * at(2))
+                )
+                packer.add(t, value)
+                later.put(
+                    partial, (t, level, here), partial[t, level, here] + sweep_across(value, columns)
+                )
+            pack_forcing(packer, count, velocity, mask, level, here)
+            later.flush()
+            pack_right[level, here] = packer.right
+            pack_left[level, here] = packer.left
+            return carry
+
+        return lax.fori_loop(1, length // 8 - 1, block_step, carry)
+
+    lax.fori_loop(0, levels, level_step, 0)
+
+
+def border(
+    tracers, velocity, mask, before, after, partial, left_in, right_in, swept, pack_left, pack_right, through
+):
+    count, levels, length, lanes = tracers.shape
     row8 = lax.broadcasted_iota(jnp.int32, (8, lanes), 0)
-    slot = lax.broadcasted_iota(jnp.int32, (8, lanes), 1) // 2
     base = 2 * PAD
 
     def level_step(level, carry):
-        wet = mask[level].astype(jnp.float32)
-        flow = velocity[0, level]
         pick = lambda ref, field, row: ref[pl.ds(base + 2 * ((count + field) * levels + level) + row, 1)]
-        wet_before, wet_after = pick(before, 1, 1), pick(after, 1, 0)
-        flow_after = pick(after, 0, 0)
-        wet_up = jnp.where(rows == 0, wet_before, pltpu.roll(wet, 1, 0))
-        lower = flow * (wet_up * wet)
-        upper = jnp.where(
-            rows == length - 1,
-            flow_after * (wet * wet_after),
-            pltpu.roll(lower, length - 1, 0),
+        weights = row_weights(
+            velocity, mask, level, pick(before, 1, 1), pick(after, 1, 0), pick(after, 0, 0)
         )
-        for n, w in enumerate(stencil(lower, upper)):
-            weights[n] = w
-        for block in range(blocks):
-            here = pl.ds(8 * block, 8)
-            wm2, wm1, w0, wp1, wp2 = [weights[n, here] for n in range(5)]
-            top, bottom = block == 0, block == blocks - 1
-            if top:
-                zm2, zm1 = jnp.where(row8 < 2, wm2, 0.0), jnp.where(row8 < 1, wm1, 0.0)
+        for side, first in enumerate((0, length - 8)):
+            here = pl.ds(first, 8)
+            wm2, wm1, w0, wp1, wp2 = [w[first : first + 8] for w in weights]
+            if side == 0:
+                z2, z1 = jnp.where(row8 < 2, wm2, 0.0), jnp.where(row8 < 1, wm1, 0.0)
                 wm2, wm1 = jnp.where(row8 < 2, 0.0, wm2), jnp.where(row8 < 1, 0.0, wm1)
-            if bottom:
-                zp2, zp1 = jnp.where(row8 > 5, wp2, 0.0), jnp.where(row8 > 6, wp1, 0.0)
+            else:
+                z2, z1 = jnp.where(row8 > 5, wp2, 0.0), jnp.where(row8 > 6, wp1, 0.0)
                 wp2, wp1 = jnp.where(row8 > 5, 0.0, wp2), jnp.where(row8 > 6, 0.0, wp1)
-            right = jnp.zeros((8, lanes), jnp.float32)
-            left = right
+            packer = Packer(lanes)
+            later = Deferred(DEPTH)
             for t in range(count):
                 centre = tracers[t, level, here]
 
-                def shifted(offset):
-                    if (top and offset < 0) or (bottom and offset > 0):
+                def at(offset):
+                    if (offset < 0) == (side == 0):
                         return pltpu.roll(centre, -offset % 8, 0)
-                    return tracers[t, level, pl.ds(8 * block + offset, 8)]
-
+                    return tracers[t, level, pl.ds(first + offset, 8)]
+
+                group = base + 2 * (t * levels + level)
+                if side == 0:
+                    beyond = z2 * before[pl.ds(group, 8)] + z1 * before[pl.ds(group + 1, 8)]
+                else:
+                    beyond = z2 * after[pl.ds(group - 6, 8)] + z1 * after[pl.ds(group - 7, 8)]
                 value = (
-                    w0 * centre
-                    + (wm1 * shifted(-1) + wm2 * shifted(-2))
-                    + (wp1 * shifted(1) + wp2 * shifted(2))
+                    (w0 * centre + beyond) + (wm1 * at(-1) + wm2 * at(-2)) + (wp1 * at(1) + wp2 * at(2))
                 )
-                group = base + 2 * (t * levels + level)
-                if top:
-                    value = value + (
-                        zm2 * before[pl.ds(group, 8)] + zm1 * before[pl.ds(group + 1, 8)]
-                    )
-                if bottom:
-                    value = value + (
-                        zp2 * after[pl.ds(group - 6, 8)] + zp1 * after[pl.ds(group - 7, 8)]
-                    )
-                swept[t, level, here] = value
-                turned = pltpu.roll(value, 2 * t + 2, 1)
-                right = jnp.where(slot == t, turned, right)
-                left = jnp.where(slot == t + 1, turned, left)
-            across_flow = velocity[1, level, here]
-            wet_here = mask[level, here].astype(jnp.float32)
-            for t, value in ((count, across_flow), (count + 1, wet_here)):
-                turned = pltpu.roll(value, 2 * t + 2, 1)
-                right = jnp.where(slot == t, turned, right)
-                left = jnp.where(slot == t + 1, turned, left)
-            pack_right[level, here] = right
-            pack_left[level, here] = left
+                later.put(swept, (t, level, pl.ds(8 * side, 8)), value)
+                packer.add(t, value)
+            pack_forcing(packer, count, velocity, mask, level, here)
+            later.flush()
+            pack_right[level, here] = packer.right
+            pack_left[level, here] = packer.left
         return carry
 
     lax.fori_loop(0, levels, level_step, 0)
 
 
-def across(swept, velocity, mask, tendency, partial):
-    count, levels, length, lanes = swept.shape
-    blocks = length // 8
-    lane = lax.broadcasted_iota(jnp.int32, (8, lanes), 1)
-
-    def level_step(level, carry):
-        for block in range(blocks):
-            here = pl.ds(8 * block, 8)
-            wet = mask[level, here].astype(jnp.float32)
-            lower = jnp.where(lane == 0, 0.0, velocity[1, level, here] * wet * pltpu.roll(wet, 1, 1))
-            upper = pltpu.roll(lower, lanes - 1, 1)
-            wm2, wm1, w0, wp1, wp2 = stencil(lower, upper)
-            wm2 = jnp.where(lane < 2, 0.0, wm2)
-            wm1 = jnp.where(lane < 1, 0.0, wm1)
-            wp1 = jnp.where(lane > lanes - 2, 0.0, wp1)
-            wp2 = jnp.where(lane > lanes - 3, 0.0, wp2)
-            for t in range(count):
-                centre = swept[t, level, here]
-                partial[t, level, here] = (
-                    (tendency[t, level, here] + w0 * centre)
-                    + (wm1 * pltpu.roll(centre, 1, 1) + wm2 * pltpu.roll(centre, 2, 1))
-                    + (wp1 * pltpu.roll(centre, lanes - 1, 1) + wp2 * pltpu.roll(centre, lanes - 2, 1))
-                )
+def border_across(swept, velocity, mask, _, partial):
+    count, levels = swept.shape[:2]
+    length = mask.shape[1]
+
+    def step(index, carry):
+        level, side = index // 2, index % 2
+        here = pl.ds(pl.multiple_of(side * (length - 8), 8), 8)
+        columns = column_weights(velocity, mask, level, here)
+        later = Deferred(DEPTH)
+        for t in range(count):
+            value = swept[t, level, pl.ds(pl.multiple_of(8 * side, 8), 8)]
+            later.put(partial, (t, level, here), partial[t, level, here] + sweep_across(value, columns))
+        later.flush()
         return carry
 
-    lax.fori_loop(0, levels, level_step, 0)
+    lax.fori_loop(0, 2 * levels, step, 0)
 
 
 def finish(
-    partial, velocity, mask, my_left, my_right, from_left, from_right, edges, updated, even, odd, done, sems
+    partial, velocity, mask, my_left, my_right, from_left, from_right, edges, done, updated, even, odd, sems
 ):
-    count, levels, length, lanes = partial.shape
+    count, levels, length, lanes = done.shape
     blocks = length // 8
     lane = lax.broadcasted_iota(jnp.int32, (8, lanes), 1)
     is_odd = lane % 2 == 1
@@ -297,25 +374,23 @@
 
     lax.fori_loop(0, levels, level_step, 0)
     outer = (lane < 2) | (lane > lanes - 3)
-    step = max(n for n in (10, 8, 5, 4, 2, 1) if count % n == 0)
-    copies = []
-    for first in range(0, count, step):
-
-        def level_add(level, carry):
+    step = max(n for n in (4, 2, 1) if count % n == 0)
+
+    def copy(chunk):
+        part = pl.ds(chunk * step, step)
+        return pltpu.make_async_copy(done.at[part], updated.at[part], sems.at[chunk])
+
+    for chunk in range(count // step):
+        for level in range(levels):
             for block in range(blocks):
                 here = pl.ds(8 * block, 8)
                 packs = (even[level, here], odd[level, here])
-                for t in range(first, first + step):
-                    edge = pltpu.roll(packs[t % 2], -2 * t % lanes, 1)
-                    done[t, level, here] = partial[t, level, here] + jnp.where(outer, edge, 0.0)
-            return carry
-
-        lax.fori_loop(0, levels, level_add, 0)
-        part = pl.ds(first, step)
-        copies.append(pltpu.make_async_copy(done.at[part], updated.at[part], sems.at[first // step]))
-        copies[-1].start()
-    for copy in copies:
-        copy.wait()
+                for t in range(chunk * step, chunk * step + step):
+                    edge = pltpu.roll(packs[t % 2], (lanes - 2 * t) % lanes, 1)
+                    done[t, level, here] = done[t, level, here] + jnp.where(outer, edge, 0.0)
+        copy(chunk).start()
+    for chunk in range(count // step):
+        copy(chunk).wait()
 
 
 def shards(
@@ -338,28 +413,31 @@
     down = lambda n: [((i + 1) % n, i) for i in range(n)]
     cells = count * levels * length * lanes
 
-    groups = 2 * PAD + (count + 2) * levels
+    assert length % 8 == 0 and length >= 16 and 2 * count + 6 <= lanes
+    groups = -(-(2 * PAD + (count + 2) * levels) // 4) * 4
     row_message = pltpu.VMEM((groups, 2, 1, lanes), f32)
     first, last = call(
         pack_rows,
         (row_message, row_message),
-        [ANY, ANY, ANY],
+        [HBM, HBM, HBM],
         scratch=[pltpu.VMEM((2, levels, 2, 1, lanes), jnp.int32), pltpu.SemaphoreType.DMA((2, 3))],
         bytes_accessed=8 * groups * lanes,
         limit=2 << 20,
     )(
-        tracers.reshape(count * levels, length, 1, lanes),
-        velocity.reshape(2, levels, length, 1, lanes),
-        land_mask.reshape(levels, length, 1, lanes),
+        in_hbm(tracers.reshape(count * levels, length, 1, lanes)),
+        in_hbm(velocity.reshape(2, levels, length, 1, lanes)),
+        in_hbm(land_mask.reshape(levels, length, 1, lanes)),
     )
     first, last = first.reshape(2 * groups, lanes), last.reshape(2 * groups, lanes)
     before = lax.ppermute(last, "tx", up(tx))
     after = lax.ppermute(first, "tx", down(tx))
 
     held, flow, mask = in_vmem(tracers), in_vmem(velocity), in_vmem(land_mask)
+    field = pltpu.VMEM(tracers.shape, f32)
+    columns = pltpu.VMEM((levels, length, lanes), f32)
     tendency = call(
         ecology,
-        pltpu.VMEM(tracers.shape, f32),
+        field,
         [VMEM, VMEM, VMEM] + [SMEM] * 7,
         flops=40 * cells,
         bytes_accessed=8 * cells,
@@ -376,43 +454,54 @@
         palatable.astype(f32),
         stoichiometry,
     )
-    column_message = pltpu.VMEM((levels, length, lanes), f32)
-    swept, pack_left, pack_right = call(
-        along,
-        (pltpu.VMEM(tracers.shape, f32), column_message, column_message),
-        [VMEM] * 5,
+    partial, pack_left, pack_right = call(
+        interior,
+        (field, columns, columns),
+        [VMEM] * 4,
         scratch=[pltpu.VMEM((5, length, lanes), f32)],
         flops=20 * cells,
         bytes_accessed=8 * cells,
         limit=2 << 20,
-    )(held, flow, mask, in_vmem(before), in_vmem(after))
+        input_output_aliases={3: 0},
+    )(held, flow, mask, tendency)
+    swept, pack_left, pack_right, partial = call(
+        border,
+        (pltpu.VMEM((count, levels, 16, lanes), f32), columns, columns, field),
+        [VMEM] * 5 + [ANY] * 3,
+        out_specs=[VMEM] * 3 + [ANY],
+        flops=10 * cells,
+        bytes_accessed=8 * cells,
+        limit=2 << 20,
+        input_output_aliases={5: 3, 6: 1, 7: 2},
+    )(held, flow, mask, in_vmem(before), in_vmem(after), partial, pack_left, pack_right)
     from_left = lax.ppermute(pack_right, "ty", up(ty))
     from_right = lax.ppermute(pack_left, "ty", down(ty))
     partial = call(
-        across,
-        pltpu.VMEM(tracers.shape, f32),
+        border_across,
+        field,
         [VMEM] * 4,
-        flops=20 * cells,
-        bytes_accessed=12 * cells,
+        flops=10 * cells,
+        bytes_accessed=6 * cells,
         limit=2 << 20,
-    )(swept, flow, mask, tendency)
+        input_output_aliases={3: 0},
+    )(swept, flow, mask, partial)
     place = lax.axis_index("ty")
     edges = jnp.stack([place > 0, place < ty - 1]).astype(f32)
     return call(
         finish,
-        jax.ShapeDtypeStruct(tracers.shape, f32),
+        (field, jax.ShapeDtypeStruct(tracers.shape, f32)),
         [VMEM] * 7 + [SMEM],
-        out_specs=ANY,
+        out_specs=[VMEM, HBM],
+        input_output_aliases={0: 0},
         scratch=[
             pltpu.VMEM((levels, length, lanes), f32),
             pltpu.VMEM((levels, length, lanes), f32),
-            pltpu.VMEM(tracers.shape, f32),
             pltpu.SemaphoreType.DMA((count,)),
         ],
         flops=4 * cells,
         bytes_accessed=8 * cells,
         limit=4 << 20,
-    )(partial, flow, mask, pack_left, pack_right, in_vmem(from_left), in_vmem(from_right), edges)
+    )(partial, flow, mask, pack_left, pack_right, in_vmem(from_left), in_vmem(from_right), edges)[1]
 
 
 def solution(mesh):

time: 28.9 us -> 21.4 us (0.74)
  local copies, waits for them, and re-layouts: 3.51 us -> 0.05 us
  waiting for transfers between devices: 6.08 us -> 2.88 us
  starting transfers between devices: 6.99 us -> 5.7 us
  Pallas kernels: 11.9 us -> 12.4 us
    unnamed x32 -> x22, local copies, waits for them, and re-layouts: 3.51 us -> 0.05 us
    ppermute x1, waiting for transfers between devices: 4.35 us -> 0.89 us  [shards(): before = lax.ppermute(last, 'tx', up(tx))]
    ppermute x1, starting transfers between devices: 3.1 us -> 0.01 us  [shards(): before = lax.ppermute(last, 'tx', up(tx))]
    ppermute x1, starting transfers between devices: 2.1 us -> 5.14 us  [shards(): after = lax.ppermute(first, 'tx', down(tx))]
    ppermute x1, waiting for transfers between devices: 0.01 us -> 1.99 us  [shards(): from_left = lax.ppermute(pack_right, 'ty', up(ty))]
    ppermute x1, waiting for transfers between devices: 1.72 us -> 0.01 us  [shards(): after = lax.ppermute(first, 'tx', down(tx))]
    ppermute x1, starting transfers between devices: 1.73 us -> 0.06 us  [shards(): from_right = lax.ppermute(pack_left, 'ty', down(ty))]
    pallas_call x5 -> x6, Pallas kernels: 11.9 us -> 12.4 us  [the longest x1 4.02 us: shards(): call(ecology, field, [VMEM, VMEM, VMEM] + [SMEM] * 7, flops=40 * cells, b...]
  transfers between devices with their start and end apart: 4 -> 4, of which waited for: 2 -> 2; matrix products, arithmetic and copies ran while one was open for 1% -> 0% of each run, Pallas kernels for 23% -> 35%
where the time goes in v2:
time: 21.4 us; the launch traced here: 21.3 us
  Pallas kernels  12.4 us (58%)
  starting transfers between devices  5.7 us (27%)
  waiting for transfers between devices  2.88 us (13%)
    ppermute x1, starting transfers between devices, shards(): after = lax.ppermute(first, 'tx', down(tx))  5.14 us
    pallas_call x1, Pallas kernels, shards(): call(ecology, field, [VMEM, VMEM, VMEM] + [SMEM] * 7, flops=40 * cells, b...  4.02 us
    pallas_call x1, Pallas kernels, shards(): call(finish, (field, jax.ShapeDtypeStruct(tracers.shape, f32)), [VMEM] *...  2.98 us
    ppermute x1, waiting for transfers between devices, shards(): from_left = lax.ppermute(pack_right, 'ty', up(ty))  1.99 us
    pallas_call x1, Pallas kernels, shards(): call(interior, (field, columns, columns), [VMEM] * 4, scratch=[pltpu.VMEM...  1.88 us
    pallas_call x1, Pallas kernels, shards(): call(border_across, field, [VMEM] * 4, flops=10 * cells, bytes_accessed=6...  1.49 us
    pallas_call x1, Pallas kernels, shards(): call(pack_rows, (row_message, row_message), [HBM, HBM, HBM], scratch=[plt...  1.17 us
    ppermute x1, waiting for transfers between devices, shards(): before = lax.ppermute(last, 'tx', up(tx))  0.89 us
  transfers between devices with their start and end apart: 4, of which 2 were waited for; matrix products, arithmetic and copies ran while one was open for 0% of the time, Pallas kernels for 35%

profile of v2, /device:TPU:0, one launch (start us, length us, event | category | flops | bytes accessed | tf_op | source)
XLA Modules:
  0.0 21.3 jit_solution(1763660426158717449)
XLA Ops:
  0.0 0.0 copy-start.7
  0.0 0.0 copy-start.6
  0.0 0.0 copy-start.4
  0.0 0.0 copy-start.5
  0.1 0.0 copy-start.3
  0.1 1.2 %shard_map.109 = (f32[136,2,1,128]{3,2,1,0:T(1,128)S(1)}, f32[136,2,1,128]{3,2,1,0:T(1,128)S(1)}) custom-call(f32[120,32,1,128]{3,2,1,0:T(1,128)} %bitcast.7, f32[2,3,32,1,128]{4,3,2,1,0:T(1,128)} %bitcast.8, s32[3,32,1,128]{3,2,1,0:T(1,128)} %bitcast.9), custom_call_target="tpu_custom_call" | custom-call | bytes 139264 | tf_op jit(solution)/shard_map/pallas_call | solution.py:419
  1.2 5.1 %collective-permute-start.1 = (f32[272,128]{1,0:T(8,128)S(1)}, f32[272,128]{1,0:T(8,128)S(1)}, u32[]{:S(2)}, u32[]{:S(2)}) collective-permute-start(f32[272,128]{1,0:T(8,128)S(1)} %bitcast.11), channel_id=1, source_target_pairs={{4,0},{8,4},{12,8},{0,12},{5,1},{9,5},{13,9},{1,13},{6,2},{10,6},{... | collective-permute-start | bytes 417800 | tf_op jit(solution)/shard_map/ppermute | solution.py:433
  6.4 0.0 collective-permute-start
  6.4 0.0 copy-done.10
  6.4 0.0 copy-done
  6.4 0.0 copy-done.2
  6.4 0.0 copy-done.9
  6.4 0.0 copy-done.8
  6.4 0.0 copy-done.7
  6.4 0.0 copy-done.6
  6.5 0.0 copy-done.4
  6.5 0.0 copy-done.5
  6.5 0.0 copy-done.3
  6.5 0.0 copy-start.1
  6.5 4.0 %shard_map.110._ = f32[40,3,32,128]{3,2,1,0:T(8,128)S(1)} custom-call(f32[40,3,32,128]{3,2,1,0:T(8,128)S(1)} %copy-done, s32[3,32,128]{2,1,0:T(8,128)S(1)} %copy-done.2, f32[32,128]{1,0:T(8,128)S(1)} %copy-done.3, f32[26]{0:T(128)S(1)} %copy-done.5, f32[4,26]{1,0:T(4,128)S(1)} %copy-done.4, f32[26]{0:T(128)S(1)} %copy-done.6, f32[10]{0:T(128)S(1)} %copy-done.7, ...), custom_call_target="tpu_custom_call" | custom-call | flops 19660800 | bytes 3932160 | tf_op jit(solution)/shard_map/pallas_call | solution.py:438
  10.5 0.0 copy-done.1
  10.5 1.9 %shard_map.111 = (f32[40,3,32,128]{3,2,1,0:T(8,128)S(1)}, f32[3,32,128]{2,1,0:T(8,128)S(1)}, f32[3,32,128]{2,1,0:T(8,128)S(1)}) custom-call(f32[40,3,32,128]{3,2,1,0:T(8,128)S(1)} %copy-done, f32[2,3,32,128]{3,2,1,0:T(8,128)S(1)} %copy-done.1, s32[3,32,128]{2,1,0:T(8,128)S(1)} %copy-done.2, ...), custom_call_target="tpu_custom_call", output_to_operand_aliasing={{0}: (3, {})} | custom-call | flops 9830400 | bytes 3932160 | tf_op jit(solution)/shard_map/pallas_call | solution.py:457
  12.4 0.0 collective-permute-done.1.after
  12.4 0.9 %collective-permute-done.before = f32[272,128]{1,0:T(8,128)S(1)} collective-permute-done((f32[272,128]{1,0:T(8,128)S(1)}, f32[272,128]{1,0:T(8,128)S(1)}, u32[]{:S(2)}, u32[]{:S(2)}) %collective-permute-start) | collective-permute-done | bytes 139296 | tf_op jit(solution)/shard_map/ppermute | solution.py:432
  13.3 0.8 %shard_map.112 = (f32[40,3,16,128]{3,2,1,0:T(8,128)S(1)}, f32[3,32,128]{2,1,0:T(8,128)S(1)}, f32[3,32,128]{2,1,0:T(8,128)S(1)}, f32[40,3,32,128]{3,2,1,0:T(8,128)S(1)}) custom-call(f32[40,3,32,128]{3,2,1,0:T(8,128)S(1)} %copy-done, f32[2,3,32,128]{3,2,1,0:T(8,128)S(1)} %copy-done.1, ...), custom_call_target="tpu_custom_call", output_to_operand_aliasing={{3}: (5, {}), {1}: (6, {}), {2}: (7, {})} | custom-call | flops 4915200 | bytes 3932160 | tf_op jit(solution)/shard_map/pallas_call | solution.py:467
  14.1 0.1 collective-permute-start.3
  14.2 0.5 %collective-permute-start.2 = (f32[3,32,128]{2,1,0:T(8,128)S(1)}, f32[3,32,128]{2,1,0:T(8,128)S(1)}, u32[]{:S(2)}, u32[]{:S(2)}) collective-permute-start(f32[3,32,128]{2,1,0:T(8,128)S(1)} %get-tuple-element.23.my_right), channel_id=1, source_target_pairs={{0,1},{1,2},{2,3},{3,0},{4,5},{5,6},{6,7},{7,4},{8,9},{9,10},{10,1... | collective-permute-start | bytes 147464 | tf_op jit(solution)/shard_map/ppermute | solution.py:477
  14.7 0.1 add_convert_fusion.edges
  14.8 1.5 %shard_map.113.partial = f32[40,3,32,128]{3,2,1,0:T(8,128)S(1)} custom-call(f32[40,3,16,128]{3,2,1,0:T(8,128)S(1)} %get-tuple-element.20.swept, f32[2,3,32,128]{3,2,1,0:T(8,128)S(1)} %copy-done.1, s32[3,32,128]{2,1,0:T(8,128)S(1)} %copy-done.2, f32[40,3,32,128]{3,2,1,0:T(8,128)S(1)} %get-tuple-element.21._), custom_call_target="tpu_custom_call", output_to_operand_aliasing={{}: (3, {})} | custom-call | flops 4915200 | bytes 2949120 | tf_op jit(solution)/shard_map/pallas_call | solution.py:479
  16.3 0.0 collective-permute-done.3.from_right
  16.3 2.0 %collective-permute-done.2.from_left = f32[3,32,128]{2,1,0:T(8,128)S(1)} collective-permute-done((f32[3,32,128]{2,1,0:T(8,128)S(1)}, f32[3,32,128]{2,1,0:T(8,128)S(1)}, u32[]{:S(2)}, u32[]{:S(2)}) %collective-permute-start.2) | collective-permute-done | bytes 49184 | tf_op jit(solution)/shard_map/ppermute | solution.py:477
  18.3 3.0 %shard_map.114 = (f32[40,3,32,128]{3,2,1,0:T(8,128)S(1)}, f32[40,3,32,128]{3,2,1,0:T(8,128)}) custom-call(f32[40,3,32,128]{3,2,1,0:T(8,128)S(1)} %shard_map.113.partial, f32[2,3,32,128]{3,2,1,0:T(8,128)S(1)} %copy-done.1, s32[3,32,128]{2,1,0:T(8,128)S(1)} %copy-done.2, f32[3,32,128]{2,1,0:T(8,128)S(1)} %get-tuple-element.22.my_left, ...), custom_call_target="tpu_custom_call", output_to_operand_aliasing={{0}: (0, {})} | custom-call | flops 1966080 | bytes 3932160 | tf_op jit(solution)/shard_map/pallas_call | solution.py:490
  (6 shorter events, 0.0 us)
Async XLA Ops:
  0.0 6.4 %copy-start = (f32[40,3,32,128]{3,2,1,0:T(8,128)S(1)}, f32[40,3,32,128]{3,2,1,0:T(8,128)}, u32[]{:S(2)}) copy-start(f32[40,3,32,128]{3,2,1,0:T(8,128)} %tracers.5) | copy-start | bytes 5898244
  0.0 6.4 %copy-start.2 = (s32[3,32,128]{2,1,0:T(8,128)S(1)}, s32[3,32,128]{2,1,0:T(8,128)}, u32[]{:S(2)}) copy-start(s32[3,32,128]{2,1,0:T(8,128)} %mask.9) | copy-start | bytes 147460
  0.0 6.4 %copy-start.10 = (s32[10,26]{1,0:T(8,128)S(1)}, s32[10,26]{1,0:T(8,128)}, u32[]{:S(2)}) copy-start(s32[10,26]{1,0:T(8,128)} %param.20) | copy-start | bytes 3124
  0.0 6.4 %copy-start.9 = (f32[4]{0:T(128)S(1)}, f32[4]{0:T(128)}, u32[]{:S(2)}) copy-start(f32[4]{0:T(128)} %stoichiometry.1) | copy-start | bytes 52
  0.0 6.4 %copy-start.8 = (f32[10]{0:T(128)S(1)}, f32[10]{0:T(128)}, u32[]{:S(2)}) copy-start(f32[10]{0:T(128)} %graze_half.1) | copy-start | bytes 124
  0.0 6.4 %copy-start.7 = (f32[10]{0:T(128)S(1)}, f32[10]{0:T(128)}, u32[]{:S(2)}) copy-start(f32[10]{0:T(128)} %graze_max.1) | copy-start | bytes 124
  0.0 6.4 %copy-start.6 = (f32[26]{0:T(128)S(1)}, f32[26]{0:T(128)}, u32[]{:S(2)}) copy-start(f32[26]{0:T(128)} %light_half.1) | copy-start | bytes 316
  0.0 6.4 %copy-start.4 = (f32[4,26]{1,0:T(4,128)S(1)}, f32[4,26]{1,0:T(4,128)}, u32[]{:S(2)}) copy-start(f32[4,26]{1,0:T(4,128)} %half_sat.1) | copy-start | bytes 1252
  0.0 6.4 %copy-start.5 = (f32[26]{0:T(128)S(1)}, f32[26]{0:T(128)}, u32[]{:S(2)}) copy-start(f32[26]{0:T(128)} %growth_max.1) | copy-start | bytes 316
  0.1 6.4 %copy-start.3 = (f32[32,128]{1,0:T(8,128)S(1)}, f32[32,128]{1,0:T(8,128)}, u32[]{:S(2)}) copy-start(f32[32,128]{1,0:T(8,128)} %sunlight.1) | copy-start | bytes 49156
  1.2 11.2 %collective-permute-start.1 = (f32[272,128]{1,0:T(8,128)S(1)}, f32[272,128]{1,0:T(8,128)S(1)}, u32[]{:S(2)}, u32[]{:S(2)}) collective-permute-start(f32[272,128]{1,0:T(8,128)S(1)} %bitcast.11), channel_id=1, source_target_pairs={{4,0},{8,4},{12,8},{0,12},{5,1},{9,5},{13,9},{1,13},{6,2},{10,6},{... | collective-permute-start | bytes 417800 | tf_op jit(solution)/shard_map/ppermute | solution.py:433
  6.4 6.9 %collective-permute-start = (f32[272,128]{1,0:T(8,128)S(1)}, f32[272,128]{1,0:T(8,128)S(1)}, u32[]{:S(2)}, u32[]{:S(2)}) collective-permute-start(f32[272,128]{1,0:T(8,128)S(1)} %bitcast.10), channel_id=1, source_target_pairs={{0,4},{4,8},{8,12},{12,0},{1,5},{5,9},{9,13},{13,1},{2,6},{6,10},{... | collective-permute-start | bytes 417800 | tf_op jit(solution)/shard_map/ppermute | solution.py:432
  6.5 4.0 %copy-start.1 = (f32[2,3,32,128]{3,2,1,0:T(8,128)S(1)}, f32[2,3,32,128]{3,2,1,0:T(8,128)}, u32[]{:S(2)}) copy-start(f32[2,3,32,128]{3,2,1,0:T(8,128)} %velocity.7) | copy-start | bytes 294916
  14.1 2.1 %collective-permute-start.3 = (f32[3,32,128]{2,1,0:T(8,128)S(1)}, f32[3,32,128]{2,1,0:T(8,128)S(1)}, u32[]{:S(2)}, u32[]{:S(2)}) collective-permute-start(f32[3,32,128]{2,1,0:T(8,128)S(1)} %get-tuple-element.22.my_left), channel_id=1, source_target_pairs={{1,0},{2,1},{3,2},{0,3},{5,4},{6,5},{7,6},{4,7},{9,8},{10,9},{11,1... | collective-permute-start | bytes 147464 | tf_op jit(solution)/shard_map/ppermute | solution.py:478
  14.2 4.1 %collective-permute-start.2 = (f32[3,32,128]{2,1,0:T(8,128)S(1)}, f32[3,32,128]{2,1,0:T(8,128)S(1)}, u32[]{:S(2)}, u32[]{:S(2)}) collective-permute-start(f32[3,32,128]{2,1,0:T(8,128)S(1)} %get-tuple-element.23.my_right), channel_id=1, source_target_pairs={{0,1},{1,2},{2,3},{3,0},{4,5},{5,6},{6,7},{7,4},{8,9},{9,10},{10,1... | collective-permute-start | bytes 147464 | tf_op jit(solution)/shard_map/ppermute | solution.py:477

commit v3 on v2

--- a/solution.py
+++ b/solution.py
@@ -58,6 +58,33 @@
     def flush(self):
         while self.queue:
             self.pop()
+
+
+def diet_matrices(palatable, to_grazers, to_plants):
+    f32, bf16 = jnp.float32, jnp.bfloat16
+    grazers = palatable.shape[0]
+
+    def picks(shape, dim, period):
+        index = lax.broadcasted_iota(jnp.int32, shape, dim)
+        other = lax.broadcasted_iota(jnp.int32, shape, 1 - dim)
+        return ((index % period) // 8 == other).astype(f32).astype(bf16)
+
+    def spread(left, middle, right, transposed):
+        dims = (((1,), (1 if transposed else 0,)), ((), ()))
+        part = lax.dot_general(left, middle, dims, preferred_element_type=f32).astype(bf16)
+        whole = jnp.dot(part, right, preferred_element_type=f32)
+        row = lax.broadcasted_iota(jnp.int32, whole.shape, 0) % 8
+        col = lax.broadcasted_iota(jnp.int32, whole.shape, 1) % 8
+        return jnp.where(row == col, whole, 0.0).astype(bf16)
+
+    eats = palatable[...].astype(f32).astype(bf16)
+    rows_z, rows_k = 8 * grazers, 8 * NPHY
+    to_grazers[...] = spread(
+        picks((rows_z, grazers), 0, rows_z), eats, picks((NPHY, 2 * rows_k), 1, rows_k), False
+    )
+    to_plants[...] = spread(
+        picks((rows_k, NPHY), 0, rows_k), eats, picks((grazers, 2 * rows_z), 1, rows_z), True
+    )
 
 
 def pack_rows(tracers, velocity, mask, first, last, edge, sems):
@@ -88,31 +115,67 @@
     tracers,
     mask,
     sunlight,
+    palatable,
     growth_max,
     half_sat,
     light_half,
     graze_max,
     graze_half,
-    palatable,
     stoichiometry,
     tendency,
+    to_grazers,
+    to_plants,
 ):
-    count, levels, length, _ = tracers.shape
+    count, levels, length, lanes = tracers.shape
     grazers = count - NNUT - NPHY
-    chunk = 16 if length % 16 == 0 else 8
+    f32, bf16 = jnp.float32, jnp.bfloat16
+    plants = pl.ds(NNUT, NPHY)
+
+    diet_matrices(palatable, to_grazers, to_plants)
+
+    def split(values):
+        wide = jnp.concatenate([v.reshape(-1, lanes) for v in values], axis=1)
+        high = wide.astype(bf16)
+        return jnp.concatenate([high, (wide - high.astype(f32)).astype(bf16)], axis=0)
+
+    def entry(wide, n):
+        part = wide[8 * n : 8 * n + 8]
+        return jnp.concatenate([part[:, :lanes], part[:, lanes:]], axis=0)
 
     def level_step(level, carry):
-        depth = jnp.exp(
-            jnp.full((8, 128), -attenuation, jnp.float32) * (level.astype(jnp.float32) + 0.5)
-        )[0:1, 0:1]
-        for start in range(0, length, chunk):
-            rows = pl.ds(start, chunk)
-            wet = mask[level, rows].astype(jnp.float32)
+        depth = jnp.exp(jnp.full((8, 128), -attenuation, f32) * (level.astype(f32) + 0.5))[0:1, 0:1]
+        for start in range(0, length, 16):
+            rows = pl.ds(start, 16)
+            halves = (pl.ds(start, 8), pl.ds(start + 8, 8))
+            available = jnp.dot(
+                to_grazers[...],
+                split([tracers[plants, level, half] for half in halves]),
+                preferred_element_type=f32,
+            )
+            wet = mask[level, rows].astype(f32)
+            recycled = jnp.zeros((16, lanes), f32)
+            rates = []
+            later = Deferred(DEPTH)
+            for z in range(grazers):
+                grazer = tracers[NNUT + NPHY + z, level, rows]
+                prey = entry(available, z)
+                rate = graze_max[z] * grazer / (graze_half[z] + prey)
+                ingested = rate * prey
+                loss = grazer_mortality * grazer * grazer
+                later.put(
+                    tendency,
+                    (NNUT + NPHY + z, level, rows),
+                    wet * (assimilation * ingested - loss),
+                )
+                recycled = recycled + (loss + (1.0 - assimilation) * ingested)
+                rates.append(rate)
+            pressure = jnp.dot(
+                to_plants[...],
+                split([jnp.concatenate([r[n : n + 8] for r in rates], axis=0) for n in (0, 8)]),
+                preferred_element_type=f32,
+            )
             darkness = 1.0 / (sunlight[rows] * depth)
             scarcity = [1.0 / tracers[j, level, rows] for j in range(NNUT)]
-            available = [None] * grazers
-            eaten = None
-            total_growth = None
             for k in range(NPHY):
                 plant = tracers[NNUT + k, level, rows]
                 worst = half_sat[0, k] * scarcity[0]
@@ -121,32 +184,15 @@
                 growth = (growth_max[k] * plant) / (
                     (1.0 + worst) * (1.0 + light_half[k] * darkness)
                 )
-                tendency[NNUT + k, level, rows] = growth - plankton_mortality * plant
-                total_growth = growth if total_growth is None else total_growth + growth
-                eaten = plant if eaten is None else eaten + plant
-                for z in range(grazers):
-                    term = palatable[z, k] * plant
-                    available[z] = term if available[z] is None else available[z] + term
-            recycled = plankton_mortality * eaten - total_growth
-            rates = []
-            for z in range(grazers):
-                grazer = tracers[NNUT + NPHY + z, level, rows]
-                rate = graze_max[z] * grazer / (graze_half[z] + available[z])
-                ingested = rate * available[z]
-                loss = grazer_mortality * grazer * grazer
-                tendency[NNUT + NPHY + z, level, rows] = wet * (assimilation * ingested - loss)
-                recycled = recycled + (loss + (1.0 - assimilation) * ingested)
-                rates.append(rate)
+                recycled = recycled + (plankton_mortality * plant - growth)
+                later.put(
+                    tendency,
+                    (NNUT + k, level, rows),
+                    wet * (growth - plant * (entry(pressure, k) + plankton_mortality)),
+                )
             for j in range(NNUT):
-                tendency[j, level, rows] = wet * (stoichiometry[j] * recycled)
-            for k in range(NPHY):
-                pressure = palatable[0, k] * rates[0]
-                for z in range(1, grazers):
-                    pressure = pressure + palatable[z, k] * rates[z]
-                plant = tracers[NNUT + k, level, rows]
-                tendency[NNUT + k, level, rows] = wet * (
-                    tendency[NNUT + k, level, rows] - plant * pressure
-                )
+                later.put(tendency, (j, level, rows), wet * (stoichiometry[j] * recycled))
+            later.flush()
         return carry
 
     lax.fori_loop(0, levels, level_step, 0)
@@ -207,19 +253,17 @@
 
 
 class Packer:
-    def __init__(self, lanes):
-        self.slot = lax.broadcasted_iota(jnp.int32, (8, lanes), 1) // 2
-        self.left = self.right = jnp.zeros((8, lanes), jnp.float32)
+    def __init__(self, count, velocity, mask, level, here):
+        wet = mask[level, here].astype(jnp.float32)
+        lane = lax.broadcasted_iota(jnp.int32, wet.shape, 1)
+        self.slot = lane // 2
+        self.left = self.right = jnp.zeros_like(wet)
+        self.add(count, jnp.where(lane < 2, velocity[1, level, here] * wet, wet))
 
     def add(self, t, value):
         turned = pltpu.roll(value, 2 * t + 2, 1)
         self.right = jnp.where(self.slot == t, turned, self.right)
         self.left = jnp.where(self.slot == t + 1, turned, self.left)
-
-
-def pack_forcing(packer, count, velocity, mask, level, here):
-    packer.add(count, velocity[1, level, here])
-    packer.add(count + 1, mask[level, here].astype(jnp.float32))
 
 
 def interior(tracers, velocity, mask, _, partial, pack_left, pack_right, weights):
@@ -235,7 +279,7 @@
             here = pl.ds(begin, 8)
             wm2, wm1, w0, wp1, wp2 = [weights[n, here] for n in range(5)]
             columns = column_weights(velocity, mask, level, here)
-            packer = Packer(lanes)
+            packer = Packer(count, velocity, mask, level, here)
             later = Deferred(DEPTH)
             for t in range(count):
                 at = lambda offset: tracers[t, level, pl.ds(begin + offset, 8)]
@@ -246,7 +290,6 @@
                 later.put(
                     partial, (t, level, here), partial[t, level, here] + sweep_across(value, columns)
                 )
-            pack_forcing(packer, count, velocity, mask, level, here)
             later.flush()
             pack_right[level, here] = packer.right
             pack_left[level, here] = packer.left
@@ -278,7 +321,7 @@
             else:
                 z2, z1 = jnp.where(row8 > 5, wp2, 0.0), jnp.where(row8 > 6, wp1, 0.0)
                 wp2, wp1 = jnp.where(row8 > 5, 0.0, wp2), jnp.where(row8 > 6, 0.0, wp1)
-            packer = Packer(lanes)
+            packer = Packer(count, velocity, mask, level, here)
             later = Deferred(DEPTH)
             for t in range(count):
                 centre = tracers[t, level, here]
@@ -298,7 +341,6 @@
                 )
                 later.put(swept, (t, level, pl.ds(8 * side, 8)), value)
                 packer.add(t, value)
-            pack_forcing(packer, count, velocity, mask, level, here)
             later.flush()
             pack_right[level, here] = packer.right
             pack_left[level, here] = packer.left
@@ -307,9 +349,16 @@
     lax.fori_loop(0, levels, level_step, 0)
 
 
-def border_across(swept, velocity, mask, _, partial):
-    count, levels = swept.shape[:2]
+PREPARED = 8
+
+
+def border_across(swept, velocity, mask, my_left, my_right, _, partial, ready):
+    count, levels, _, lanes = swept.shape
     length = mask.shape[1]
+    place, size = lax.axis_index("ty"), lax.axis_size("ty")
+    has_left = jnp.where(place > 0, 1.0, 0.0)
+    has_right = jnp.where(place < size - 1, 1.0, 0.0)
+    col = lambda value, n: jnp.broadcast_to(value[:, n : n + 1], value.shape)
 
     def step(index, carry):
         level, side = index // 2, index % 2
@@ -324,73 +373,93 @@
 
     lax.fori_loop(0, 2 * levels, step, 0)
 
-
-def finish(
-    partial, velocity, mask, my_left, my_right, from_left, from_right, edges, done, updated, even, odd, sems
-):
+    def prepare(level, carry):
+        for block in range(length // 8):
+            here = pl.ds(8 * block, 8)
+            wet = mask[level, here].astype(jnp.float32)
+            flow = velocity[1, level, here]
+            opened = flow * wet * pltpu.roll(wet, 1, 1)
+            left, right = my_left[level, here], my_right[level, here]
+            arrays = (
+                col(flow * wet, 0) * has_left,
+                col(wet, lanes - 1) * has_right,
+                face_terms(col(opened, 1))[0] * has_left,
+                face_terms(col(opened, lanes - 1))[3] * has_right,
+                pltpu.roll(left, lanes - 2, 1),
+                pltpu.roll(left, lanes - 3, 1),
+                pltpu.roll(right, lanes - 2, 1),
+                pltpu.roll(right, lanes - 1, 1),
+            )
+            for n, array in enumerate(arrays):
+                ready[n, level, here] = array
+        return carry
+
+    lax.fori_loop(0, levels, prepare, 0)
+
+
+def finish(ready, from_left, from_right, _, done, updated, even, odd, sems):
     count, levels, length, lanes = done.shape
     blocks = length // 8
     lane = lax.broadcasted_iota(jnp.int32, (8, lanes), 1)
     is_odd = lane % 2 == 1
     slot_odd = (lane // 2) % 2 == 1
-    has_left, has_right = edges[0], edges[1]
+    col = lambda value, n: jnp.broadcast_to(value[:, n : n + 1], value.shape)
 
     def level_step(level, carry):
         for block in range(blocks):
             here = pl.ds(8 * block, 8)
-            wet = mask[level, here].astype(jnp.float32)
-            flow = velocity[1, level, here]
-            own_left = pltpu.roll(my_left[level, here], lanes - 2, 1)
-            own_right = my_right[level, here]
-            left = from_left[level, here] * has_left
-            right = pltpu.roll(from_right[level, here], lanes - 2, 1) * has_right
-            col = lambda value, n: jnp.broadcast_to(value[:, n : n + 1], value.shape)
-            s_wet, s_flow = 2 * (count + 1), 2 * count
-            wet_first, wet_last = col(wet, 0), col(wet, lanes - 1)
-            u0 = col(flow, 0) * (wet_first * col(left, s_wet + 1))
-            u1 = col(flow, 1) * (wet_first * col(wet, 1))
-            u127 = col(flow, lanes - 1) * (wet_last * col(wet, lanes - 2))
-            u128 = col(right, s_flow) * (wet_last * col(right, s_wet))
+            open_low, open_high, a1, e127, s0, s1, s127, s126 = (
+                ready[n, level, here] for n in range(PREPARED)
+            )
+            left, right = from_left[level, here], pltpu.roll(from_right[level, here], lanes - 4, 1)
+            u0 = open_low * col(left, 2 * count + 1)
+            u128 = open_high * col(right, 2 * count - 2)
             a0, b0, d0, e0 = face_terms(u0)
-            a1 = face_terms(u1)[0]
-            e127 = face_terms(u127)[3]
             a128, b128, d128, e128 = face_terms(u128)
-            low = (
-                jnp.where(is_odd, a1, a0) * left
-                + jnp.where(is_odd, 0.0, b0 - a1) * pltpu.roll(left, lanes - 1, 1)
-                + jnp.where(is_odd, 0.0, d0 - u0) * own_left
-                + jnp.where(is_odd, 0.0, e0) * pltpu.roll(own_left, lanes - 1, 1)
+            low = jnp.where(is_odd, a1, a0) * left + jnp.where(
+                is_odd,
+                0.0,
+                (b0 - a1) * pltpu.roll(left, lanes - 1, 1) + ((d0 - u0) * s0 + e0 * s1),
             )
-            high = (
-                jnp.where(is_odd, -e128, -e127) * right
-                + jnp.where(is_odd, e127 - d128, 0.0) * pltpu.roll(right, 1, 1)
-                + jnp.where(is_odd, u128 - b128, 0.0) * own_right
-                + jnp.where(is_odd, -a128, 0.0) * pltpu.roll(own_right, 1, 1)
-            )
-            high = pltpu.roll(high, lanes - 2, 1)
+            high = jnp.where(
+                is_odd,
+                (e127 - d128) * pltpu.roll(right, 1, 1) + ((u128 - b128) * s127 - a128 * s126),
+                0.0,
+            ) - jnp.where(is_odd, e128, e127) * right
             even[level, here] = jnp.where(slot_odd, high, low)
             odd[level, here] = jnp.where(slot_odd, low, high)
         return carry
 
     lax.fori_loop(0, levels, level_step, 0)
     outer = (lane < 2) | (lane > lanes - 3)
-    step = max(n for n in (4, 2, 1) if count % n == 0)
+    step = 8 if count % 8 == 0 else 2
 
     def copy(chunk):
         part = pl.ds(chunk * step, step)
         return pltpu.make_async_copy(done.at[part], updated.at[part], sems.at[chunk])
 
-    for chunk in range(count // step):
+    def add(chunk, carry):
+        start = chunk * step
+        turns = [jnp.where(start + n == 0, 0, lanes - 2 * (start + n)) for n in range(step)]
+        later = Deferred(2 * DEPTH)
         for level in range(levels):
             for block in range(blocks):
                 here = pl.ds(8 * block, 8)
                 packs = (even[level, here], odd[level, here])
-                for t in range(chunk * step, chunk * step + step):
-                    edge = pltpu.roll(packs[t % 2], (lanes - 2 * t) % lanes, 1)
-                    done[t, level, here] = done[t, level, here] + jnp.where(outer, edge, 0.0)
+                for n in range(step):
+                    edge = pltpu.roll(packs[n % 2], turns[n], 1)
+                    at = (start + n, level, here)
+                    later.put(done, at, done[at] + jnp.where(outer, edge, 0.0))
+        later.flush()
         copy(chunk).start()
-    for chunk in range(count // step):
+        return carry
+
+    def wait(chunk, carry):
         copy(chunk).wait()
+        return carry
+
+    lax.fori_loop(0, count // step, add, 0)
+    lax.fori_loop(0, count // step, wait, 0)
 
 
 def shards(
@@ -413,9 +482,10 @@
     down = lambda n: [((i + 1) % n, i) for i in range(n)]
     cells = count * levels * length * lanes
 
-    assert length % 8 == 0 and length >= 16 and 2 * count + 6 <= lanes
+    assert length % 16 == 0 and count % 2 == 0 and 2 * count + 4 <= lanes
     groups = -(-(2 * PAD + (count + 2) * levels) // 4) * 4
     row_message = pltpu.VMEM((groups, 2, 1, lanes), f32)
+    grazers = count - NNUT - NPHY
     first, last = call(
         pack_rows,
         (row_message, row_message),
@@ -438,7 +508,11 @@
     tendency = call(
         ecology,
         field,
-        [VMEM, VMEM, VMEM] + [SMEM] * 7,
+        [VMEM] * 4 + [SMEM] * 6,
+        scratch=[
+            pltpu.VMEM((8 * grazers, 16 * NPHY), jnp.bfloat16),
+            pltpu.VMEM((8 * NPHY, 16 * grazers), jnp.bfloat16),
+        ],
         flops=40 * cells,
         bytes_accessed=8 * cells,
         limit=2 << 20,
@@ -446,12 +520,12 @@
         held,
         mask,
         in_vmem(sunlight),
+        in_vmem(palatable),
         growth_max,
         half_sat,
         light_half,
         graze_max,
         graze_half,
-        palatable.astype(f32),
         stoichiometry,
     )
     partial, pack_left, pack_right = call(
@@ -476,32 +550,30 @@
     )(held, flow, mask, in_vmem(before), in_vmem(after), partial, pack_left, pack_right)
     from_left = lax.ppermute(pack_right, "ty", up(ty))
     from_right = lax.ppermute(pack_left, "ty", down(ty))
-    partial = call(
+    partial, ready = call(
         border_across,
-        field,
-        [VMEM] * 4,
+        (field, pltpu.VMEM((PREPARED, levels, length, lanes), f32)),
+        [VMEM] * 6,
         flops=10 * cells,
         bytes_accessed=6 * cells,
         limit=2 << 20,
-        input_output_aliases={3: 0},
-    )(swept, flow, mask, partial)
-    place = lax.axis_index("ty")
-    edges = jnp.stack([place > 0, place < ty - 1]).astype(f32)
+        input_output_aliases={5: 0},
+    )(swept, flow, mask, pack_left, pack_right, partial)
     return call(
         finish,
         (field, jax.ShapeDtypeStruct(tracers.shape, f32)),
-        [VMEM] * 7 + [SMEM],
+        [VMEM] * 4,
         out_specs=[VMEM, HBM],
-        input_output_aliases={0: 0},
+        input_output_aliases={3: 0},
         scratch=[
             pltpu.VMEM((levels, length, lanes), f32),
             pltpu.VMEM((levels, length, lanes), f32),
-            pltpu.SemaphoreType.DMA((count,)),
+            pltpu.SemaphoreType.DMA((count // 2,)),
         ],
         flops=4 * cells,
         bytes_accessed=8 * cells,
-        limit=4 << 20,
-    )(partial, flow, mask, pack_left, pack_right, in_vmem(from_left), in_vmem(from_right), edges)[1]
+        limit=2 << 20,
+    )(ready, in_vmem(from_left), in_vmem(from_right), partial)[1]
 
 
 def solution(mesh):

time: 21.4 us -> 20.7 us (0.967)
  Pallas kernels: 12.4 us -> 11.2 us
  waiting for transfers between devices: 2.88 us -> 3.44 us
    ppermute x1, waiting for transfers between devices: 0.89 us -> 1.83 us  [shards(): before = lax.ppermute(last, 'tx', up(tx))]
    pallas_call x1, Pallas kernels: 2.98 us -> 2.27 us  [shards(): call(finish, (field, jax.ShapeDtypeStruct(tracers.shape, f32)), [VMEM] *...]
    pallas_call x2, Pallas kernels: 5.52 us -> 5.06 us  [the longest x1 3.1 us: shards(): call(ecology, field, [VMEM] * 4 + [SMEM] * 6, scratch=[pltpu.VMEM((8 * gr...]
    ppermute x1, waiting for transfers between devices: 1.99 us -> 1.6 us  [shards(): from_left = lax.ppermute(pack_right, 'ty', up(ty))]
  transfers between devices with their start and end apart: 4 -> 4, of which waited for: 2 -> 2; matrix products, arithmetic and copies ran while one was open for 0% -> 0% of each run, Pallas kernels for 35% -> 34%
where the time goes in v3:
time: 20.7 us; the launch traced here: 20.5 us
  Pallas kernels  11.2 us (54%)
  starting transfers between devices  5.7 us (28%)
  waiting for transfers between devices  3.44 us (17%)
    ppermute x1, starting transfers between devices, shards(): after = lax.ppermute(first, 'tx', down(tx))  5.14 us
    pallas_call x1, Pallas kernels, shards(): call(ecology, field, [VMEM] * 4 + [SMEM] * 6, scratch=[pltpu.VMEM((8 * gr...  3.1 us
    pallas_call x1, Pallas kernels, shards(): call(finish, (field, jax.ShapeDtypeStruct(tracers.shape, f32)), [VMEM] *...  2.27 us
    pallas_call x1, Pallas kernels, shards(): call(border_across, (field, pltpu.VMEM((PREPARED, levels, length, lanes),...  1.96 us
    pallas_call x1, Pallas kernels, shards(): call(interior, (field, columns, columns), [VMEM] * 4, scratch=[pltpu.VMEM...  1.88 us
    ppermute x1, waiting for transfers between devices, shards(): before = lax.ppermute(last, 'tx', up(tx))  1.83 us
    ppermute x1, waiting for transfers between devices, shards(): from_left = lax.ppermute(pack_right, 'ty', up(ty))  1.6 us
    pallas_call x1, Pallas kernels, shards(): call(pack_rows, (row_message, row_message), [HBM, HBM, HBM], scratch=[plt...  1.17 us
  transfers between devices with their start and end apart: 4, of which 2 were waited for; matrix products, arithmetic and copies ran while one was open for 0% of the time, Pallas kernels for 34%

profile of v3, /device:TPU:0, one launch (start us, length us, event | category | flops | bytes accessed | tf_op | source)
XLA Modules:
  0.0 20.5 jit_solution(7615079768799944046)
XLA Ops:
  0.0 0.0 copy-start
  0.0 0.0 copy-start.2
  0.0 0.0 copy-start.8
  0.0 0.0 copy-start.7
  0.0 0.0 copy-start.5
  0.0 0.0 copy-start.6
  0.1 0.0 copy-start.3
  0.1 1.2 %shard_map.109 = (f32[136,2,1,128]{3,2,1,0:T(1,128)S(1)}, f32[136,2,1,128]{3,2,1,0:T(1,128)S(1)}) custom-call(f32[120,32,1,128]{3,2,1,0:T(1,128)} %bitcast.5, f32[2,3,32,1,128]{4,3,2,1,0:T(1,128)} %bitcast.6, s32[3,32,1,128]{3,2,1,0:T(1,128)} %bitcast.7), custom_call_target="tpu_custom_call" | custom-call | bytes 139264 | tf_op jit(solution)/shard_map/pallas_call | solution.py:489
  1.2 5.1 %collective-permute-start.1 = (f32[272,128]{1,0:T(8,128)S(1)}, f32[272,128]{1,0:T(8,128)S(1)}, u32[]{:S(2)}, u32[]{:S(2)}) collective-permute-start(f32[272,128]{1,0:T(8,128)S(1)} %bitcast.9), channel_id=1, source_target_pairs={{4,0},{8,4},{12,8},{0,12},{5,1},{9,5},{13,9},{1,13},{6,2},{10,6},{... | collective-permute-start | bytes 417800 | tf_op jit(solution)/shard_map/ppermute | solution.py:503
  6.4 0.0 collective-permute-start
  6.4 0.0 copy-done
  6.4 0.0 copy-done.2
  6.4 0.0 copy-done.10
  6.4 0.0 copy-done.4
  6.4 0.0 copy-done.9
  6.4 0.0 copy-done.8
  6.4 0.0 copy-done.7
  6.4 0.0 copy-done.5
  6.5 0.0 copy-done.6
  6.5 0.0 copy-done.3
  6.5 3.1 %shard_map.110._ = f32[40,3,32,128]{3,2,1,0:T(8,128)S(1)} custom-call(f32[40,3,32,128]{3,2,1,0:T(8,128)S(1)} %copy-done, s32[3,32,128]{2,1,0:T(8,128)S(1)} %copy-done.2, f32[32,128]{1,0:T(8,128)S(1)} %copy-done.3, s32[10,26]{1,0:T(8,128)S(1)} %copy-done.4, f32[26]{0:T(128)S(1)} %copy-done.6, f32[4,26]{1,0:T(4,128)S(1)} %copy-done.5, f32[26]{0:T(128)S(1)} %copy-done.7, ...), custom_call_target="tpu_custom_call" | custom-call | flops 19660800 | bytes 3932160 | tf_op jit(solution)/shard_map/pallas_call | solution.py:508
  9.6 0.0 copy-done.1
  9.6 1.9 %shard_map.111 = (f32[40,3,32,128]{3,2,1,0:T(8,128)S(1)}, f32[3,32,128]{2,1,0:T(8,128)S(1)}, f32[3,32,128]{2,1,0:T(8,128)S(1)}) custom-call(f32[40,3,32,128]{3,2,1,0:T(8,128)S(1)} %copy-done, f32[2,3,32,128]{3,2,1,0:T(8,128)S(1)} %copy-done.1, s32[3,32,128]{2,1,0:T(8,128)S(1)} %copy-done.2, ...), custom_call_target="tpu_custom_call", output_to_operand_aliasing={{0}: (3, {})} | custom-call | flops 9830400 | bytes 3932160 | tf_op jit(solution)/shard_map/pallas_call | solution.py:531
  11.5 0.0 collective-permute-done.1.after
  11.5 1.8 %collective-permute-done.before = f32[272,128]{1,0:T(8,128)S(1)} collective-permute-done((f32[272,128]{1,0:T(8,128)S(1)}, f32[272,128]{1,0:T(8,128)S(1)}, u32[]{:S(2)}, u32[]{:S(2)}) %collective-permute-start) | collective-permute-done | bytes 139296 | tf_op jit(solution)/shard_map/ppermute | solution.py:502
  13.3 0.8 %shard_map.112 = (f32[40,3,16,128]{3,2,1,0:T(8,128)S(1)}, f32[3,32,128]{2,1,0:T(8,128)S(1)}, f32[3,32,128]{2,1,0:T(8,128)S(1)}, f32[40,3,32,128]{3,2,1,0:T(8,128)S(1)}) custom-call(f32[40,3,32,128]{3,2,1,0:T(8,128)S(1)} %copy-done, f32[2,3,32,128]{3,2,1,0:T(8,128)S(1)} %copy-done.1, ...), custom_call_target="tpu_custom_call", output_to_operand_aliasing={{3}: (5, {}), {1}: (6, {}), {2}: (7, {})} | custom-call | flops 4915200 | bytes 3932160 | tf_op jit(solution)/shard_map/pallas_call | solution.py:541
  14.1 0.1 collective-permute-start.3
  14.2 0.5 %collective-permute-start.2 = (f32[3,32,128]{2,1,0:T(8,128)S(1)}, f32[3,32,128]{2,1,0:T(8,128)S(1)}, u32[]{:S(2)}, u32[]{:S(2)}) collective-permute-start(f32[3,32,128]{2,1,0:T(8,128)S(1)} %get-tuple-element.24.my_right), channel_id=1, source_target_pairs={{0,1},{1,2},{2,3},{3,0},{4,5},{5,6},{6,7},{7,4},{8,9},{9,10},{10,1... | collective-permute-start | bytes 147464 | tf_op jit(solution)/shard_map/ppermute | solution.py:551
  14.7 2.0 %shard_map.113 = (f32[40,3,32,128]{3,2,1,0:T(8,128)S(1)}, f32[8,3,32,128]{3,2,1,0:T(8,128)S(1)}) custom-call(f32[40,3,16,128]{3,2,1,0:T(8,128)S(1)} %get-tuple-element.22.swept, f32[2,3,32,128]{3,2,1,0:T(8,128)S(1)} %copy-done.1, s32[3,32,128]{2,1,0:T(8,128)S(1)} %copy-done.2, ...), custom_call_target="tpu_custom_call", output_to_operand_aliasing={{0}: (5, {})} | custom-call | flops 4915200 | bytes 2949120 | tf_op jit(solution)/shard_map/pallas_call | solution.py:553
  16.6 0.0 collective-permute-done.3.from_right
  16.7 1.6 %collective-permute-done.2.from_left = f32[3,32,128]{2,1,0:T(8,128)S(1)} collective-permute-done((f32[3,32,128]{2,1,0:T(8,128)S(1)}, f32[3,32,128]{2,1,0:T(8,128)S(1)}, u32[]{:S(2)}, u32[]{:S(2)}) %collective-permute-start.2) | collective-permute-done | bytes 49184 | tf_op jit(solution)/shard_map/ppermute | solution.py:551
  18.3 2.3 %shard_map.114 = (f32[40,3,32,128]{3,2,1,0:T(8,128)S(1)}, f32[40,3,32,128]{3,2,1,0:T(8,128)}) custom-call(f32[8,3,32,128]{3,2,1,0:T(8,128)S(1)} %get-tuple-element.26.ready, f32[3,32,128]{2,1,0:T(8,128)S(1)} %collective-permute-done.2.from_left, f32[3,32,128]{2,1,0:T(8,128)S(1)} %collective-permute-done.3.from_right, ...), custom_call_target="tpu_custom_call", output_to_operand_aliasing={{0}: (3, {})} | custom-call | flops 1966080 | bytes 3932160 | tf_op jit(solution)/shard_map/pallas_call | solution.py:562
  (4 shorter events, 0.0 us)
Async XLA Ops:
  0.0 6.4 %copy-start = (f32[40,3,32,128]{3,2,1,0:T(8,128)S(1)}, f32[40,3,32,128]{3,2,1,0:T(8,128)}, u32[]{:S(2)}) copy-start(f32[40,3,32,128]{3,2,1,0:T(8,128)} %tracers.5) | copy-start | bytes 5898244
  0.0 6.4 %copy-start.2 = (s32[3,32,128]{2,1,0:T(8,128)S(1)}, s32[3,32,128]{2,1,0:T(8,128)}, u32[]{:S(2)}) copy-start(s32[3,32,128]{2,1,0:T(8,128)} %mask.7) | copy-start | bytes 147460
  0.0 6.4 %copy-start.10 = (f32[4]{0:T(128)S(1)}, f32[4]{0:T(128)}, u32[]{:S(2)}) copy-start(f32[4]{0:T(128)} %stoichiometry.1) | copy-start | bytes 52
  0.0 6.4 %copy-start.4 = (s32[10,26]{1,0:T(8,128)S(1)}, s32[10,26]{1,0:T(8,128)}, u32[]{:S(2)}) copy-start(s32[10,26]{1,0:T(8,128)} %palatable.1) | copy-start | bytes 3124
  0.0 6.4 %copy-start.9 = (f32[10]{0:T(128)S(1)}, f32[10]{0:T(128)}, u32[]{:S(2)}) copy-start(f32[10]{0:T(128)} %graze_half.1) | copy-start | bytes 124
  0.0 6.4 %copy-start.8 = (f32[10]{0:T(128)S(1)}, f32[10]{0:T(128)}, u32[]{:S(2)}) copy-start(f32[10]{0:T(128)} %graze_max.1) | copy-start | bytes 124
  0.0 6.4 %copy-start.7 = (f32[26]{0:T(128)S(1)}, f32[26]{0:T(128)}, u32[]{:S(2)}) copy-start(f32[26]{0:T(128)} %light_half.1) | copy-start | bytes 316
  0.0 6.4 %copy-start.5 = (f32[4,26]{1,0:T(4,128)S(1)}, f32[4,26]{1,0:T(4,128)}, u32[]{:S(2)}) copy-start(f32[4,26]{1,0:T(4,128)} %half_sat.1) | copy-start | bytes 1252
  0.0 6.4 %copy-start.6 = (f32[26]{0:T(128)S(1)}, f32[26]{0:T(128)}, u32[]{:S(2)}) copy-start(f32[26]{0:T(128)} %growth_max.1) | copy-start | bytes 316
  0.1 6.4 %copy-start.3 = (f32[32,128]{1,0:T(8,128)S(1)}, f32[32,128]{1,0:T(8,128)}, u32[]{:S(2)}) copy-start(f32[32,128]{1,0:T(8,128)} %sunlight.1) | copy-start | bytes 49156
  1.2 10.2 %collective-permute-start.1 = (f32[272,128]{1,0:T(8,128)S(1)}, f32[272,128]{1,0:T(8,128)S(1)}, u32[]{:S(2)}, u32[]{:S(2)}) collective-permute-start(f32[272,128]{1,0:T(8,128)S(1)} %bitcast.9), channel_id=1, source_target_pairs={{4,0},{8,4},{12,8},{0,12},{5,1},{9,5},{13,9},{1,13},{6,2},{10,6},{... | collective-permute-start | bytes 417800 | tf_op jit(solution)/shard_map/ppermute | solution.py:503
  6.4 3.2 %copy-start.1 = (f32[2,3,32,128]{3,2,1,0:T(8,128)S(1)}, f32[2,3,32,128]{3,2,1,0:T(8,128)}, u32[]{:S(2)}) copy-start(f32[2,3,32,128]{3,2,1,0:T(8,128)} %velocity.5) | copy-start | bytes 294916
  6.4 6.9 %collective-permute-start = (f32[272,128]{1,0:T(8,128)S(1)}, f32[272,128]{1,0:T(8,128)S(1)}, u32[]{:S(2)}, u32[]{:S(2)}) collective-permute-start(f32[272,128]{1,0:T(8,128)S(1)} %bitcast.8), channel_id=1, source_target_pairs={{0,4},{4,8},{8,12},{12,0},{1,5},{5,9},{9,13},{13,1},{2,6},{6,10},{... | collective-permute-start | bytes 417800 | tf_op jit(solution)/shard_map/ppermute | solution.py:502
  14.1 2.5 %collective-permute-start.3 = (f32[3,32,128]{2,1,0:T(8,128)S(1)}, f32[3,32,128]{2,1,0:T(8,128)S(1)}, u32[]{:S(2)}, u32[]{:S(2)}) collective-permute-start(f32[3,32,128]{2,1,0:T(8,128)S(1)} %get-tuple-element.23.my_left), channel_id=1, source_target_pairs={{1,0},{2,1},{3,2},{0,3},{5,4},{6,5},{7,6},{4,7},{9,8},{10,9},{11,1... | collective-permute-start | bytes 147464 | tf_op jit(solution)/shard_map/ppermute | solution.py:552
  14.2 4.1 %collective-permute-start.2 = (f32[3,32,128]{2,1,0:T(8,128)S(1)}, f32[3,32,128]{2,1,0:T(8,128)S(1)}, u32[]{:S(2)}, u32[]{:S(2)}) collective-permute-start(f32[3,32,128]{2,1,0:T(8,128)S(1)} %get-tuple-element.24.my_right), channel_id=1, source_target_pairs={{0,1},{1,2},{2,3},{3,0},{4,5},{5,6},{6,7},{7,4},{8,9},{9,10},{10,1... | collective-permute-start | bytes 147464 | tf_op jit(solution)/shard_map/ppermute | solution.py:551

commit v4 on v3

--- a/solution.py
+++ b/solution.py
@@ -9,7 +9,6 @@
 NNUT = 4
 NPHY = 26
 DEPTH = 12
-PAD = 4
 
 plankton_mortality = 0.05
 grazer_mortality = 0.3
@@ -90,25 +89,26 @@
 def pack_rows(tracers, velocity, mask, first, last, edge, sems):
     count, length = tracers.shape[0], tracers.shape[1]
     levels = mask.shape[0]
+    forcing = pl.ds(count, levels)
     copies = []
-    for side, (out, start) in enumerate(((first, 0), (last, length - 2))):
-        rows = pl.ds(start, 2)
+    for side, (out, rows, row) in enumerate(
+        ((first, pl.ds(0, 2), pl.ds(0, 1)), (last, pl.ds(length - 2, 2), pl.ds(length - 1, 1)))
+    ):
         copies += [
-            pltpu.make_async_copy(tracers.at[:, rows], out.at[pl.ds(PAD, count)], sems.at[side, 0]),
+            pltpu.make_async_copy(tracers.at[:, rows], out.at[pl.ds(0, count)], sems.at[side, 0]),
             pltpu.make_async_copy(
-                velocity.at[0, :, rows], out.at[pl.ds(PAD + count, levels)], sems.at[side, 1]
+                velocity.at[0, :, row], out.at[forcing, pl.ds(0, 1)], sems.at[side, 1]
             ),
-            pltpu.make_async_copy(mask.at[:, rows], edge.at[side], sems.at[side, 2]),
+            pltpu.make_async_copy(mask.at[:, row], edge.at[side], sems.at[side, 2]),
         ]
     for copy in copies:
         copy.start()
     for out in (first, last):
-        out[0:PAD] = jnp.zeros((PAD,) + out.shape[1:], out.dtype)
-        out[PAD + count + 2 * levels :] = jnp.zeros_like(out[PAD + count + 2 * levels :])
+        out[count + levels :] = jnp.zeros_like(out[count + levels :])
     for copy in copies:
         copy.wait()
     for side, out in enumerate((first, last)):
-        out[PAD + count + levels : PAD + count + 2 * levels] = edge[side].astype(jnp.float32)
+        out[forcing, pl.ds(1, 1)] = edge[side].astype(jnp.float32)
 
 
 def ecology(
@@ -122,6 +122,7 @@
     graze_max,
     graze_half,
     stoichiometry,
+    _,
     tendency,
     to_grazers,
     to_plants,
@@ -156,17 +157,17 @@
             recycled = jnp.zeros((16, lanes), f32)
             rates = []
             later = Deferred(DEPTH)
+
+            def add(t, change):
+                later.put(tendency, (t, level, rows), tendency[t, level, rows] + wet * change)
+
             for z in range(grazers):
                 grazer = tracers[NNUT + NPHY + z, level, rows]
                 prey = entry(available, z)
                 rate = graze_max[z] * grazer / (graze_half[z] + prey)
                 ingested = rate * prey
                 loss = grazer_mortality * grazer * grazer
-                later.put(
-                    tendency,
-                    (NNUT + NPHY + z, level, rows),
-                    wet * (assimilation * ingested - loss),
-                )
+                add(NNUT + NPHY + z, assimilation * ingested - loss)
                 recycled = recycled + (loss + (1.0 - assimilation) * ingested)
                 rates.append(rate)
             pressure = jnp.dot(
@@ -185,13 +186,9 @@
                     (1.0 + worst) * (1.0 + light_half[k] * darkness)
                 )
                 recycled = recycled + (plankton_mortality * plant - growth)
-                later.put(
-                    tendency,
-                    (NNUT + k, level, rows),
-                    wet * (growth - plant * (entry(pressure, k) + plankton_mortality)),
-                )
+                add(NNUT + k, growth - plant * (entry(pressure, k) + plankton_mortality))
             for j in range(NNUT):
-                later.put(tendency, (j, level, rows), wet * (stoichiometry[j] * recycled))
+                add(j, stoichiometry[j] * recycled)
             later.flush()
         return carry
 
@@ -266,7 +263,7 @@
         self.left = jnp.where(self.slot == t + 1, turned, self.left)
 
 
-def interior(tracers, velocity, mask, _, partial, pack_left, pack_right, weights):
+def interior(tracers, velocity, mask, partial, pack_left, pack_right, weights):
     count, levels, length, lanes = tracers.shape
     zero = jnp.zeros((1, lanes), jnp.float32)
 
@@ -287,14 +284,15 @@
                     w0 * at(0) + (wm1 * at(-1) + wm2 * at(-2)) + (wp1 * at(1) + wp2 * at(2))
                 )
                 packer.add(t, value)
-                later.put(
-                    partial, (t, level, here), partial[t, level, here] + sweep_across(value, columns)
-                )
+                later.put(partial, (t, level, here), sweep_across(value, columns))
             later.flush()
             pack_right[level, here] = packer.right
             pack_left[level, here] = packer.left
             return carry
 
+        for t in range(count):
+            partial[t, level, 0:8] = jnp.zeros((8, lanes), jnp.float32)
+            partial[t, level, length - 8 : length] = jnp.zeros((8, lanes), jnp.float32)
         return lax.fori_loop(1, length // 8 - 1, block_step, carry)
 
     lax.fori_loop(0, levels, level_step, 0)
@@ -305,13 +303,10 @@
 ):
     count, levels, length, lanes = tracers.shape
     row8 = lax.broadcasted_iota(jnp.int32, (8, lanes), 0)
-    base = 2 * PAD
 
     def level_step(level, carry):
-        pick = lambda ref, field, row: ref[pl.ds(base + 2 * ((count + field) * levels + level) + row, 1)]
-        weights = row_weights(
-            velocity, mask, level, pick(before, 1, 1), pick(after, 1, 0), pick(after, 0, 0)
-        )
+        pick = lambda ref, field: ref[pl.ds(2 * (count * levels + level) + field, 1)]
+        weights = row_weights(velocity, mask, level, pick(before, 1), pick(after, 1), pick(after, 0))
         for side, first in enumerate((0, length - 8)):
             here = pl.ds(first, 8)
             wm2, wm1, w0, wp1, wp2 = [w[first : first + 8] for w in weights]
@@ -331,9 +326,12 @@
                         return pltpu.roll(centre, -offset % 8, 0)
                     return tracers[t, level, pl.ds(first + offset, 8)]
 
-                group = base + 2 * (t * levels + level)
+                group = 2 * (t * levels + level)
                 if side == 0:
                     beyond = z2 * before[pl.ds(group, 8)] + z1 * before[pl.ds(group + 1, 8)]
+                elif 2 * t * levels < 7:
+                    outside = after[pl.ds(group, 8)]
+                    beyond = z2 * pltpu.roll(outside, 6, 0) + z1 * pltpu.roll(outside, 7, 0)
                 else:
                     beyond = z2 * after[pl.ds(group - 6, 8)] + z1 * after[pl.ds(group - 7, 8)]
                 value = (
@@ -483,14 +481,14 @@
     cells = count * levels * length * lanes
 
     assert length % 16 == 0 and count % 2 == 0 and 2 * count + 4 <= lanes
-    groups = -(-(2 * PAD + (count + 2) * levels) // 4) * 4
+    groups = -(-(count * levels + levels + 1) // 4) * 4
     row_message = pltpu.VMEM((groups, 2, 1, lanes), f32)
     grazers = count - NNUT - NPHY
     first, last = call(
         pack_rows,
         (row_message, row_message),
         [HBM, HBM, HBM],
-        scratch=[pltpu.VMEM((2, levels, 2, 1, lanes), jnp.int32), pltpu.SemaphoreType.DMA((2, 3))],
+        scratch=[pltpu.VMEM((2, levels, 1, 1, lanes), jnp.int32), pltpu.SemaphoreType.DMA((2, 3))],
         bytes_accessed=8 * groups * lanes,
         limit=2 << 20,
     )(
@@ -505,10 +503,19 @@
     held, flow, mask = in_vmem(tracers), in_vmem(velocity), in_vmem(land_mask)
     field = pltpu.VMEM(tracers.shape, f32)
     columns = pltpu.VMEM((levels, length, lanes), f32)
-    tendency = call(
+    partial, pack_left, pack_right = call(
+        interior,
+        (field, columns, columns),
+        [VMEM] * 3,
+        scratch=[pltpu.VMEM((5, length, lanes), f32)],
+        flops=20 * cells,
+        bytes_accessed=8 * cells,
+        limit=2 << 20,
+    )(held, flow, mask)
+    partial = call(
         ecology,
         field,
-        [VMEM] * 4 + [SMEM] * 6,
+        [VMEM] * 4 + [SMEM] * 6 + [VMEM],
         scratch=[
             pltpu.VMEM((8 * grazers, 16 * NPHY), jnp.bfloat16),
             pltpu.VMEM((8 * NPHY, 16 * grazers), jnp.bfloat16),
@@ -516,6 +523,7 @@
         flops=40 * cells,
         bytes_accessed=8 * cells,
         limit=2 << 20,
+        input_output_aliases={10: 0},
     )(
         held,
         mask,
@@ -527,17 +535,8 @@
         graze_max,
         graze_half,
         stoichiometry,
-    )
-    partial, pack_left, pack_right = call(
-        interior,
-        (field, columns, columns),
-        [VMEM] * 4,
-        scratch=[pltpu.VMEM((5, length, lanes), f32)],
-        flops=20 * cells,
-        bytes_accessed=8 * cells,
-        limit=2 << 20,
-        input_output_aliases={3: 0},
-    )(held, flow, mask, tendency)
+        partial,
+    )
     swept, pack_left, pack_right, partial = call(
         border,
         (pltpu.VMEM((count, levels, 16, lanes), f32), columns, columns, field),

time: 20.7 us -> 20.5 us (level)
  waiting for transfers between devices: 3.44 us -> 3.16 us
    ppermute x1, waiting for transfers between devices: 1.83 us -> 1.56 us  [shards(): before = lax.ppermute(last, 'tx', up(tx))]
where the time goes in v4:
time: 20.5 us; the launch traced here: 20.4 us
  Pallas kernels  11.3 us (55%)
  starting transfers between devices  5.7 us (28%)
  waiting for transfers between devices  3.16 us (15%)
    ppermute x1, starting transfers between devices, shards(): after = lax.ppermute(first, 'tx', down(tx))  5.14 us
    pallas_call x1, Pallas kernels, shards(): call(ecology, field, [VMEM] * 4 + [SMEM] * 6 + [VMEM], scratch=[pltpu.VME...  3.18 us
    pallas_call x1, Pallas kernels, shards(): call(finish, (field, jax.ShapeDtypeStruct(tracers.shape, f32)), [VMEM] *...  2.27 us
    pallas_call x1, Pallas kernels, shards(): call(border_across, (field, pltpu.VMEM((PREPARED, levels, length, lanes),...  1.97 us
    pallas_call x1, Pallas kernels, shards(): call(interior, (field, columns, columns), [VMEM] * 3, scratch=[pltpu.VMEM...  1.85 us
    ppermute x1, waiting for transfers between devices, shards(): from_left = lax.ppermute(pack_right, 'ty', up(ty))  1.59 us
    ppermute x1, waiting for transfers between devices, shards(): before = lax.ppermute(last, 'tx', up(tx))  1.56 us
    pallas_call x1, Pallas kernels, shards(): call(pack_rows, (row_message, row_message), [HBM, HBM, HBM], scratch=[plt...  1.17 us
  transfers between devices with their start and end apart: 4, of which 2 were waited for; matrix products, arithmetic and copies ran while one was open for 0% of the time, Pallas kernels for 34%

profile of v4, /device:TPU:0, one launch (start us, length us, event | category | flops | bytes accessed | tf_op | source)
XLA Modules:
  0.0 20.4 jit_solution(17183217938426218510)
XLA Ops:
  0.0 0.0 copy-start
  0.0 0.0 copy-start.5
  0.0 0.0 copy-start.6
  0.0 0.0 copy-start.7
  0.0 0.0 copy-start.8
  0.1 0.0 copy-start.9
  0.1 0.0 copy-start.10
  0.1 1.2 %shard_map.109 = (f32[124,2,1,128]{3,2,1,0:T(1,128)S(1)}, f32[124,2,1,128]{3,2,1,0:T(1,128)S(1)}) custom-call(f32[120,32,1,128]{3,2,1,0:T(1,128)} %bitcast.5, f32[2,3,32,1,128]{4,3,2,1,0:T(1,128)} %bitcast.6, s32[3,32,1,128]{3,2,1,0:T(1,128)} %bitcast.7), custom_call_target="tpu_custom_call" | custom-call | bytes 126976 | tf_op jit(solution)/shard_map/pallas_call | solution.py:487
  1.3 5.1 %collective-permute-start.1 = (f32[248,128]{1,0:T(8,128)S(1)}, f32[248,128]{1,0:T(8,128)S(1)}, u32[]{:S(2)}, u32[]{:S(2)}) collective-permute-start(f32[248,128]{1,0:T(8,128)S(1)} %bitcast.9), channel_id=1, source_target_pairs={{4,0},{8,4},{12,8},{0,12},{5,1},{9,5},{13,9},{1,13},{6,2},{10,6},{... | collective-permute-start | bytes 380936 | tf_op jit(solution)/shard_map/ppermute | solution.py:501
  6.4 0.0 collective-permute-start
  6.4 0.0 copy-done
  6.4 0.0 copy-done.1
  6.4 0.0 copy-done.2
  6.4 1.8 %shard_map.110 = (f32[40,3,32,128]{3,2,1,0:T(8,128)S(1)}, f32[3,32,128]{2,1,0:T(8,128)S(1)}, f32[3,32,128]{2,1,0:T(8,128)S(1)}) custom-call(f32[40,3,32,128]{3,2,1,0:T(8,128)S(1)} %copy-done, f32[2,3,32,128]{3,2,1,0:T(8,128)S(1)} %copy-done.1, s32[3,32,128]{2,1,0:T(8,128)S(1)} %copy-done.2), custom_call_target="tpu_custom_call" | custom-call | flops 9830400 | bytes 3932160 | tf_op jit(solution)/shard_map/pallas_call | solution.py:506
  8.3 0.0 copy-done.3
  8.3 0.0 copy-done.4
  8.3 0.0 copy-done.5
  8.3 0.0 copy-done.6
  8.3 0.0 copy-done.7
  8.3 0.0 copy-done.8
  8.3 0.0 copy-done.9
  8.3 0.0 copy-done.10
  8.4 3.2 %shard_map.111.partial = f32[40,3,32,128]{3,2,1,0:T(8,128)S(1)} custom-call(f32[40,3,32,128]{3,2,1,0:T(8,128)S(1)} %copy-done, s32[3,32,128]{2,1,0:T(8,128)S(1)} %copy-done.2, f32[32,128]{1,0:T(8,128)S(1)} %copy-done.3, s32[10,26]{1,0:T(8,128)S(1)} %copy-done.4, f32[26]{0:T(128)S(1)} %copy-done.6, ...), custom_call_target="tpu_custom_call", output_to_operand_aliasing={{}: (10, {})} | custom-call | flops 19660800 | bytes 3932160 | tf_op jit(solution)/shard_map/pallas_call | solution.py:515
  11.5 0.0 collective-permute-done.1.after
  11.6 1.6 %collective-permute-done.before = f32[248,128]{1,0:T(8,128)S(1)} collective-permute-done((f32[248,128]{1,0:T(8,128)S(1)}, f32[248,128]{1,0:T(8,128)S(1)}, u32[]{:S(2)}, u32[]{:S(2)}) %collective-permute-start) | collective-permute-done | bytes 127008 | tf_op jit(solution)/shard_map/ppermute | solution.py:500
  13.1 0.8 %shard_map.112 = (f32[40,3,16,128]{3,2,1,0:T(8,128)S(1)}, f32[3,32,128]{2,1,0:T(8,128)S(1)}, f32[3,32,128]{2,1,0:T(8,128)S(1)}, f32[40,3,32,128]{3,2,1,0:T(8,128)S(1)}) custom-call(f32[40,3,32,128]{3,2,1,0:T(8,128)S(1)} %copy-done, f32[2,3,32,128]{3,2,1,0:T(8,128)S(1)} %copy-done.1, ...), custom_call_target="tpu_custom_call", output_to_operand_aliasing={{3}: (5, {}), {1}: (6, {}), {2}: (7, {})} | custom-call | flops 4915200 | bytes 3932160 | tf_op jit(solution)/shard_map/pallas_call | solution.py:540
  14.0 0.1 collective-permute-start.3
  14.0 0.5 %collective-permute-start.2 = (f32[3,32,128]{2,1,0:T(8,128)S(1)}, f32[3,32,128]{2,1,0:T(8,128)S(1)}, u32[]{:S(2)}, u32[]{:S(2)}) collective-permute-start(f32[3,32,128]{2,1,0:T(8,128)S(1)} %get-tuple-element.24.my_right), channel_id=1, source_target_pairs={{0,1},{1,2},{2,3},{3,0},{4,5},{5,6},{6,7},{7,4},{8,9},{9,10},{10,1... | collective-permute-start | bytes 147464 | tf_op jit(solution)/shard_map/ppermute | solution.py:550
  14.5 2.0 %shard_map.113 = (f32[40,3,32,128]{3,2,1,0:T(8,128)S(1)}, f32[8,3,32,128]{3,2,1,0:T(8,128)S(1)}) custom-call(f32[40,3,16,128]{3,2,1,0:T(8,128)S(1)} %get-tuple-element.22.swept, f32[2,3,32,128]{3,2,1,0:T(8,128)S(1)} %copy-done.1, s32[3,32,128]{2,1,0:T(8,128)S(1)} %copy-done.2, ...), custom_call_target="tpu_custom_call", output_to_operand_aliasing={{0}: (5, {})} | custom-call | flops 4915200 | bytes 2949120 | tf_op jit(solution)/shard_map/pallas_call | solution.py:552
  16.5 0.0 collective-permute-done.3.from_right
  16.5 1.6 %collective-permute-done.2.from_left = f32[3,32,128]{2,1,0:T(8,128)S(1)} collective-permute-done((f32[3,32,128]{2,1,0:T(8,128)S(1)}, f32[3,32,128]{2,1,0:T(8,128)S(1)}, u32[]{:S(2)}, u32[]{:S(2)}) %collective-permute-start.2) | collective-permute-done | bytes 49184 | tf_op jit(solution)/shard_map/ppermute | solution.py:550
  18.1 2.3 %shard_map.114 = (f32[40,3,32,128]{3,2,1,0:T(8,128)S(1)}, f32[40,3,32,128]{3,2,1,0:T(8,128)}) custom-call(f32[8,3,32,128]{3,2,1,0:T(8,128)S(1)} %get-tuple-element.26.ready, f32[3,32,128]{2,1,0:T(8,128)S(1)} %collective-permute-done.2.from_left, f32[3,32,128]{2,1,0:T(8,128)S(1)} %collective-permute-done.3.from_right, ...), custom_call_target="tpu_custom_call", output_to_operand_aliasing={{0}: (3, {})} | custom-call | flops 1966080 | bytes 3932160 | tf_op jit(solution)/shard_map/pallas_call | solution.py:561
  (4 shorter events, 0.0 us)
Async XLA Ops:
  0.0 6.4 %copy-start = (f32[40,3,32,128]{3,2,1,0:T(8,128)S(1)}, f32[40,3,32,128]{3,2,1,0:T(8,128)}, u32[]{:S(2)}) copy-start(f32[40,3,32,128]{3,2,1,0:T(8,128)} %tracers.5) | copy-start | bytes 5898244
  0.0 6.4 %copy-start.1 = (f32[2,3,32,128]{3,2,1,0:T(8,128)S(1)}, f32[2,3,32,128]{3,2,1,0:T(8,128)}, u32[]{:S(2)}) copy-start(f32[2,3,32,128]{3,2,1,0:T(8,128)} %velocity.5) | copy-start | bytes 294916
  0.0 6.4 %copy-start.2 = (s32[3,32,128]{2,1,0:T(8,128)S(1)}, s32[3,32,128]{2,1,0:T(8,128)}, u32[]{:S(2)}) copy-start(s32[3,32,128]{2,1,0:T(8,128)} %mask.7) | copy-start | bytes 147460
  0.0 8.3 %copy-start.3 = (f32[32,128]{1,0:T(8,128)S(1)}, f32[32,128]{1,0:T(8,128)}, u32[]{:S(2)}) copy-start(f32[32,128]{1,0:T(8,128)} %sunlight.1) | copy-start | bytes 49156
  0.0 8.3 %copy-start.4 = (s32[10,26]{1,0:T(8,128)S(1)}, s32[10,26]{1,0:T(8,128)}, u32[]{:S(2)}) copy-start(s32[10,26]{1,0:T(8,128)} %palatable.1) | copy-start | bytes 3124
  0.0 8.3 %copy-start.5 = (f32[4,26]{1,0:T(4,128)S(1)}, f32[4,26]{1,0:T(4,128)}, u32[]{:S(2)}) copy-start(f32[4,26]{1,0:T(4,128)} %half_sat.1) | copy-start | bytes 1252
  0.0 8.3 %copy-start.6 = (f32[26]{0:T(128)S(1)}, f32[26]{0:T(128)}, u32[]{:S(2)}) copy-start(f32[26]{0:T(128)} %growth_max.1) | copy-start | bytes 316
  0.0 8.3 %copy-start.7 = (f32[26]{0:T(128)S(1)}, f32[26]{0:T(128)}, u32[]{:S(2)}) copy-start(f32[26]{0:T(128)} %light_half.1) | copy-start | bytes 316
  0.0 8.3 %copy-start.8 = (f32[10]{0:T(128)S(1)}, f32[10]{0:T(128)}, u32[]{:S(2)}) copy-start(f32[10]{0:T(128)} %graze_max.1) | copy-start | bytes 124
  0.1 8.3 %copy-start.9 = (f32[10]{0:T(128)S(1)}, f32[10]{0:T(128)}, u32[]{:S(2)}) copy-start(f32[10]{0:T(128)} %graze_half.1) | copy-start | bytes 124
  0.1 8.3 %copy-start.10 = (f32[4]{0:T(128)S(1)}, f32[4]{0:T(128)}, u32[]{:S(2)}) copy-start(f32[4]{0:T(128)} %stoichiometry.1) | copy-start | bytes 52
  1.3 10.3 %collective-permute-start.1 = (f32[248,128]{1,0:T(8,128)S(1)}, f32[248,128]{1,0:T(8,128)S(1)}, u32[]{:S(2)}, u32[]{:S(2)}) collective-permute-start(f32[248,128]{1,0:T(8,128)S(1)} %bitcast.9), channel_id=1, source_target_pairs={{4,0},{8,4},{12,8},{0,12},{5,1},{9,5},{13,9},{1,13},{6,2},{10,6},{... | collective-permute-start | bytes 380936 | tf_op jit(solution)/shard_map/ppermute | solution.py:501
  6.4 6.7 %collective-permute-start = (f32[248,128]{1,0:T(8,128)S(1)}, f32[248,128]{1,0:T(8,128)S(1)}, u32[]{:S(2)}, u32[]{:S(2)}) collective-permute-start(f32[248,128]{1,0:T(8,128)S(1)} %bitcast.8), channel_id=1, source_target_pairs={{0,4},{4,8},{8,12},{12,0},{1,5},{5,9},{9,13},{13,1},{2,6},{6,10},{... | collective-permute-start | bytes 380936 | tf_op jit(solution)/shard_map/ppermute | solution.py:500
  14.0 2.5 %collective-permute-start.3 = (f32[3,32,128]{2,1,0:T(8,128)S(1)}, f32[3,32,128]{2,1,0:T(8,128)S(1)}, u32[]{:S(2)}, u32[]{:S(2)}) collective-permute-start(f32[3,32,128]{2,1,0:T(8,128)S(1)} %get-tuple-element.23.my_left), channel_id=1, source_target_pairs={{1,0},{2,1},{3,2},{0,3},{5,4},{6,5},{7,6},{4,7},{9,8},{10,9},{11,1... | collective-permute-start | bytes 147464 | tf_op jit(solution)/shard_map/ppermute | solution.py:551
  14.0 4.1 %collective-permute-start.2 = (f32[3,32,128]{2,1,0:T(8,128)S(1)}, f32[3,32,128]{2,1,0:T(8,128)S(1)}, u32[]{:S(2)}, u32[]{:S(2)}) collective-permute-start(f32[3,32,128]{2,1,0:T(8,128)S(1)} %get-tuple-element.24.my_right), channel_id=1, source_target_pairs={{0,1},{1,2},{2,3},{3,0},{4,5},{5,6},{6,7},{7,4},{8,9},{9,10},{10,1... | collective-permute-start | bytes 147464 | tf_op jit(solution)/shard_map/ppermute | solution.py:550

commit v5 on v4

--- a/solution.py
+++ b/solution.py
@@ -65,15 +65,16 @@
 
     def picks(shape, dim, period):
         index = lax.broadcasted_iota(jnp.int32, shape, dim)
+        index = jnp.where(index < period, index, index - period)
         other = lax.broadcasted_iota(jnp.int32, shape, 1 - dim)
-        return ((index % period) // 8 == other).astype(f32).astype(bf16)
+        return jnp.where((index >> 3) == other, 1.0, 0.0).astype(bf16)
 
     def spread(left, middle, right, transposed):
         dims = (((1,), (1 if transposed else 0,)), ((), ()))
         part = lax.dot_general(left, middle, dims, preferred_element_type=f32).astype(bf16)
         whole = jnp.dot(part, right, preferred_element_type=f32)
-        row = lax.broadcasted_iota(jnp.int32, whole.shape, 0) % 8
-        col = lax.broadcasted_iota(jnp.int32, whole.shape, 1) % 8
+        row = lax.broadcasted_iota(jnp.int32, whole.shape, 0) & 7
+        col = lax.broadcasted_iota(jnp.int32, whole.shape, 1) & 7
         return jnp.where(row == col, whole, 0.0).astype(bf16)
 
     eats = palatable[...].astype(f32).astype(bf16)
@@ -249,6 +250,22 @@
     )
 
 
+def swaps(size):
+    return size % 2 == 0
+
+
+def first_is_right():
+    size = lax.axis_size("ty")
+    if not swaps(size):
+        return True, True
+    even = lax.axis_index("ty") % 2 == 0
+    return even, jnp.logical_not(even)
+
+
+def pick(choice, a, b):
+    return (a if choice else b) if isinstance(choice, bool) else jnp.where(choice, a, b)
+
+
 class Packer:
     def __init__(self, count, velocity, mask, level, here):
         wet = mask[level, here].astype(jnp.float32)
@@ -263,7 +280,7 @@
         self.left = jnp.where(self.slot == t + 1, turned, self.left)
 
 
-def interior(tracers, velocity, mask, partial, pack_left, pack_right, weights):
+def interior(tracers, velocity, mask, partial, pack_first, pack_second, weights):
     count, levels, length, lanes = tracers.shape
     zero = jnp.zeros((1, lanes), jnp.float32)
 
@@ -286,8 +303,9 @@
                 packer.add(t, value)
                 later.put(partial, (t, level, here), sweep_across(value, columns))
             later.flush()
-            pack_right[level, here] = packer.right
-            pack_left[level, here] = packer.left
+            to_right, _ = first_is_right()
+            pack_first[level, here] = pick(to_right, packer.right, packer.left)
+            pack_second[level, here] = pick(to_right, packer.left, packer.right)
             return carry
 
         for t in range(count):
@@ -299,14 +317,14 @@
 
 
 def border(
-    tracers, velocity, mask, before, after, partial, left_in, right_in, swept, pack_left, pack_right, through
+    tracers, velocity, mask, before, after, partial, first_in, second_in, swept, pack_first, pack_second, through
 ):
     count, levels, length, lanes = tracers.shape
     row8 = lax.broadcasted_iota(jnp.int32, (8, lanes), 0)
 
     def level_step(level, carry):
-        pick = lambda ref, field: ref[pl.ds(2 * (count * levels + level) + field, 1)]
-        weights = row_weights(velocity, mask, level, pick(before, 1), pick(after, 1), pick(after, 0))
+        row = lambda ref, field: ref[pl.ds(2 * (count * levels + level) + field, 1)]
+        weights = row_weights(velocity, mask, level, row(before, 1), row(after, 1), row(after, 0))
         for side, first in enumerate((0, length - 8)):
             here = pl.ds(first, 8)
             wm2, wm1, w0, wp1, wp2 = [w[first : first + 8] for w in weights]
@@ -340,8 +358,9 @@
                 later.put(swept, (t, level, pl.ds(8 * side, 8)), value)
                 packer.add(t, value)
             later.flush()
-            pack_right[level, here] = packer.right
-            pack_left[level, here] = packer.left
+            to_right, _ = first_is_right()
+            pack_first[level, here] = pick(to_right, packer.right, packer.left)
+            pack_second[level, here] = pick(to_right, packer.left, packer.right)
         return carry
 
     lax.fori_loop(0, levels, level_step, 0)
@@ -350,7 +369,7 @@
 PREPARED = 8
 
 
-def border_across(swept, velocity, mask, my_left, my_right, _, partial, ready):
+def border_across(swept, velocity, mask, my_first, my_second, _, partial, ready):
     count, levels, _, lanes = swept.shape
     length = mask.shape[1]
     place, size = lax.axis_index("ty"), lax.axis_size("ty")
@@ -377,7 +396,9 @@
             wet = mask[level, here].astype(jnp.float32)
             flow = velocity[1, level, here]
             opened = flow * wet * pltpu.roll(wet, 1, 1)
-            left, right = my_left[level, here], my_right[level, here]
+            to_right, _ = first_is_right()
+            first, second = my_first[level, here], my_second[level, here]
+            left, right = pick(to_right, second, first), pick(to_right, first, second)
             arrays = (
                 col(flow * wet, 0) * has_left,
                 col(wet, lanes - 1) * has_right,
@@ -395,7 +416,7 @@
     lax.fori_loop(0, levels, prepare, 0)
 
 
-def finish(ready, from_left, from_right, _, done, updated, even, odd, sems):
+def finish(ready, first, second, _, done, updated, even, odd, sems):
     count, levels, length, lanes = done.shape
     blocks = length // 8
     lane = lax.broadcasted_iota(jnp.int32, (8, lanes), 1)
@@ -409,7 +430,10 @@
             open_low, open_high, a1, e127, s0, s1, s127, s126 = (
                 ready[n, level, here] for n in range(PREPARED)
             )
-            left, right = from_left[level, here], pltpu.roll(from_right[level, here], lanes - 4, 1)
+            _, of_left = first_is_right()
+            one, two = first[level, here], second[level, here]
+            left = pick(of_left, one, two)
+            right = pltpu.roll(pick(of_left, two, one), lanes - 4, 1)
             u0 = open_low * col(left, 2 * count + 1)
             u128 = open_high * col(right, 2 * count - 2)
             a0, b0, d0, e0 = face_terms(u0)
@@ -503,7 +527,7 @@
     held, flow, mask = in_vmem(tracers), in_vmem(velocity), in_vmem(land_mask)
     field = pltpu.VMEM(tracers.shape, f32)
     columns = pltpu.VMEM((levels, length, lanes), f32)
-    partial, pack_left, pack_right = call(
+    partial, pack_first, pack_second = call(
         interior,
         (field, columns, columns),
         [VMEM] * 3,
@@ -537,7 +561,7 @@
         stoichiometry,
         partial,
     )
-    swept, pack_left, pack_right, partial = call(
+    swept, pack_first, pack_second, partial = call(
         border,
         (pltpu.VMEM((count, levels, 16, lanes), f32), columns, columns, field),
         [VMEM] * 5 + [ANY] * 3,
@@ -546,9 +570,11 @@
         bytes_accessed=8 * cells,
         limit=2 << 20,
         input_output_aliases={5: 3, 6: 1, 7: 2},
-    )(held, flow, mask, in_vmem(before), in_vmem(after), partial, pack_left, pack_right)
-    from_left = lax.ppermute(pack_right, "ty", up(ty))
-    from_right = lax.ppermute(pack_left, "ty", down(ty))
+    )(held, flow, mask, in_vmem(before), in_vmem(after), partial, pack_first, pack_second)
+    pair = lambda n, odd: [p for i in range(odd, n, 2) for p in ((i, (i + 1) % n), ((i + 1) % n, i))]
+    turns = (pair(ty, 0), pair(ty, 1)) if swaps(ty) else (up(ty), down(ty))
+    from_first = lax.ppermute(pack_first, "ty", turns[0])
+    from_second = lax.ppermute(pack_second, "ty", turns[1])
     partial, ready = call(
         border_across,
         (field, pltpu.VMEM((PREPARED, levels, length, lanes), f32)),
@@ -557,7 +583,7 @@
         bytes_accessed=6 * cells,
         limit=2 << 20,
         input_output_aliases={5: 0},
-    )(swept, flow, mask, pack_left, pack_right, partial)
+    )(swept, flow, mask, pack_first, pack_second, partial)
     return call(
         finish,
         (field, jax.ShapeDtypeStruct(tracers.shape, f32)),
@@ -572,7 +598,7 @@
         flops=4 * cells,
         bytes_accessed=8 * cells,
         limit=2 << 20,
-    )(ready, in_vmem(from_left), in_vmem(from_right), partial)[1]
+    )(ready, in_vmem(from_first), in_vmem(from_second), partial)[1]
 
 
 def solution(mesh):

time: 20.5 us -> 20.1 us (0.980)
  waiting for transfers between devices: 3.16 us -> 1.61 us
  starting transfers between devices: 5.7 us -> 6.81 us
    ppermute x2, waiting for transfers between devices: 1.6 us -> 0.01 us  [the longest x1 0.01 us: shards(): from_second = lax.ppermute(pack_second, 'ty', turns[1])]
    ppermute x2, starting transfers between devices: 0.55 us -> 1.66 us  [the longest x1 1.59 us: shards(): from_second = lax.ppermute(pack_second, 'ty', turns[1])]
  transfers between devices with their start and end apart: 4 -> 4, of which waited for: 2 -> 1; matrix products, arithmetic and copies ran while one was open for 0% -> 0% of each run, Pallas kernels for 34% -> 35%
where the time goes in v5:
time: 20.1 us; the launch traced here: 19.9 us
  Pallas kernels  11.3 us (56%)
  starting transfers between devices  6.81 us (34%)
  waiting for transfers between devices  1.61 us (8%)
    ppermute x1, starting transfers between devices, shards(): after = lax.ppermute(first, 'tx', down(tx))  5.14 us
    pallas_call x1, Pallas kernels, shards(): call(ecology, field, [VMEM] * 4 + [SMEM] * 6 + [VMEM], scratch=[pltpu.VME...  3.16 us
    pallas_call x1, Pallas kernels, shards(): call(finish, (field, jax.ShapeDtypeStruct(tracers.shape, f32)), [VMEM] *...  2.29 us
    pallas_call x1, Pallas kernels, shards(): call(border_across, (field, pltpu.VMEM((PREPARED, levels, length, lanes),...  1.97 us
    pallas_call x1, Pallas kernels, shards(): call(interior, (field, columns, columns), [VMEM] * 3, scratch=[pltpu.VMEM...  1.83 us
    ppermute x1, waiting for transfers between devices, shards(): before = lax.ppermute(last, 'tx', up(tx))  1.61 us
    ppermute x1, starting transfers between devices, shards(): from_second = lax.ppermute(pack_second, 'ty', turns[1])  1.59 us
    pallas_call x1, Pallas kernels, shards(): call(pack_rows, (row_message, row_message), [HBM, HBM, HBM], scratch=[plt...  1.17 us
  transfers between devices with their start and end apart: 4, of which 1 were waited for; matrix products, arithmetic and copies ran while one was open for 0% of the time, Pallas kernels for 35%

profile of v5, /device:TPU:0, one launch (start us, length us, event | category | flops | bytes accessed | tf_op | source)
XLA Modules:
  0.0 19.9 jit_solution(17252825152352577126)
XLA Ops:
  0.0 0.0 copy-start
  0.0 0.0 copy-start.5
  0.0 0.0 copy-start.6
  0.0 0.0 copy-start.7
  0.0 0.0 copy-start.8
  0.1 0.0 copy-start.9
  0.1 0.0 copy-start.10
  0.1 1.2 %shard_map.109 = (f32[124,2,1,128]{3,2,1,0:T(1,128)S(1)}, f32[124,2,1,128]{3,2,1,0:T(1,128)S(1)}) custom-call(f32[120,32,1,128]{3,2,1,0:T(1,128)} %bitcast.5, f32[2,3,32,1,128]{4,3,2,1,0:T(1,128)} %bitcast.6, s32[3,32,1,128]{3,2,1,0:T(1,128)} %bitcast.7), custom_call_target="tpu_custom_call" | custom-call | bytes 126976 | tf_op jit(solution)/shard_map/pallas_call | solution.py:511
  1.3 5.1 %collective-permute-start.1 = (f32[248,128]{1,0:T(8,128)S(1)}, f32[248,128]{1,0:T(8,128)S(1)}, u32[]{:S(2)}, u32[]{:S(2)}) collective-permute-start(f32[248,128]{1,0:T(8,128)S(1)} %bitcast.9), channel_id=1, source_target_pairs={{4,0},{8,4},{12,8},{0,12},{5,1},{9,5},{13,9},{1,13},{6,2},{10,6},{... | collective-permute-start | bytes 380936 | tf_op jit(solution)/shard_map/ppermute | solution.py:525
  6.4 0.0 collective-permute-start
  6.4 0.0 copy-done
  6.4 0.0 copy-done.1
  6.4 0.0 copy-done.2
  6.4 1.8 %shard_map.110 = (f32[40,3,32,128]{3,2,1,0:T(8,128)S(1)}, f32[3,32,128]{2,1,0:T(8,128)S(1)}, f32[3,32,128]{2,1,0:T(8,128)S(1)}) custom-call(f32[40,3,32,128]{3,2,1,0:T(8,128)S(1)} %copy-done, f32[2,3,32,128]{3,2,1,0:T(8,128)S(1)} %copy-done.1, s32[3,32,128]{2,1,0:T(8,128)S(1)} %copy-done.2), custom_call_target="tpu_custom_call" | custom-call | flops 9830400 | bytes 3932160 | tf_op jit(solution)/shard_map/pallas_call | solution.py:530
  8.3 0.0 copy-done.3
  8.3 0.0 copy-done.4
  8.3 0.0 copy-done.5
  8.3 0.0 copy-done.6
  8.3 0.0 copy-done.7
  8.3 0.0 copy-done.8
  8.3 0.0 copy-done.9
  8.3 0.0 copy-done.10
  8.3 3.2 %shard_map.111.partial = f32[40,3,32,128]{3,2,1,0:T(8,128)S(1)} custom-call(f32[40,3,32,128]{3,2,1,0:T(8,128)S(1)} %copy-done, s32[3,32,128]{2,1,0:T(8,128)S(1)} %copy-done.2, f32[32,128]{1,0:T(8,128)S(1)} %copy-done.3, s32[10,26]{1,0:T(8,128)S(1)} %copy-done.4, f32[26]{0:T(128)S(1)} %copy-done.6, ...), custom_call_target="tpu_custom_call", output_to_operand_aliasing={{}: (10, {})} | custom-call | flops 19660800 | bytes 3932160 | tf_op jit(solution)/shard_map/pallas_call | solution.py:539
  11.5 0.0 collective-permute-done.1.after
  11.5 1.6 %collective-permute-done.before = f32[248,128]{1,0:T(8,128)S(1)} collective-permute-done((f32[248,128]{1,0:T(8,128)S(1)}, f32[248,128]{1,0:T(8,128)S(1)}, u32[]{:S(2)}, u32[]{:S(2)}) %collective-permute-start) | collective-permute-done | bytes 127008 | tf_op jit(solution)/shard_map/ppermute | solution.py:524
  13.1 0.8 %shard_map.112 = (f32[40,3,16,128]{3,2,1,0:T(8,128)S(1)}, f32[3,32,128]{2,1,0:T(8,128)S(1)}, f32[3,32,128]{2,1,0:T(8,128)S(1)}, f32[40,3,32,128]{3,2,1,0:T(8,128)S(1)}) custom-call(f32[40,3,32,128]{3,2,1,0:T(8,128)S(1)} %copy-done, f32[2,3,32,128]{3,2,1,0:T(8,128)S(1)} %copy-done.1, ...), custom_call_target="tpu_custom_call", output_to_operand_aliasing={{3}: (5, {}), {1}: (6, {}), {2}: (7, {})} | custom-call | flops 4915200 | bytes 3932160 | tf_op jit(solution)/shard_map/pallas_call | solution.py:564
  14.0 0.1 collective-permute-start.2
  14.0 1.6 %collective-permute-start.3 = (f32[3,32,128]{2,1,0:T(8,128)S(1)}, f32[3,32,128]{2,1,0:T(8,128)S(1)}, u32[]{:S(2)}, u32[]{:S(2)}) collective-permute-start(f32[3,32,128]{2,1,0:T(8,128)S(1)} %get-tuple-element.24.my_second), channel_id=1, source_target_pairs={{1,2},{2,1},{3,0},{0,3},{5,6},{6,5},{7,4},{4,7},{9,10},{10,9},{11,... | collective-permute-start | bytes 147464 | tf_op jit(solution)/shard_map/ppermute | solution.py:577
  15.6 2.0 %shard_map.113 = (f32[40,3,32,128]{3,2,1,0:T(8,128)S(1)}, f32[8,3,32,128]{3,2,1,0:T(8,128)S(1)}) custom-call(f32[40,3,16,128]{3,2,1,0:T(8,128)S(1)} %get-tuple-element.22.swept, f32[2,3,32,128]{3,2,1,0:T(8,128)S(1)} %copy-done.1, s32[3,32,128]{2,1,0:T(8,128)S(1)} %copy-done.2, ...), custom_call_target="tpu_custom_call", output_to_operand_aliasing={{0}: (5, {})} | custom-call | flops 4915200 | bytes 2949120 | tf_op jit(solution)/shard_map/pallas_call | solution.py:578
  17.6 0.0 collective-permute-done.2.first
  17.6 0.0 collective-permute-done.3.second
  17.6 2.3 %shard_map.114 = (f32[40,3,32,128]{3,2,1,0:T(8,128)S(1)}, f32[40,3,32,128]{3,2,1,0:T(8,128)}) custom-call(f32[8,3,32,128]{3,2,1,0:T(8,128)S(1)} %get-tuple-element.26.ready, f32[3,32,128]{2,1,0:T(8,128)S(1)} %collective-permute-done.2.first, f32[3,32,128]{2,1,0:T(8,128)S(1)} %collective-permute-done.3.second, ...), custom_call_target="tpu_custom_call", output_to_operand_aliasing={{0}: (3, {})} | custom-call | flops 1966080 | bytes 3932160 | tf_op jit(solution)/shard_map/pallas_call | solution.py:587
  (4 shorter events, 0.0 us)
Async XLA Ops:
  0.0 6.4 %copy-start = (f32[40,3,32,128]{3,2,1,0:T(8,128)S(1)}, f32[40,3,32,128]{3,2,1,0:T(8,128)}, u32[]{:S(2)}) copy-start(f32[40,3,32,128]{3,2,1,0:T(8,128)} %tracers.5) | copy-start | bytes 5898244
  0.0 6.4 %copy-start.1 = (f32[2,3,32,128]{3,2,1,0:T(8,128)S(1)}, f32[2,3,32,128]{3,2,1,0:T(8,128)}, u32[]{:S(2)}) copy-start(f32[2,3,32,128]{3,2,1,0:T(8,128)} %velocity.5) | copy-start | bytes 294916
  0.0 6.4 %copy-start.2 = (s32[3,32,128]{2,1,0:T(8,128)S(1)}, s32[3,32,128]{2,1,0:T(8,128)}, u32[]{:S(2)}) copy-start(s32[3,32,128]{2,1,0:T(8,128)} %mask.7) | copy-start | bytes 147460
  0.0 8.3 %copy-start.3 = (f32[32,128]{1,0:T(8,128)S(1)}, f32[32,128]{1,0:T(8,128)}, u32[]{:S(2)}) copy-start(f32[32,128]{1,0:T(8,128)} %sunlight.1) | copy-start | bytes 49156
  0.0 8.3 %copy-start.4 = (s32[10,26]{1,0:T(8,128)S(1)}, s32[10,26]{1,0:T(8,128)}, u32[]{:S(2)}) copy-start(s32[10,26]{1,0:T(8,128)} %palatable.1) | copy-start | bytes 3124
  0.0 8.3 %copy-start.5 = (f32[4,26]{1,0:T(4,128)S(1)}, f32[4,26]{1,0:T(4,128)}, u32[]{:S(2)}) copy-start(f32[4,26]{1,0:T(4,128)} %half_sat.1) | copy-start | bytes 1252
  0.0 8.3 %copy-start.6 = (f32[26]{0:T(128)S(1)}, f32[26]{0:T(128)}, u32[]{:S(2)}) copy-start(f32[26]{0:T(128)} %growth_max.1) | copy-start | bytes 316
  0.0 8.3 %copy-start.7 = (f32[26]{0:T(128)S(1)}, f32[26]{0:T(128)}, u32[]{:S(2)}) copy-start(f32[26]{0:T(128)} %light_half.1) | copy-start | bytes 316
  0.0 8.3 %copy-start.8 = (f32[10]{0:T(128)S(1)}, f32[10]{0:T(128)}, u32[]{:S(2)}) copy-start(f32[10]{0:T(128)} %graze_max.1) | copy-start | bytes 124
  0.1 8.3 %copy-start.9 = (f32[10]{0:T(128)S(1)}, f32[10]{0:T(128)}, u32[]{:S(2)}) copy-start(f32[10]{0:T(128)} %graze_half.1) | copy-start | bytes 124
  0.1 8.3 %copy-start.10 = (f32[4]{0:T(128)S(1)}, f32[4]{0:T(128)}, u32[]{:S(2)}) copy-start(f32[4]{0:T(128)} %stoichiometry.1) | copy-start | bytes 52
  1.3 10.3 %collective-permute-start.1 = (f32[248,128]{1,0:T(8,128)S(1)}, f32[248,128]{1,0:T(8,128)S(1)}, u32[]{:S(2)}, u32[]{:S(2)}) collective-permute-start(f32[248,128]{1,0:T(8,128)S(1)} %bitcast.9), channel_id=1, source_target_pairs={{4,0},{8,4},{12,8},{0,12},{5,1},{9,5},{13,9},{1,13},{6,2},{10,6},{... | collective-permute-start | bytes 380936 | tf_op jit(solution)/shard_map/ppermute | solution.py:525
  6.4 6.7 %collective-permute-start = (f32[248,128]{1,0:T(8,128)S(1)}, f32[248,128]{1,0:T(8,128)S(1)}, u32[]{:S(2)}, u32[]{:S(2)}) collective-permute-start(f32[248,128]{1,0:T(8,128)S(1)} %bitcast.8), channel_id=1, source_target_pairs={{0,4},{4,8},{8,12},{12,0},{1,5},{5,9},{9,13},{13,1},{2,6},{6,10},{... | collective-permute-start | bytes 380936 | tf_op jit(solution)/shard_map/ppermute | solution.py:524
  14.0 3.6 %collective-permute-start.2 = (f32[3,32,128]{2,1,0:T(8,128)S(1)}, f32[3,32,128]{2,1,0:T(8,128)S(1)}, u32[]{:S(2)}, u32[]{:S(2)}) collective-permute-start(f32[3,32,128]{2,1,0:T(8,128)S(1)} %get-tuple-element.23.my_first), channel_id=1, source_target_pairs={{0,1},{1,0},{2,3},{3,2},{4,5},{5,4},{6,7},{7,6},{8,9},{9,8},{10,11... | collective-permute-start | bytes 147464 | tf_op jit(solution)/shard_map/ppermute | solution.py:576
  14.0 3.6 %collective-permute-start.3 = (f32[3,32,128]{2,1,0:T(8,128)S(1)}, f32[3,32,128]{2,1,0:T(8,128)S(1)}, u32[]{:S(2)}, u32[]{:S(2)}) collective-permute-start(f32[3,32,128]{2,1,0:T(8,128)S(1)} %get-tuple-element.24.my_second), channel_id=1, source_target_pairs={{1,2},{2,1},{3,0},{0,3},{5,6},{6,5},{7,4},{4,7},{9,10},{10,9},{11,... | collective-permute-start | bytes 147464 | tf_op jit(solution)/shard_map/ppermute | solution.py:577

commit v6 on v5

--- a/solution.py
+++ b/solution.py
@@ -280,54 +280,66 @@
         self.left = jnp.where(self.slot == t + 1, turned, self.left)
 
 
-def interior(tracers, velocity, mask, partial, pack_first, pack_second, weights):
+def interior(
+    tracers, velocity, mask, partial, pack_first, pack_second, columns, weights
+):
     count, levels, length, lanes = tracers.shape
     zero = jnp.zeros((1, lanes), jnp.float32)
-
-    def level_step(level, carry):
+    for level in range(levels):
         for n, w in enumerate(row_weights(velocity, mask, level, zero, zero, zero)):
-            weights[n] = w
-
-        def block_step(block, carry):
-            begin = pl.multiple_of(8 * block, 8)
-            here = pl.ds(begin, 8)
-            wm2, wm1, w0, wp1, wp2 = [weights[n, here] for n in range(5)]
-            columns = column_weights(velocity, mask, level, here)
-            packer = Packer(count, velocity, mask, level, here)
-            later = Deferred(DEPTH)
-            for t in range(count):
-                at = lambda offset: tracers[t, level, pl.ds(begin + offset, 8)]
-                value = (
-                    w0 * at(0) + (wm1 * at(-1) + wm2 * at(-2)) + (wp1 * at(1) + wp2 * at(2))
-                )
-                packer.add(t, value)
-                later.put(partial, (t, level, here), sweep_across(value, columns))
-            later.flush()
-            to_right, _ = first_is_right()
-            pack_first[level, here] = pick(to_right, packer.right, packer.left)
-            pack_second[level, here] = pick(to_right, packer.left, packer.right)
-            return carry
-
+            weights[n, level] = w
+        for block in range(length // 8):
+            here = pl.ds(8 * block, 8)
+            for n, w in enumerate(column_weights(velocity, mask, level, here)):
+                columns[n, level, here] = w
+    to_right, _ = first_is_right()
+    blocks = length // 8 - 2
+
+    def step(index, carry):
+        level = index // blocks
+        begin = pl.multiple_of(8 * (1 + index % blocks), 8)
+        here = pl.ds(begin, 8)
+        wm2, wm1, w0, wp1, wp2 = [weights[n, level, here] for n in range(5)]
+        sideways = [columns[n, level, here] for n in range(5)]
+        packer = Packer(count, velocity, mask, level, here)
+        later = Deferred(DEPTH)
+        for t in range(count):
+            at = lambda offset: tracers[t, level, pl.ds(begin + offset, 8)]
+            value = w0 * at(0) + (wm1 * at(-1) + wm2 * at(-2)) + (wp1 * at(1) + wp2 * at(2))
+            packer.add(t, value)
+            later.put(partial, (t, level, here), sweep_across(value, sideways))
+        later.flush()
+        pack_first[level, here] = pick(to_right, packer.right, packer.left)
+        pack_second[level, here] = pick(to_right, packer.left, packer.right)
+        return carry
+
+    def clear(level, carry):
         for t in range(count):
             partial[t, level, 0:8] = jnp.zeros((8, lanes), jnp.float32)
             partial[t, level, length - 8 : length] = jnp.zeros((8, lanes), jnp.float32)
-        return lax.fori_loop(1, length // 8 - 1, block_step, carry)
-
-    lax.fori_loop(0, levels, level_step, 0)
+        return carry
+
+    lax.fori_loop(0, levels, clear, 0)
+    lax.fori_loop(0, levels * blocks, step, 0)
 
 
 def border(
-    tracers, velocity, mask, before, after, partial, first_in, second_in, swept, pack_first, pack_second, through
+    tracers, velocity, mask, before, after, partial, first_in, second_in, swept, pack_first, pack_second, through, weights
 ):
     count, levels, length, lanes = tracers.shape
     row8 = lax.broadcasted_iota(jnp.int32, (8, lanes), 0)
 
+    for level in range(levels):
+        row = lambda ref, field: ref[pl.ds(2 * (count * levels + level) + field, 1)]
+        for n, w in enumerate(
+            row_weights(velocity, mask, level, row(before, 1), row(after, 1), row(after, 0))
+        ):
+            weights[n, level] = w
+
     def level_step(level, carry):
-        row = lambda ref, field: ref[pl.ds(2 * (count * levels + level) + field, 1)]
-        weights = row_weights(velocity, mask, level, row(before, 1), row(after, 1), row(after, 0))
         for side, first in enumerate((0, length - 8)):
             here = pl.ds(first, 8)
-            wm2, wm1, w0, wp1, wp2 = [w[first : first + 8] for w in weights]
+            wm2, wm1, w0, wp1, wp2 = [weights[n, level, here] for n in range(5)]
             if side == 0:
                 z2, z1 = jnp.where(row8 < 2, wm2, 0.0), jnp.where(row8 < 1, wm1, 0.0)
                 wm2, wm1 = jnp.where(row8 < 2, 0.0, wm2), jnp.where(row8 < 1, 0.0, wm1)
@@ -369,7 +381,7 @@
 PREPARED = 8
 
 
-def border_across(swept, velocity, mask, my_first, my_second, _, partial, ready):
+def border_across(swept, velocity, mask, columns, my_first, my_second, _, partial, ready):
     count, levels, _, lanes = swept.shape
     length = mask.shape[1]
     place, size = lax.axis_index("ty"), lax.axis_size("ty")
@@ -380,11 +392,11 @@
     def step(index, carry):
         level, side = index // 2, index % 2
         here = pl.ds(pl.multiple_of(side * (length - 8), 8), 8)
-        columns = column_weights(velocity, mask, level, here)
+        sideways = [columns[n, level, here] for n in range(5)]
         later = Deferred(DEPTH)
         for t in range(count):
             value = swept[t, level, pl.ds(pl.multiple_of(8 * side, 8), 8)]
-            later.put(partial, (t, level, here), partial[t, level, here] + sweep_across(value, columns))
+            later.put(partial, (t, level, here), partial[t, level, here] + sweep_across(value, sideways))
         later.flush()
         return carry
 
@@ -413,7 +425,8 @@
                 ready[n, level, here] = array
         return carry
 
-    lax.fori_loop(0, levels, prepare, 0)
+    for level in range(levels):
+        prepare(level, 0)
 
 
 def finish(ready, first, second, _, done, updated, even, odd, sems):
@@ -452,7 +465,8 @@
             odd[level, here] = jnp.where(slot_odd, low, high)
         return carry
 
-    lax.fori_loop(0, levels, level_step, 0)
+    for level in range(levels):
+        level_step(level, 0)
     outer = (lane < 2) | (lane > lanes - 3)
     step = 8 if count % 8 == 0 else 2
 
@@ -464,12 +478,11 @@
         start = chunk * step
         turns = [jnp.where(start + n == 0, 0, lanes - 2 * (start + n)) for n in range(step)]
         later = Deferred(2 * DEPTH)
-        for level in range(levels):
-            for block in range(blocks):
-                here = pl.ds(8 * block, 8)
-                packs = (even[level, here], odd[level, here])
-                for n in range(step):
-                    edge = pltpu.roll(packs[n % 2], turns[n], 1)
+        for n in range(step):
+            for level in range(levels):
+                for block in range(blocks):
+                    here = pl.ds(8 * block, 8)
+                    edge = pltpu.roll((even, odd)[n % 2][level, here], turns[n], 1)
                     at = (start + n, level, here)
                     later.put(done, at, done[at] + jnp.where(outer, edge, 0.0))
         later.flush()
@@ -527,11 +540,12 @@
     held, flow, mask = in_vmem(tracers), in_vmem(velocity), in_vmem(land_mask)
     field = pltpu.VMEM(tracers.shape, f32)
     columns = pltpu.VMEM((levels, length, lanes), f32)
-    partial, pack_first, pack_second = call(
+    stencils = pltpu.VMEM((5, levels, length, lanes), f32)
+    partial, pack_first, pack_second, sideways = call(
         interior,
-        (field, columns, columns),
+        (field, columns, columns, stencils),
         [VMEM] * 3,
-        scratch=[pltpu.VMEM((5, length, lanes), f32)],
+        scratch=[stencils],
         flops=20 * cells,
         bytes_accessed=8 * cells,
         limit=2 << 20,
@@ -566,6 +580,7 @@
         (pltpu.VMEM((count, levels, 16, lanes), f32), columns, columns, field),
         [VMEM] * 5 + [ANY] * 3,
         out_specs=[VMEM] * 3 + [ANY],
+        scratch=[stencils],
         flops=10 * cells,
         bytes_accessed=8 * cells,
         limit=2 << 20,
@@ -578,12 +593,12 @@
     partial, ready = call(
         border_across,
         (field, pltpu.VMEM((PREPARED, levels, length, lanes), f32)),
-        [VMEM] * 6,
+        [VMEM] * 7,
         flops=10 * cells,
         bytes_accessed=6 * cells,
         limit=2 << 20,
-        input_output_aliases={5: 0},
-    )(swept, flow, mask, pack_first, pack_second, partial)
+        input_output_aliases={6: 0},
+    )(swept, flow, mask, sideways, pack_first, pack_second, partial)
     return call(
         finish,
         (field, jax.ShapeDtypeStruct(tracers.shape, f32)),

time: 20.1 us -> 19.8 us (0.985)
  Pallas kernels: 11.3 us -> 10.9 us
    pallas_call x1, Pallas kernels: 2.29 us -> 1.97 us  [shards(): call(finish, (field, jax.ShapeDtypeStruct(tracers.shape, f32)), [VMEM] *...]
    ppermute x1, waiting for transfers between devices: 0.01 us -> 0.25 us  [shards(): from_second = lax.ppermute(pack_second, 'ty', turns[1])]
    pallas_call x1, Pallas kernels: 1.97 us -> 1.72 us  [shards(): call(border_across, (field, pltpu.VMEM((PREPARED, levels, length, lanes),...]
  transfers between devices with their start and end apart: 4 -> 4, of which waited for: 1 -> 2; matrix products, arithmetic and copies ran while one was open for 0% -> 0% of each run, Pallas kernels for 35% -> 35%
where the time goes in v6:
time: 19.8 us; the launch traced here: 19.6 us
  Pallas kernels  10.9 us (55%)
  starting transfers between devices  6.81 us (34%)
  waiting for transfers between devices  1.71 us (9%)
    ppermute x1, starting transfers between devices, shards(): after = lax.ppermute(first, 'tx', down(tx))  5.14 us
    pallas_call x1, Pallas kernels, shards(): call(ecology, field, [VMEM] * 4 + [SMEM] * 6 + [VMEM], scratch=[pltpu.VME...  3.15 us
    pallas_call x1, Pallas kernels, shards(): call(interior, (field, columns, columns, stencils), [VMEM] * 3, scratch=[...  1.99 us
    pallas_call x1, Pallas kernels, shards(): call(finish, (field, jax.ShapeDtypeStruct(tracers.shape, f32)), [VMEM] *...  1.97 us
    pallas_call x1, Pallas kernels, shards(): call(border_across, (field, pltpu.VMEM((PREPARED, levels, length, lanes),...  1.72 us
    ppermute x1, starting transfers between devices, shards(): from_second = lax.ppermute(pack_second, 'ty', turns[1])  1.59 us
    ppermute x1, waiting for transfers between devices, shards(): before = lax.ppermute(last, 'tx', up(tx))  1.45 us
    pallas_call x1, Pallas kernels, shards(): call(pack_rows, (row_message, row_message), [HBM, HBM, HBM], scratch=[plt...  1.17 us
  transfers between devices with their start and end apart: 4, of which 2 were waited for; matrix products, arithmetic and copies ran while one was open for 0% of the time, Pallas kernels for 35%

profile of v6, /device:TPU:0, one launch (start us, length us, event | category | flops | bytes accessed | tf_op | source)
XLA Modules:
  0.0 19.6 jit_solution(2202688684716984780)
XLA Ops:
  0.0 0.0 copy-start
  0.0 0.0 copy-start.5
  0.0 0.0 copy-start.6
  0.0 0.0 copy-start.7
  0.0 0.0 copy-start.8
  0.1 0.0 copy-start.9
  0.1 0.0 copy-start.10
  0.1 1.2 %shard_map.109 = (f32[124,2,1,128]{3,2,1,0:T(1,128)S(1)}, f32[124,2,1,128]{3,2,1,0:T(1,128)S(1)}) custom-call(f32[120,32,1,128]{3,2,1,0:T(1,128)} %bitcast.5, f32[2,3,32,1,128]{4,3,2,1,0:T(1,128)} %bitcast.6, s32[3,32,1,128]{3,2,1,0:T(1,128)} %bitcast.7), custom_call_target="tpu_custom_call" | custom-call | bytes 126976 | tf_op jit(solution)/shard_map/pallas_call | solution.py:524
  1.3 5.1 %collective-permute-start.1 = (f32[248,128]{1,0:T(8,128)S(1)}, f32[248,128]{1,0:T(8,128)S(1)}, u32[]{:S(2)}, u32[]{:S(2)}) collective-permute-start(f32[248,128]{1,0:T(8,128)S(1)} %bitcast.9), channel_id=1, source_target_pairs={{4,0},{8,4},{12,8},{0,12},{5,1},{9,5},{13,9},{1,13},{6,2},{10,6},{... | collective-permute-start | bytes 380936 | tf_op jit(solution)/shard_map/ppermute | solution.py:538
  6.4 0.0 collective-permute-start
  6.4 0.0 copy-done
  6.4 0.0 copy-done.1
  6.4 0.0 copy-done.2
  6.4 2.0 %shard_map.110 = (f32[40,3,32,128]{3,2,1,0:T(8,128)S(1)}, f32[3,32,128]{2,1,0:T(8,128)S(1)}, f32[3,32,128]{2,1,0:T(8,128)S(1)}, f32[5,3,32,128]{3,2,1,0:T(8,128)S(1)}) custom-call(f32[40,3,32,128]{3,2,1,0:T(8,128)S(1)} %copy-done, f32[2,3,32,128]{3,2,1,0:T(8,128)S(1)} %copy-done.1, s32[3,32,128]{2,1,0:T(8,128)S(1)} %copy-done.2), custom_call_target="tpu_custom_call" | custom-call | flops 9830400 | bytes 3932160 | tf_op jit(solution)/shard_map/pallas_call | solution.py:544
  8.4 0.0 copy-done.3
  8.4 0.0 copy-done.4
  8.4 0.0 copy-done.5
  8.4 0.0 copy-done.6
  8.4 0.0 copy-done.7
  8.5 0.0 copy-done.8
  8.5 0.0 copy-done.9
  8.5 0.0 copy-done.10
  8.5 3.2 %shard_map.111.partial = f32[40,3,32,128]{3,2,1,0:T(8,128)S(1)} custom-call(f32[40,3,32,128]{3,2,1,0:T(8,128)S(1)} %copy-done, s32[3,32,128]{2,1,0:T(8,128)S(1)} %copy-done.2, f32[32,128]{1,0:T(8,128)S(1)} %copy-done.3, s32[10,26]{1,0:T(8,128)S(1)} %copy-done.4, f32[26]{0:T(128)S(1)} %copy-done.6, ...), custom_call_target="tpu_custom_call", output_to_operand_aliasing={{}: (10, {})} | custom-call | flops 19660800 | bytes 3932160 | tf_op jit(solution)/shard_map/pallas_call | solution.py:553
  11.7 0.0 collective-permute-done.1.after
  11.7 1.5 %collective-permute-done.before = f32[248,128]{1,0:T(8,128)S(1)} collective-permute-done((f32[248,128]{1,0:T(8,128)S(1)}, f32[248,128]{1,0:T(8,128)S(1)}, u32[]{:S(2)}, u32[]{:S(2)}) %collective-permute-start) | collective-permute-done | bytes 127008 | tf_op jit(solution)/shard_map/ppermute | solution.py:537
  13.1 0.9 %shard_map.112 = (f32[40,3,16,128]{3,2,1,0:T(8,128)S(1)}, f32[3,32,128]{2,1,0:T(8,128)S(1)}, f32[3,32,128]{2,1,0:T(8,128)S(1)}, f32[40,3,32,128]{3,2,1,0:T(8,128)S(1)}) custom-call(f32[40,3,32,128]{3,2,1,0:T(8,128)S(1)} %copy-done, f32[2,3,32,128]{3,2,1,0:T(8,128)S(1)} %copy-done.1, ...), custom_call_target="tpu_custom_call", output_to_operand_aliasing={{3}: (5, {}), {1}: (6, {}), {2}: (7, {})} | custom-call | flops 4915200 | bytes 3932160 | tf_op jit(solution)/shard_map/pallas_call | solution.py:578
  14.0 0.1 collective-permute-start.2
  14.1 1.6 %collective-permute-start.3 = (f32[3,32,128]{2,1,0:T(8,128)S(1)}, f32[3,32,128]{2,1,0:T(8,128)S(1)}, u32[]{:S(2)}, u32[]{:S(2)}) collective-permute-start(f32[3,32,128]{2,1,0:T(8,128)S(1)} %get-tuple-element.26.my_second), channel_id=1, source_target_pairs={{1,2},{2,1},{3,0},{0,3},{5,6},{6,5},{7,4},{4,7},{9,10},{10,9},{11,... | collective-permute-start | bytes 147464 | tf_op jit(solution)/shard_map/ppermute | solution.py:592
  15.7 1.7 %shard_map.113 = (f32[40,3,32,128]{3,2,1,0:T(8,128)S(1)}, f32[8,3,32,128]{3,2,1,0:T(8,128)S(1)}) custom-call(f32[40,3,16,128]{3,2,1,0:T(8,128)S(1)} %get-tuple-element.23.swept, f32[2,3,32,128]{3,2,1,0:T(8,128)S(1)} %copy-done.1, s32[3,32,128]{2,1,0:T(8,128)S(1)} %copy-done.2, ...), custom_call_target="tpu_custom_call", output_to_operand_aliasing={{0}: (6, {})} | custom-call | flops 4915200 | bytes 2949120 | tf_op jit(solution)/shard_map/pallas_call | solution.py:593
  17.4 0.0 collective-permute-done.2.first
  17.4 0.2 %collective-permute-done.3.second = f32[3,32,128]{2,1,0:T(8,128)S(1)} collective-permute-done((f32[3,32,128]{2,1,0:T(8,128)S(1)}, f32[3,32,128]{2,1,0:T(8,128)S(1)}, u32[]{:S(2)}, u32[]{:S(2)}) %collective-permute-start.3) | collective-permute-done | bytes 49184 | tf_op jit(solution)/shard_map/ppermute | solution.py:592
  17.7 2.0 %shard_map.114 = (f32[40,3,32,128]{3,2,1,0:T(8,128)S(1)}, f32[40,3,32,128]{3,2,1,0:T(8,128)}) custom-call(f32[8,3,32,128]{3,2,1,0:T(8,128)S(1)} %get-tuple-element.28.ready, f32[3,32,128]{2,1,0:T(8,128)S(1)} %collective-permute-done.2.first, f32[3,32,128]{2,1,0:T(8,128)S(1)} %collective-permute-done.3.second, ...), custom_call_target="tpu_custom_call", output_to_operand_aliasing={{0}: (3, {})} | custom-call | flops 1966080 | bytes 3932160 | tf_op jit(solution)/shard_map/pallas_call | solution.py:602
  (4 shorter events, 0.0 us)
Async XLA Ops:
  0.0 6.4 %copy-start = (f32[40,3,32,128]{3,2,1,0:T(8,128)S(1)}, f32[40,3,32,128]{3,2,1,0:T(8,128)}, u32[]{:S(2)}) copy-start(f32[40,3,32,128]{3,2,1,0:T(8,128)} %tracers.5) | copy-start | bytes 5898244
  0.0 6.4 %copy-start.1 = (f32[2,3,32,128]{3,2,1,0:T(8,128)S(1)}, f32[2,3,32,128]{3,2,1,0:T(8,128)}, u32[]{:S(2)}) copy-start(f32[2,3,32,128]{3,2,1,0:T(8,128)} %velocity.5) | copy-start | bytes 294916
  0.0 6.4 %copy-start.2 = (s32[3,32,128]{2,1,0:T(8,128)S(1)}, s32[3,32,128]{2,1,0:T(8,128)}, u32[]{:S(2)}) copy-start(s32[3,32,128]{2,1,0:T(8,128)} %mask.7) | copy-start | bytes 147460
  0.0 8.4 %copy-start.3 = (f32[32,128]{1,0:T(8,128)S(1)}, f32[32,128]{1,0:T(8,128)}, u32[]{:S(2)}) copy-start(f32[32,128]{1,0:T(8,128)} %sunlight.1) | copy-start | bytes 49156
  0.0 8.4 %copy-start.4 = (s32[10,26]{1,0:T(8,128)S(1)}, s32[10,26]{1,0:T(8,128)}, u32[]{:S(2)}) copy-start(s32[10,26]{1,0:T(8,128)} %palatable.1) | copy-start | bytes 3124
  0.0 8.4 %copy-start.5 = (f32[4,26]{1,0:T(4,128)S(1)}, f32[4,26]{1,0:T(4,128)}, u32[]{:S(2)}) copy-start(f32[4,26]{1,0:T(4,128)} %half_sat.1) | copy-start | bytes 1252
  0.0 8.4 %copy-start.6 = (f32[26]{0:T(128)S(1)}, f32[26]{0:T(128)}, u32[]{:S(2)}) copy-start(f32[26]{0:T(128)} %growth_max.1) | copy-start | bytes 316
  0.0 8.4 %copy-start.7 = (f32[26]{0:T(128)S(1)}, f32[26]{0:T(128)}, u32[]{:S(2)}) copy-start(f32[26]{0:T(128)} %light_half.1) | copy-start | bytes 316
  0.0 8.4 %copy-start.8 = (f32[10]{0:T(128)S(1)}, f32[10]{0:T(128)}, u32[]{:S(2)}) copy-start(f32[10]{0:T(128)} %graze_max.1) | copy-start | bytes 124
  0.1 8.4 %copy-start.9 = (f32[10]{0:T(128)S(1)}, f32[10]{0:T(128)}, u32[]{:S(2)}) copy-start(f32[10]{0:T(128)} %graze_half.1) | copy-start | bytes 124
  0.1 8.4 %copy-start.10 = (f32[4]{0:T(128)S(1)}, f32[4]{0:T(128)}, u32[]{:S(2)}) copy-start(f32[4]{0:T(128)} %stoichiometry.1) | copy-start | bytes 52
  1.3 10.4 %collective-permute-start.1 = (f32[248,128]{1,0:T(8,128)S(1)}, f32[248,128]{1,0:T(8,128)S(1)}, u32[]{:S(2)}, u32[]{:S(2)}) collective-permute-start(f32[248,128]{1,0:T(8,128)S(1)} %bitcast.9), channel_id=1, source_target_pairs={{4,0},{8,4},{12,8},{0,12},{5,1},{9,5},{13,9},{1,13},{6,2},{10,6},{... | collective-permute-start | bytes 380936 | tf_op jit(solution)/shard_map/ppermute | solution.py:538
  6.4 6.7 %collective-permute-start = (f32[248,128]{1,0:T(8,128)S(1)}, f32[248,128]{1,0:T(8,128)S(1)}, u32[]{:S(2)}, u32[]{:S(2)}) collective-permute-start(f32[248,128]{1,0:T(8,128)S(1)} %bitcast.8), channel_id=1, source_target_pairs={{0,4},{4,8},{8,12},{12,0},{1,5},{5,9},{9,13},{13,1},{2,6},{6,10},{... | collective-permute-start | bytes 380936 | tf_op jit(solution)/shard_map/ppermute | solution.py:537
  14.0 3.4 %collective-permute-start.2 = (f32[3,32,128]{2,1,0:T(8,128)S(1)}, f32[3,32,128]{2,1,0:T(8,128)S(1)}, u32[]{:S(2)}, u32[]{:S(2)}) collective-permute-start(f32[3,32,128]{2,1,0:T(8,128)S(1)} %get-tuple-element.25.my_first), channel_id=1, source_target_pairs={{0,1},{1,0},{2,3},{3,2},{4,5},{5,4},{6,7},{7,6},{8,9},{9,8},{10,11... | collective-permute-start | bytes 147464 | tf_op jit(solution)/shard_map/ppermute | solution.py:591
  14.1 3.6 %collective-permute-start.3 = (f32[3,32,128]{2,1,0:T(8,128)S(1)}, f32[3,32,128]{2,1,0:T(8,128)S(1)}, u32[]{:S(2)}, u32[]{:S(2)}) collective-permute-start(f32[3,32,128]{2,1,0:T(8,128)S(1)} %get-tuple-element.26.my_second), channel_id=1, source_target_pairs={{1,2},{2,1},{3,0},{0,3},{5,6},{6,5},{7,4},{4,7},{9,10},{10,9},{11,... | collective-permute-start | bytes 147464 | tf_op jit(solution)/shard_map/ppermute | solution.py:592
